TPU v7x, 32 devices: a whole 2x2x4 slice. The times are simulated.
32 devices in a mesh: parts: 2 (over y), seq: 4 (over z), head: 4 (over x, core).
Axes of the slice: x: 2, y: 2, z: 4, core: 2. Of those that a mesh axis runs over, the one named last changes fastest.
Arguments:
- query_raw: bfloat16 [6144, 4096], P(('parts', 'seq'), 'head'), parts along dimension 0, may hold values from -6 to 6
- key_raw: bfloat16 [6144, 4096], P(('parts', 'seq'), 'head'), parts along dimension 0, may hold values from -18 to 18
- value_raw: bfloat16 [6144, 4096], P(('parts', 'seq'), 'head'), parts along dimension 0, may hold values from -6 to 6
- out_gate: bfloat16 [6144, 4096], P(('parts', 'seq'), 'head'), parts along dimension 0, may hold values from -6 to 6
- log_decay: float32 [32, 6144], P('head', ('parts', 'seq')), parts along dimension 1, may hold values from -1.2 to 0
- write_strength: float32 [32, 6144], P('head', ('parts', 'seq')), parts along dimension 1, may hold values from 0 to 1
- conv_weight: float32 [3, 4, 4096], P(None, None, 'head'), may hold values from -3 to 3
- norm_gain: float32 [128], replicated, may hold values from 0.25 to 1.75
- out_weight: bfloat16 [4096, 2304], P('head'), may hold values from -0.09375 to 0.09375
- history_end: int32 [2], P('parts'), parts along dimension 0, may hold values from 1536 to 3072
Outputs:
- layer_out: bfloat16 [6144, 2304], P(('parts', 'seq', 'head')), parts along dimension 0
There are 2 independent parts, one for each index of `parts`. A program takes and returns all parts, laid end to end along the dimension named above; an argument that names none is the same for every part. Nothing has to cross between parts.
Inputs may be any that keep to these rules, and one draw needn't show every extreme that they name: Positions at and after history_end[0] are padding.
All inputs are finite; a program needn't handle non-finite values.
Results may differ from a plain program's by a relative error of at most 0.014.
Values may be sent and summed in bfloat16 or wider, within the bound.
No kernel may reach another device: no remote copies, remote signals or barrier semaphores. Data moves between devices by JAX's collectives and lax.ppermute only.
A program may use at most 192 MiB of HBM per device.

v0:
```python
import jax
import jax.numpy as jnp
from jax import lax
from jax.sharding import PartitionSpec as P

block_len = 64


def passed_along(block, axis, distance):
    devices = range(lax.axis_size(axis))
    route = [(i - distance, i) for i in devices if i - distance in devices]
    return lax.ppermute(block, axis, route)


def prefix(array, axis, combine, identity):
    count, place = (lax.axis_size(axis), lax.axis_index(axis))
    everything = jax.tree.map(
        lambda part, kind: lax.all_gather(part.astype(kind), axis),
        array,
        jax.tree.map(lambda a: jnp.bfloat16 if a.dtype == jnp.float32 else a.dtype, array),
    )
    start = jax.tree.map(
        lambda part, zero: jnp.broadcast_to(jnp.asarray(zero, part.dtype), part.shape),
        array,
        identity,
    )

    def hop(k, before):
        reached = k < place
        new = combine(
            before, jax.tree.map(lambda part, own: part[k].astype(own.dtype), everything, array)
        )
        return jax.tree.map(lambda a, b: jnp.where(reached, a, b), new, before)

    return lax.fori_loop(0, count, hop, start)


def exact_einsum(form, left, right):
    return jnp.einsum(form, left, right, precision=lax.Precision.HIGHEST)


def conv_silu(raw_rows, rim_rows, taps):
    rows_total = raw_rows.shape[0]
    padded = jnp.concatenate([rim_rows, raw_rows], axis=0).astype(jnp.float32)
    summed = taps[0] * padded[0:rows_total]
    for tap_index in range(1, 4):
        summed = summed + taps[tap_index] * padded[tap_index : tap_index + rows_total]
    return jax.nn.silu(summed)


def unit_heads(values, head_width, multiplier):
    shaped = values.reshape(values.shape[0], -1, head_width)
    norms = lax.rsqrt(jnp.sum(shaped * shaped, axis=-1, keepdims=True) + 1e-06)
    return (shaped * norms * multiplier).reshape(values.shape).astype(jnp.bfloat16)


def stretch_terms(queries, keys, values, decays, writes):
    span = decays.shape[-1]
    head_width = keys.shape[-1]
    cumulative = jnp.cumsum(decays, axis=-1)
    gammas = jnp.exp(cumulative)
    log_gaps = cumulative[:, :, None] - cumulative[:, None, :]
    row_ids = lax.broadcasted_iota(jnp.int32, (span, span), 0)
    col_ids = lax.broadcasted_iota(jnp.int32, (span, span), 1)
    inclusive = col_ids <= row_ids
    strict = col_ids < row_ids
    decay_incl = jnp.where(inclusive, jnp.exp(jnp.where(inclusive, log_gaps, 0.0)), 0.0)
    decay_strict = jnp.where(strict, decay_incl, 0.0)
    key_gram = exact_einsum("hid,hjd->hij", keys, keys)
    system = jnp.eye(span, dtype=jnp.float32) + writes[:, :, None] * key_gram * decay_strict
    both_sides = jnp.concatenate(
        [(writes * gammas)[:, :, None] * keys, writes[:, :, None] * values], axis=-1
    )
    both_mix = jax.scipy.linalg.solve_triangular(system, both_sides, lower=True, unit_diagonal=True)
    key_mix = both_mix[:, :, :head_width]
    value_mix = both_mix[:, :, head_width:]
    scores = exact_einsum("hid,hjd->hij", queries, keys) * decay_incl
    last_decay = gammas[:, -1]
    keys_out = keys * jnp.exp(cumulative[:, -1:] - cumulative)[:, :, None]
    return (gammas, key_mix, value_mix, scores, last_decay, keys_out)


def block_terms(block_inputs):
    query_block, key_block, value_block, decay_block, write_block = block_inputs
    query_f = query_block.astype(jnp.float32).transpose(1, 0, 2)
    key_f = key_block.astype(jnp.float32).transpose(1, 0, 2)
    value_f = value_block.astype(jnp.float32).transpose(1, 0, 2)
    return (query_f, stretch_terms(query_f, key_f, value_f, decay_block, write_block))


def advance(summary, terms):
    transition, carried = summary
    gammas, key_mix, value_mix, scores, last_decay, keys_out = terms
    mixed_transition = exact_einsum("hcd,hde->hce", key_mix, transition)
    new_transition = last_decay[:, None, None] * transition - exact_einsum(
        "hcd,hce->hde", keys_out, mixed_transition
    )
    fresh = value_mix - exact_einsum("hcd,hde->hce", key_mix, carried)
    new_carried = last_decay[:, None, None] * carried + exact_einsum(
        "hcd,hce->hde", keys_out, fresh
    )
    return ((new_transition, new_carried), fresh)


def compose(earlier, latter):
    joined = exact_einsum("hde,hef->hdf", latter[0], earlier[0])
    carried = exact_einsum("hde,hef->hdf", latter[0], earlier[1]) + latter[1]
    return (joined, carried)


def on_device(
    query_raw,
    key_raw,
    value_raw,
    out_gate,
    log_decay,
    write_strength,
    conv_weight,
    norm_gain,
    out_weight,
    history_end,
):
    tok_rows, channels = query_raw.shape
    head_count = log_decay.shape[0]
    head_width = channels // head_count
    rim_rows = passed_along((query_raw[-3:], key_raw[-3:], value_raw[-3:]), "seq", 1)
    queries = unit_heads(
        conv_silu(query_raw, rim_rows[0], conv_weight[0]), head_width, head_width ** (-0.5)
    )
    keys_all = unit_heads(conv_silu(key_raw, rim_rows[1], conv_weight[1]), head_width, 1.0)
    values_all = conv_silu(value_raw, rim_rows[2], conv_weight[2]).astype(jnp.bfloat16)
    stretch_count = tok_rows // block_len

    def by_stretch(array):
        return array.reshape(stretch_count, block_len, head_count, head_width)

    def gate_stretches(array):
        return array.reshape(head_count, stretch_count, block_len).transpose(1, 0, 2)

    inputs = (
        by_stretch(queries),
        by_stretch(keys_all),
        by_stretch(values_all),
        gate_stretches(log_decay),
        gate_stretches(write_strength),
    )
    stored = jax.vmap(block_terms)(inputs)
    identity_mat = jnp.broadcast_to(
        jnp.eye(head_width, dtype=jnp.float32), (head_count, head_width, head_width)
    )
    zero_state = jnp.zeros((head_count, head_width, head_width), jnp.float32)

    def summary_step(summary, block_stored):
        query_f, terms = block_stored
        new_summary, fresh = advance(summary, terms)
        return (new_summary, None)

    summary, unused_out = lax.scan(summary_step, (identity_mat, zero_state), stored)
    state_in = prefix(summary, "seq", compose, (identity_mat, zero_state))[1]

    def replay_step(state, block_stored):
        query_f, terms = block_stored
        gammas, key_mix, value_mix, scores, last_decay, keys_out = terms
        fresh = value_mix - exact_einsum("hcd,hde->hce", key_mix, state)
        output = gammas[:, :, None] * exact_einsum("hcd,hde->hce", query_f, state) + exact_einsum(
            "hij,hje->hie", scores, fresh
        )
        new_state = last_decay[:, None, None] * state + exact_einsum(
            "hcd,hce->hde", keys_out, fresh
        )
        return (new_state, output)

    final_state, outputs = lax.scan(replay_step, state_in, stored)
    mixed_heads = outputs.transpose(0, 2, 1, 3).reshape(tok_rows, head_count, head_width)
    normed = (
        mixed_heads
        * lax.rsqrt(jnp.mean(mixed_heads * mixed_heads, axis=-1, keepdims=True) + 1e-06)
        * norm_gain
    )
    gated = normed.reshape(tok_rows, channels) * jax.nn.silu(out_gate.astype(jnp.float32))
    positions = lax.axis_index("seq") * tok_rows + jnp.arange(tok_rows, dtype=jnp.int32)
    gated = jnp.where((positions < history_end[0])[:, None], gated, 0.0).astype(jnp.bfloat16)
    return lax.psum_scatter(
        jnp.dot(gated, out_weight, preferred_element_type=jnp.float32).astype(jnp.bfloat16),
        "head",
        scatter_dimension=0,
        tiled=True,
    )


def solution(mesh):
    return jax.shard_map(
        on_device,
        mesh=mesh,
        in_specs=(
            P(("parts", "seq"), "head"),
            P(("parts", "seq"), "head"),
            P(("parts", "seq"), "head"),
            P(("parts", "seq"), "head"),
            P("head", ("parts", "seq")),
            P("head", ("parts", "seq")),
            P(None, None, "head"),
            P(),
            P("head", None),
            P("parts"),
        ),
        out_specs=P(("parts", "seq", "head"), None),
        check_vma=False,
    )
```

profile of v0, /device:TPU:8, one launch (start us, length us, event | category | flops | bytes accessed | tf_op | source)
XLA Modules:
  0.0 835.3 jit_solution(9891644804070825372)
XLA Ops:
  7.3 3.5 collective-permute-start
  11.5 3.5 collective-permute-start.1
  16.9 2.6 reduce_window_sum.11
  22.9 3.2 multiply_bitcast_fusion.1
  26.1 2.4 copy.66
  28.5 2.8 reduce_sum.27
  34.8 3.9 add_bitcast_fusion
  38.7 473.3 %custom-call.4 = f32[12,8,1,64,64]{3,4,2,1,0:T(8,128)} custom-call(f32[12,8,1,64,64]{4,3,2,1,0:T(8,128)} %add_bitcast_fusion), custom_call_target="InvertDiagBlocksLowerTriangular" | custom-call | tf_op jit(solution)/shard_map/vmap(jit(_solve_triangular))/vmap()/triangular_solve | solution.py:74
  517.4 3.2 convert_multiply_fusion.1
  520.6 6.5 fusion.38
  527.2 3.6 fusion.82
  530.8 88.4 %while.40 = (s32[]{:T(128)}, f32[8,128,128]{2,1,0:T(8,128)S(1)}, f32[8,128,128]{2,1,0:T(8,128)S(1)}, f32[12,8]{1,0:T(8,128)S(1)}, f32[12,8,64,128]{3,2,1,0:T(8,1...) while((s32[]{:T(128)}, f32[8,128,128]{2,1,0:T(8,128)S(1)}, ...), condition=%wide.region_3.4_spmd.clone, body=%wide.region_2.3_spmd.clone.sunk | while | flops 403505152 | bytes 5507820 | solution.py:158
  628.2 3.4 multiply_bitcast_fusion
  631.6 2.4 copy.70
  634.0 2.8 reduce_sum.28
  640.4 2.2 bitcast_bitcast_fusion
  642.6 2.9 fusion.61
  647.2 29.0 %all-gather.7.cloned.1.call-done = bf16[32,128,128]{2,1,0:T(8,128)(2,1)} async-done(((bf16[8,128,128]{2,1,0:T(8,128)(2,1)}), bf16[32,128,128]{2,1,0:T(8,128)(2,1)}) %all-gather.7.cloned.1.call-update) | async-done | bytes 1048592 | tf_op jit(solution)/shard_map/all_gather | solution.py:18
  676.2 6.4 while.41
  682.5 89.2 %while.39 = (s32[]{:T(128)}, f32[8,128,128]{2,1,0:T(8,128)S(1)}, f32[12,8,64,128]{3,2,1,0:T(8,128)}, f32[12,8]{1,0:T(8,128)S(1)}, f32[12,8,64,128]{3,2,1,0:T(8,1...) while((s32[]{:T(128)}, f32[8,128,128]{2,1,0:T(8,128)S(1)}, ...), condition=%wide.region_8.9_spmd, body=%wide.region_7.8_spmd.sunk | while | flops 352780288 | bytes 5513945 | solution.py:173
  771.7 2.9 multiply_reduce_fusion
  776.3 2.2 copy.56
  779.9 8.7 %convolution_convert_fusion = bf16[768,2304]{1,0:T(8,128)(2,1)} fusion(bf16[1024,2304]{1,0:T(8,128)(2,1)} %param.24, bf16[768,1024]{1,0:T(8,128)(2,1)S(1)} %copy-done.6, f32[96,8,8,128]{3,2,1,0:T(8,128)S(1)} %bitcast.210, f32[96,8,8,128]{3,2,1,0:T(8,128)S(1)} %bitcast.209, f32[1024]{0:T(1024)S(1)} %broadcast_bitcast_fusion, ...), kind=kOutput, calls=%fused_computation.55 | convolution fusion | flops 3633512448 | bytes 16126720 | tf_op jit(solution)/shard_map/dot_general | solution.py:184
  788.6 40.1 %reduce-scatter.2.cloned.1.call-done = bf16[192,2304]{1,0:T(8,128)(2,1)} async-done(((bf16[768,2304]{1,0:T(8,128)(2,1)}), bf16[192,2304]{1,0:T(8,128)(2,1)}) %reduce-scatter.2.cloned.1.call-update) | async-done | bytes 884752 | tf_op jit(solution)/shard_map/reduce_scatter | solution.py:183
  (219 shorter events, 214.4 us)
Async XLA Ops:
  6.5 616.8 %copy-start = (f32[128]{0:T(128)S(1)}, f32[128]{0:T(128)}, u32[]{:S(2)}) copy-start(f32[128]{0:T(128)} %param.23) | copy-start | bytes 1540
  6.5 640.6 %all-gather.5.cloned.1.call-start = ((), (), s32[]{:S(2)}) async-start(), calls=%async_computation.2 | async-start | bytes 1310720 | tf_op jit(solution)/shard_map/all_gather | solution.py:18
  7.3 13.7 %collective-permute-start = (bf16[3,1024]{1,0:T(4,128)(2,1)S(1)}, bf16[3,1024]{1,0:T(4,128)(2,1)S(1)}, u32[]{:S(2)}, u32[]{:S(2)}) collective-permute-start(bf16[3,1024]{1,0:T(4,128)(2,1)S(1)} %slice.128), channel_id=1, source_target_pairs={{0,4},{4,8},{8,12},{1,5},{5,9},{9,13},{2,6},{6,10},{10,14},{3,7},{... | collective-permute-start | bytes 18440 | tf_op jit(solution)/shard_map/ppermute | solution.py:12
  11.5 500.5 %collective-permute-start.1 = (bf16[3,1024]{1,0:T(4,128)(2,1)S(1)}, bf16[3,1024]{1,0:T(4,128)(2,1)S(1)}, u32[]{:S(2)}, u32[]{:S(2)}) collective-permute-start(bf16[3,1024]{1,0:T(4,128)(2,1)S(1)} %slice.138), channel_id=1, source_target_pairs={{0,4},{4,8},{8,12},{1,5},{5,9},{9,13},{2,6},{6,10},{10,14},{3,7},{... | collective-permute-start | bytes 18440 | tf_op jit(solution)/shard_map/ppermute | solution.py:12
  31.3 1.9 copy-start.4
  517.4 3.2 copy-start.5
  620.0 56.2 %all-gather.7.cloned.1.call-start = ((), (), s32[]{:S(2)}) async-start(), calls=%async_computation.3 | async-start | bytes 1310720 | tf_op jit(solution)/shard_map/all_gather | solution.py:18
  620.7 5.5 collective-permute-start.2
  624.1 204.6 %reduce-scatter.2.cloned.1.call-start = ((), (), s32[]{:S(2)}) async-start(), calls=%async_computation.1 | async-start | bytes 4423680 | tf_op jit(solution)/shard_map/reduce_scatter | solution.py:183
  636.8 1.9 copy-start.3
  771.7 4.5 copy-start.2
  778.5 1.4 copy-start.6
  779.9 48.9 %copy-start.1 = (f32[128]{0:T(128)S(1)}, f32[128]{0:T(128)}, u32[]{:S(2)}) copy-start(f32[128]{0:T(128)} %param.23) | copy-start | bytes 1540
Sparse Core Ops, SparseCore 0:
  620.1 27.0 all-gather.4
  648.7 27.4 all-gather.6
  788.8 39.9 reduce-scatter.1
where the time goes:
time: 841 us; the launch traced here: 835 us
  other arithmetic  510 us (61%)
  matrix products  192 us (23%)
  waiting for transfers between devices  73 us (9%)
  local copies, waits for them, and re-layouts  35.7 us (4%)
  between operations  14.1 us (2%)
  starting transfers between devices  8.94 us (1%)
    another operation x4, other arithmetic, stretch_terms(): jax.scipy.linalg.solve_triangular(system, both_sides, lower=True, unit_di...  473 us
    dot_general x102, matrix products, exact_einsum(): return jnp.einsum(form, left, right, precision=lax.Precision.HIGHEST)  177 us
    reduce_scatter x1, waiting for transfers between devices, on_device(): lax.psum_scatter(jnp.dot(gated, out_weight, preferred_element_type=jnp.fl...  40.1 us
    all_gather x2, waiting for transfers between devices, prefix(): lax.all_gather(part.astype(kind), axis)  30.7 us
  transfers between devices with their start and end apart: 6, of which 4 were waited for; matrix products, arithmetic and copies ran while one was open for 62% of the time, Pallas kernels for 0%

commit v1 on v0

v1 whole, which is shorter than its diff:
```python
import jax
import jax.numpy as jnp
from jax import lax
from jax.experimental import pallas as pl
from jax.experimental.pallas import tpu as pltpu
from jax.sharding import PartitionSpec as P

CHUNK = 128
RIM = 16
INV_PASSES = 1
F32 = jnp.float32
BF16 = jnp.bfloat16
NN = (((1,), (0,)), ((), ()))
NT = (((1,), (1,)), ((), ()))


def mm(left, right, dims=NN):
    return lax.dot_general(left, right, dims, preferred_element_type=F32)


def exact(left, right, dims=NN):
    return lax.dot_general(
        left, right, dims, precision=lax.Precision.HIGHEST, preferred_element_type=F32
    )


def halves(x):
    high = x.astype(BF16)
    return high, (x - high.astype(F32)).astype(BF16)


def mm3(left, right):
    if INV_PASSES == 1:
        return mm(left.astype(BF16), right.astype(BF16))
    if INV_PASSES == 6:
        return exact(left, right)
    lh, ll = halves(left)
    rh, rl = halves(right)
    return mm(
        jnp.concatenate([lh, ll], axis=1), jnp.concatenate([rh, rh], axis=0)
    ) + mm(lh, rl)


def conv_silu(raw, rim, taps):
    rows = raw.shape[0]
    padded = jnp.concatenate([rim, raw], axis=0)
    n = rim.shape[0]
    total = taps[3:4] * raw
    for j in range(3):
        total = total + taps[j : j + 1] * padded[n - 3 + j : n - 3 + j + rows]
    return total * (1.0 / (1.0 + jnp.exp(-total)))


def chunk_kernel(
    rim_ref, q_ref, k_ref, v_ref, qp_ref, kp_ref, vp_ref, dec_ref, wr_ref, taps_ref,
    local_ref, qeff_ref, summary_ref, state_ref,
):
    step = pl.program_id(0)
    c = q_ref.shape[0]
    heads = dec_ref.shape[0]
    width = q_ref.shape[1] // heads

    @pl.when(step == 0)
    def _():
        rows = lax.broadcasted_iota(jnp.int32, (width, 2 * width), 0)
        cols = lax.broadcasted_iota(jnp.int32, (width, 2 * width), 1)
        eye = jnp.where(rows == cols, 1.0, 0.0).astype(F32)
        for h in range(heads):
            state_ref[h] = eye

    ri = lax.broadcasted_iota(jnp.int32, (c, c), 0)
    ci = lax.broadcasted_iota(jnp.int32, (c, c), 1)
    tril = jnp.where(ci <= ri, 1.0, 0.0).astype(F32)
    eye = jnp.where(ci == ri, 1.0, 0.0).astype(F32)
    strict = ci < ri
    inclusive = ci <= ri
    differ = ri ^ ci
    dec = dec_ref[...]
    wr = wr_ref[...]
    cum_row = exact(dec, tril, NT)
    cum_col = exact(tril, dec, NT)
    wr_col = exact(eye, wr, NT)
    last = cum_row[:, c - 1 : c]
    gamma_row = jnp.exp(cum_row)
    gamma_col = jnp.exp(cum_col)
    kout_row = jnp.exp(last - cum_row)
    last_decay = jnp.exp(last)
    first = step == 0

    def channels(ref, prev_ref, which, h):
        sl = slice(h * width, (h + 1) * width)
        raw = ref[:, sl].astype(F32)
        rim = jnp.where(
            first, rim_ref[which, :, sl].astype(F32), prev_ref[:, sl].astype(F32)
        )
        return conv_silu(raw, rim[-8:], taps_ref[which, :, sl])

    for h in range(heads):
        sl = slice(h * width, (h + 1) * width)
        q = channels(q_ref, qp_ref, 0, h)
        k = channels(k_ref, kp_ref, 1, h)
        v = channels(v_ref, vp_ref, 2, h).astype(BF16)
        q = (q * (lax.rsqrt(jnp.sum(q * q, axis=-1, keepdims=True) + 1e-06) * width ** -0.5)).astype(BF16)
        k = (k * lax.rsqrt(jnp.sum(k * k, axis=-1, keepdims=True) + 1e-06)).astype(BF16)
        grams = mm(jnp.concatenate([q, k], axis=0), k, NT)
        gap = cum_col[:, h : h + 1] - cum_row[h : h + 1, :]
        decay = jnp.exp(jnp.minimum(gap, 0.0))
        scores = jnp.where(inclusive, grams[:c] * decay, 0.0).astype(BF16)
        low = jnp.where(strict, grams[c:] * decay * wr_col[:, h : h + 1], 0.0)
        inv = eye - jnp.where(differ == 1, low, 0.0)
        size = 2
        while size < c:
            part = jnp.where((differ >= size) & (differ < 2 * size), low, 0.0)
            inv = inv - mm3(inv, mm3(part, inv))
            size *= 2
        wr_r = wr[h : h + 1, :]
        key_mix = mm((inv * (wr_r * gamma_row[h : h + 1, :])).astype(BF16), k)
        value_mix = mm((inv * wr_r).astype(BF16), v)
        kf = k.astype(F32)
        q_in = (q.astype(F32) * gamma_col[:, h : h + 1]).astype(BF16)
        k_out = (kf.T * kout_row[h : h + 1, :]).astype(BF16)
        state = state_ref[h]
        read = mm(jnp.concatenate([key_mix.astype(BF16), q_in], axis=0), state.astype(BF16))
        fresh = jnp.concatenate(
            [-read[:c, :width], value_mix - read[:c, width:]], axis=1
        ).astype(BF16)
        both = mm(jnp.concatenate([scores, k_out], axis=0), fresh)
        out = read[c:] + both[:c]
        qeff_ref[:, sl] = out[:, :width].astype(BF16)
        local_ref[:, sl] = out[:, width:]
        state = last_decay[h : h + 1, :] * state + both[c:]
        state_ref[h] = state

    @pl.when(step == pl.num_programs(0) - 1)
    def _():
        summary_ref[...] = state_ref[...].astype(BF16)


def finish_kernel(
    info_ref, all_ref, local_ref, qeff_ref, gate_ref, gain_ref, weight_ref, out_ref, state_ref
):
    step = pl.program_id(0)
    count = pl.num_programs(0) - info_ref[2]
    heads, width = state_ref.shape[0], state_ref.shape[1]
    rows = local_ref.shape[0]

    @pl.when(step == 0)
    def _():
        state_ref[...] = jnp.zeros(state_ref.shape, F32)

    @pl.when(step < info_ref[0])
    def _():
        for h in range(heads):
            state_ref[h] = (
                mm(all_ref[0, h, :, :width], state_ref[h].astype(BF16))
                + all_ref[0, h, :, width:].astype(F32)
            )

    @pl.when(step >= count)
    def _():
        base = info_ref[1] + (step - count) * rows
        pos = base + lax.broadcasted_iota(jnp.int32, (rows, width), 0)
        valid = pos < info_ref[3]
        gated = []
        for h in range(heads):
            sl = slice(h * width, (h + 1) * width)
            o = local_ref[:, sl] + mm(qeff_ref[:, sl], state_ref[h].astype(BF16))
            norm = lax.rsqrt(jnp.mean(o * o, axis=-1, keepdims=True) + 1e-06)
            g = gate_ref[:, sl].astype(F32)
            o = o * norm * gain_ref[...] * (g * (1.0 / (1.0 + jnp.exp(-g))))
            gated.append(jnp.where(valid, o, 0.0).astype(BF16))
        out_ref[...] = mm(jnp.concatenate(gated, axis=1), weight_ref[...]).astype(BF16)


def passed_along(block, axis, distance):
    devices = range(lax.axis_size(axis))
    route = [(i - distance, i) for i in devices if i - distance in devices]
    return lax.ppermute(block, axis, route)


def on_device(
    query_raw, key_raw, value_raw, out_gate, log_decay, write_strength,
    conv_weight, norm_gain, out_weight, history_end,
):
    rows, channels = query_raw.shape
    heads = log_decay.shape[0]
    width = channels // heads
    c = CHUNK
    steps = rows // c
    rim = passed_along(
        jnp.stack([query_raw[-RIM:], key_raw[-RIM:], value_raw[-RIM:]]), "seq", 1
    )
    per = c // RIM
    block = pl.BlockSpec((c, channels), lambda i: (i, 0))
    prev = pl.BlockSpec((RIM, channels), lambda i: (jnp.maximum(i * per - 1, 0), 0))
    gates = pl.BlockSpec((heads, c), lambda i: (0, i))
    local, qeff, summary = pl.pallas_call(
        chunk_kernel,
        grid=(steps,),
        in_specs=[
            pl.BlockSpec((3, RIM, channels), lambda i: (0, 0, 0)),
            block, block, block, prev, prev, prev, gates, gates,
            pl.BlockSpec((3, 4, channels), lambda i: (0, 0, 0)),
        ],
        out_specs=[
            block, block,
            pl.BlockSpec((heads, width, 2 * width), lambda i: (0, 0, 0)),
        ],
        out_shape=[
            jax.ShapeDtypeStruct((rows, channels), F32),
            jax.ShapeDtypeStruct((rows, channels), BF16),
            jax.ShapeDtypeStruct((heads, width, 2 * width), BF16),
        ],
        scratch_shapes=[pltpu.VMEM((heads, width, 2 * width), F32)],
        compiler_params=pltpu.CompilerParams(vmem_limit_bytes=48 << 20),
        name="chunks",
    )(rim, query_raw, key_raw, value_raw, query_raw, key_raw, value_raw,
      log_decay, write_strength, conv_weight)
    count = lax.axis_size("seq")
    place = lax.axis_index("seq")
    gathered = lax.all_gather(summary, "seq")
    dim = out_weight.shape[1]
    tile = 256
    tiles = rows // tile
    info = jnp.stack([place, place * rows, tiles, history_end[0]]).astype(jnp.int32)
    row_block = lambda i, s: (jnp.maximum(i - count, 0), 0)
    partial = pl.pallas_call(
        finish_kernel,
        grid_spec=pltpu.PrefetchScalarGridSpec(
            num_scalar_prefetch=1,
            grid=(count + tiles,),
            in_specs=[
                pl.BlockSpec((1, heads, width, 2 * width), lambda i, s: (jnp.minimum(i, count - 1), 0, 0, 0)),
                pl.BlockSpec((tile, channels), row_block),
                pl.BlockSpec((tile, channels), row_block),
                pl.BlockSpec((tile, channels), row_block),
                pl.BlockSpec((1, width), lambda i, s: (0, 0)),
                pl.BlockSpec((channels, dim), lambda i, s: (0, 0)),
            ],
            out_specs=pl.BlockSpec((tile, dim), row_block),
            scratch_shapes=[pltpu.VMEM((heads, width, width), F32)],
        ),
        out_shape=jax.ShapeDtypeStruct((rows, dim), BF16),
        compiler_params=pltpu.CompilerParams(vmem_limit_bytes=48 << 20),
        name="finish",
    )(info, gathered, local, qeff, out_gate, norm_gain.reshape(1, width), out_weight)
    return lax.psum_scatter(partial, "head", scatter_dimension=0, tiled=True)


def solution(mesh):
    return jax.shard_map(
        on_device,
        mesh=mesh,
        in_specs=(
            P(("parts", "seq"), "head"),
            P(("parts", "seq"), "head"),
            P(("parts", "seq"), "head"),
            P(("parts", "seq"), "head"),
            P("head", ("parts", "seq")),
            P("head", ("parts", "seq")),
            P(None, None, "head"),
            P(),
            P("head", None),
            P("parts"),
        ),
        out_specs=P(("parts", "seq", "head"), None),
        check_vma=False,
    )
```

time: 841 us -> 223 us (0.27)
  other arithmetic: 510 us -> 0.09 us
  matrix products: 192 us -> 0 us
  Pallas kernels: 0 us -> 105 us
  local copies, waits for them, and re-layouts: 35.7 us -> 9.02 us
  waiting for transfers between devices: 73 us -> 89.2 us
    another operation x5 -> x2, other arithmetic: 476 us -> 0.09 us  [the longest x1 0.08 us: on_device(): jnp.stack([place, place * rows, tiles, history_end[0]]).astype(jnp.int32)]
    dot_general x103 -> x0, matrix products: 186 us -> none  [the longest x102 177 us: exact_einsum(): return jnp.einsum(form, left, right, precision=lax.Precision.HIGHEST)]
    pallas_call x0 -> x2, Pallas kernels: none -> 105 us  [the longest x1 94.4 us: on_device(): pl.pallas_call(chunk_kernel, grid=(steps,), in_specs=[pl.BlockSpec((3, RI...]
    all_gather x2 -> x1, waiting for transfers between devices: 30.7 us -> 44.9 us  [on_device(): gathered = lax.all_gather(summary, 'seq')]
    dynamic_slice x12 -> x0, local copies, waits for them, and re-layouts: 11.7 us -> none  [on_device(): lax.scan(summary_step, (identity_mat, zero_state), stored)]
    unnamed x7 -> x0, other arithmetic: 10.8 us -> none
    reduce_sum x3 -> x0, other arithmetic: 8.53 us -> none  [the longest x2 5.6 us: unit_heads(): norms = lax.rsqrt(jnp.sum(shaped * shaped, axis=-1, keepdims=True) + 1e-06)]
  transfers between devices with their start and end apart: 6 -> 3, of which waited for: 4 -> 3; matrix products, arithmetic and copies ran while one was open for 62% -> 0% of each run, Pallas kernels for 0% -> 0%
where the time goes in v1:
time: 223 us; the launch traced here: 221 us
  Pallas kernels  105 us (47%)
  waiting for transfers between devices  89.2 us (40%)
  between operations  14.1 us (6%)
  local copies, waits for them, and re-layouts  9.02 us (4%)
  starting transfers between devices  3.53 us (2%)
    pallas_call x1, Pallas kernels, on_device(): pl.pallas_call(chunk_kernel, grid=(steps,), in_specs=[pl.BlockSpec((3, RI...  94.4 us
    all_gather x1, waiting for transfers between devices, on_device(): gathered = lax.all_gather(summary, 'seq')  44.9 us
    reduce_scatter x1, waiting for transfers between devices, on_device(): return lax.psum_scatter(partial, 'head', scatter_dimension=0, tiled=True)  41.3 us
    pallas_call x1, Pallas kernels, on_device(): pl.pallas_call(finish_kernel, grid_spec=pltpu.PrefetchScalarGridSpec(num_...  10.7 us
    unnamed x18, local copies, waits for them, and re-layouts  7.48 us
  transfers between devices with their start and end apart: 3, of which 3 were waited for; matrix products, arithmetic and copies ran while one was open for 0% of the time, Pallas kernels for 0%

profile of v1, /device:TPU:8, one launch (start us, length us, event | category | flops | bytes accessed | tf_op | source)
XLA Modules:
  0.0 221.0 jit_solution(2372508305816017598)
XLA Ops:
  6.5 0.0 all-gather.3.cloned.1.call-start
  6.5 0.8 slice_bitcast_fusion.2
  7.3 0.8 slice_bitcast_fusion
  8.1 0.0 copy-start.8
  8.1 3.5 %collective-permute-start = (bf16[3,16,1024]{2,1,0:T(8,128)(2,1)S(1)}, bf16[3,16,1024]{2,1,0:T(8,128)(2,1)S(1)}, u32[]{:S(2)}, u32[]{:S(2)}) collective-permute-start(bf16[3,16,1024]{2,1,0:T(8,128)(2,1)S(1)} %pad_maximum_fusion), channel_id=1, source_target_pairs={{0,4},{4,8},{8,12},{1,5},{5,9},{9,13},{2,6},{6,10},{10,14},{3,7},{... | collective-permute-start | bytes 294920 | tf_op jit(solution)/shard_map/ppermute | solution.py:178
  11.6 3.0 %collective-permute-done.rim_ref = bf16[3,16,1024]{2,1,0:T(8,128)(2,1)S(1)} collective-permute-done((bf16[3,16,1024]{2,1,0:T(8,128)(2,1)S(1)}, bf16[3,16,1024]{2,1,0:T(8,128)(2,1)S(1)}, u32[]{:S(2)}, u32[]{:S(2)}) %collective-permute-start) | collective-permute-done | bytes 98336 | tf_op jit(solution)/shard_map/ppermute | solution.py:178
  14.6 0.0 copy-start
  14.6 1.4 copy-done
  16.0 1.4 copy-done.1
  17.4 0.8 copy-done.5
  18.2 0.7 copy-done.6
  19.0 0.7 copy-done.7
  19.7 94.4 %chunks.1 = (f32[768,1024]{1,0:T(8,128)}, bf16[768,1024]{1,0:T(8,128)(2,1)S(1)}, bf16[8,128,256]{2,1,0:T(8,128)(2,1)S(1)}) custom-call(bf16[3,16,1024]{2,1,0:T(8,128)(2,1)S(1)} %collective-permute-done.rim_ref, bf16[768,1024]{1,0:T(8,128)(2,1)S(1)} %copy-done.1, bf16[768,1024]{1,0:T(8,128)(2,1)S(1)} %copy-done, bf16[768,1024]{1,0:T(8,128)(2,1)} %vp_ref.1, ...), custom_call_target="tpu_custom_call" | custom-call | tf_op jit(solution)/shard_map/chunks/pallas_call | solution.py:197
  114.1 0.8 copy-done.4
  114.9 0.0 all-gather.3.cloned.1.call-update
  114.9 0.0 reduce-scatter.2.cloned.1.call-start
  115.6 0.1 pad_add_fusion.info_ref
  115.7 44.9 %all-gather.3.cloned.1.call-done = bf16[32,128,256]{2,1,0:T(8,128)(2,1)} async-done(((bf16[8,128,256]{2,1,0:T(8,128)(2,1)}), bf16[32,128,256]{2,1,0:T(8,128)(2,1)}) %all-gather.3.cloned.1.call-update) | async-done | bytes 2097168 | tf_op jit(solution)/shard_map/all_gather | solution.py:221
  160.6 0.0 copy-done.8
  160.6 0.0 copy-done.3
  160.6 1.6 copy-done.2
  162.2 10.7 %finish.1 = bf16[768,2304]{1,0:T(8,128)(2,1)} custom-call(s32[4]{0:T(128)S(1)} %pad_add_fusion.info_ref, bf16[4,8,128,256]{3,2,1,0:T(8,128)(2,1)S(1)} %bitcast.10, f32[768,1024]{1,0:T(8,128)} %get-tuple-element.9.local_ref, bf16[768,1024]{1,0:T(8,128)(2,1)S(1)} %get-tuple-element.10.qeff_ref, bf16[768,1024]{1,0:T(8,128)(2,1)S(1)} %copy-done.3, ...), custom_call_target="tpu_custom_call" | custom-call | tf_op jit(solution)/shard_map/finish/pallas_call | solution.py:227
  172.9 0.0 reduce-scatter.2.cloned.1.call-update
  172.9 41.3 %reduce-scatter.2.cloned.1.call-done = bf16[192,2304]{1,0:T(8,128)(2,1)} async-done(((bf16[768,2304]{1,0:T(8,128)(2,1)}), bf16[192,2304]{1,0:T(8,128)(2,1)}) %reduce-scatter.2.cloned.1.call-update) | async-done | bytes 884752 | tf_op jit(solution)/shard_map/reduce_scatter | solution.py:247
  (8 shorter events, 0.0 us)
Async XLA Ops:
  6.5 154.0 %all-gather.3.cloned.1.call-start = ((), (), s32[]{:S(2)}) async-start(), calls=%async_computation.2 | async-start | bytes 2621440 | tf_op jit(solution)/shard_map/all_gather | solution.py:221
  8.1 152.5 %copy-start.8 = (f32[128]{0:T(128)S(1)}, f32[128]{0:T(128)}, u32[]{:S(2)}) copy-start(f32[128]{0:T(128)} %param.17) | copy-start | bytes 1540
  8.1 6.5 %collective-permute-start = (bf16[3,16,1024]{2,1,0:T(8,128)(2,1)S(1)}, bf16[3,16,1024]{2,1,0:T(8,128)(2,1)S(1)}, u32[]{:S(2)}, u32[]{:S(2)}) collective-permute-start(bf16[3,16,1024]{2,1,0:T(8,128)(2,1)S(1)} %pad_maximum_fusion), channel_id=1, source_target_pairs={{0,4},{4,8},{8,12},{1,5},{5,9},{9,13},{2,6},{6,10},{10,14},{3,7},{... | collective-permute-start | bytes 294920 | tf_op jit(solution)/shard_map/ppermute | solution.py:178
  14.6 1.4 copy-start
  16.0 1.4 copy-start.1
  17.4 0.8 copy-start.5
  18.2 0.7 copy-start.6
  19.0 0.7 copy-start.7
  19.7 140.9 %copy-start.3 = (bf16[768,1024]{1,0:T(8,128)(2,1)S(1)}, bf16[768,1024]{1,0:T(8,128)(2,1)}, u32[]{:S(2)}) copy-start(bf16[768,1024]{1,0:T(8,128)(2,1)} %gate_ref.1) | copy-start | bytes 4718596
  114.1 0.8 copy-start.4
  114.9 99.3 %reduce-scatter.2.cloned.1.call-start = ((), (), s32[]{:S(2)}) async-start(), calls=%async_computation.1 | async-start | bytes 4423680 | tf_op jit(solution)/shard_map/reduce_scatter | solution.py:247
  160.6 1.6 copy-start.2
Sparse Core Ops, SparseCore 0:
  115.1 45.4 all-gather.2
  173.0 41.1 reduce-scatter.1

commit v2 on v1

v2 whole, which is shorter than its diff:
```python
import jax
import jax.numpy as jnp
import numpy as np
from jax import lax
from jax.experimental import pallas as pl
from jax.experimental.pallas import tpu as pltpu
from jax.sharding import PartitionSpec as P

CHUNK = 128
RIM = 16
GROUP = 8
F32 = jnp.float32
BF16 = jnp.bfloat16
NN = (((1,), (0,)), ((), ()))
NT = (((1,), (1,)), ((), ()))


def mm(left, right, dims=NN):
    return lax.dot_general(left, right, dims, preferred_element_type=F32)


def exact(left, right, dims=NN):
    return lax.dot_general(
        left, right, dims, precision=lax.Precision.HIGHEST, preferred_element_type=F32
    )


def sigmoid(x):
    return 1.0 / (1.0 + jnp.exp(-x))


def conv_silu(raw, rim, taps):
    rows = raw.shape[0]
    padded = jnp.concatenate([rim, raw], axis=0)
    n = rim.shape[0]
    total = taps[3:4] * raw
    for j in range(3):
        total = total + taps[j : j + 1] * padded[n - 3 + j : n - 3 + j + rows]
    return total * sigmoid(total)


def unit(x, scale):
    return (x * (lax.rsqrt(jnp.sum(x * x, axis=-1, keepdims=True) + 1e-06) * scale)).astype(BF16)


def positions(c):
    return (
        lax.broadcasted_iota(jnp.int32, (c, c), 0),
        lax.broadcasted_iota(jnp.int32, (c, c), 1),
    )


def channels(rim_ref, ref, prev_ref, taps_ref, which, sl, first):
    raw = ref[:, sl].astype(F32)
    rim = jnp.where(first, rim_ref[which, :, sl].astype(F32), prev_ref[:, sl].astype(F32))
    return conv_silu(raw, rim[-8:], taps_ref[which, :, sl])


def summary_kernel(
    rim_ref, k_ref, v_ref, kp_ref, vp_ref, dec_ref, wr_ref, taps_ref, mask_ref,
    keys_ref, fresh_ref, start_ref, summary_ref, state_ref,
):
    step = pl.program_id(0)
    c = k_ref.shape[0]
    heads = dec_ref.shape[0]
    width = k_ref.shape[1] // heads

    @pl.when(step == 0)
    def _():
        rows = lax.broadcasted_iota(jnp.int32, (width, 2 * width), 0)
        cols = lax.broadcasted_iota(jnp.int32, (width, 2 * width), 1)
        eye = jnp.where(rows == cols, 1.0, 0.0).astype(F32)
        for h in range(heads):
            state_ref[h] = eye

    ri, ci = positions(c)
    tril = jnp.where(ci <= ri, 1.0, 0.0).astype(F32)
    eye = jnp.where(ci == ri, 1.0, 0.0).astype(F32)
    dec = dec_ref[...]
    wr = wr_ref[...]
    cum_row = exact(dec, tril, NT)
    cum_col = exact(tril, dec, NT)
    wr_col = exact(eye, wr, NT)
    last = cum_row[:, c - 1 : c]
    wg_row = wr * jnp.exp(cum_row)
    kout_row = jnp.exp(last - cum_row)
    last_decay = jnp.exp(last)
    first = step == 0

    for g in range(0, heads, GROUP):
        hs = range(g, g + GROUP)
        sls = [slice(h * width, (h + 1) * width) for h in hs]
        n = range(GROUP)
        k = [unit(channels(rim_ref, k_ref, kp_ref, taps_ref, 1, sl, first), 1.0) for sl in sls]
        for i in n:
            keys_ref[:, sls[i]] = k[i]
        gram = [mm(x, x, NT) for x in k]
        low = []
        for i in n:
            h = hs[i]
            gap = cum_col[:, h : h + 1] - cum_row[h : h + 1, :]
            decay = jnp.exp(jnp.minimum(gap, 0.0)) * wr_col[:, h : h + 1]
            low.append(jnp.where(ci < ri, gram[i] * decay, 0.0).astype(BF16))
        inv = [eye - (x * mask_ref[0]).astype(F32) for x in low]
        level = 1
        while (1 << level) < c:
            mask = mask_ref[level]
            invb = [x.astype(BF16) for x in inv]
            inner = [mm(low[i] * mask, invb[i]).astype(BF16) for i in n]
            inv = [inv[i] - mm(invb[i], inner[i]) for i in n]
            level += 1
        v = [channels(rim_ref, v_ref, vp_ref, taps_ref, 2, sl, first).astype(BF16) for sl in sls]
        key_mix = [mm((inv[i] * wg_row[hs[i] : hs[i] + 1, :]).astype(BF16), k[i]).astype(BF16) for i in n]
        value_mix = [mm((inv[i] * wr[hs[i] : hs[i] + 1, :]).astype(BF16), v[i]) for i in n]
        k_out = [(k[i].astype(F32).T * kout_row[hs[i] : hs[i] + 1, :]).astype(BF16) for i in n]
        start = [state_ref[h].astype(BF16) for h in hs]
        for i in n:
            start_ref[0, hs[i]] = start[i]
        read = [mm(key_mix[i], start[i]) for i in n]
        fresh = [
            jnp.concatenate(
                [-read[i][:, :width], value_mix[i] - read[i][:, width:]], axis=1
            ).astype(BF16)
            for i in n
        ]
        for i in n:
            h = hs[i]
            fresh_ref[:, 2 * h * width : 2 * (h + 1) * width] = fresh[i]
        both = [mm(k_out[i], fresh[i]) for i in n]
        for i in n:
            h = hs[i]
            state_ref[h] = last_decay[h : h + 1, :] * state_ref[h] + both[i]

    @pl.when(step == pl.num_programs(0) - 1)
    def _():
        summary_ref[...] = state_ref[...].astype(BF16)


def local_kernel(
    rim_ref, q_ref, qp_ref, keys_ref, fresh_ref, start_ref, dec_ref, taps_ref,
    local_ref, qeff_ref,
):
    step = pl.program_id(0)
    c = q_ref.shape[0]
    heads = dec_ref.shape[0]
    width = q_ref.shape[1] // heads
    ri, ci = positions(c)
    tril = jnp.where(ci <= ri, 1.0, 0.0).astype(F32)
    dec = dec_ref[...]
    cum_row = exact(dec, tril, NT)
    cum_col = exact(tril, dec, NT)
    gamma_col = jnp.exp(cum_col)
    first = step == 0
    for g in range(0, heads, GROUP):
        hs = range(g, g + GROUP)
        sls = [slice(h * width, (h + 1) * width) for h in hs]
        n = range(GROUP)
        q = [unit(channels(rim_ref, q_ref, qp_ref, taps_ref, 0, sl, first), width ** -0.5) for sl in sls]
        gram = [mm(q[i], keys_ref[:, sls[i]], NT) for i in n]
        for i in n:
            h = hs[i]
            gap = cum_col[:, h : h + 1] - cum_row[h : h + 1, :]
            scores = jnp.where(ci <= ri, gram[i] * jnp.exp(jnp.minimum(gap, 0.0)), 0.0).astype(BF16)
            q_in = (q[i].astype(F32) * gamma_col[:, h : h + 1]).astype(BF16)
            out = mm(
                jnp.concatenate([q_in, scores], axis=1),
                jnp.concatenate(
                    [start_ref[0, h], fresh_ref[:, 2 * h * width : 2 * (h + 1) * width]], axis=0
                ),
            )
            qeff_ref[:, sls[i]] = out[:, :width].astype(BF16)
            local_ref[:, sls[i]] = out[:, width:]


def level_masks(c):
    r = np.arange(c)
    differ = r[:, None] ^ r[None, :]
    lower = r[:, None] > r[None, :]
    levels = []
    size = 1
    while size < c:
        levels.append(lower & (differ >= size) & (differ < 2 * size))
        size *= 2
    return jnp.asarray(np.stack(levels), BF16)


def front(rim, query_raw, key_raw, value_raw, log_decay, write_strength, conv_weight):
    rows, channel_count = query_raw.shape
    heads = log_decay.shape[0]
    width = channel_count // heads
    c = CHUNK
    steps = rows // c
    per = c // RIM
    masks = level_masks(c)
    block = pl.BlockSpec((c, channel_count), lambda i: (i, 0))
    wide = pl.BlockSpec((c, 2 * channel_count), lambda i: (i, 0))
    prev = pl.BlockSpec((RIM, channel_count), lambda i: (jnp.maximum(i * per - 1, 0), 0))
    gates = pl.BlockSpec((heads, c), lambda i: (0, i))
    rims = pl.BlockSpec((3, RIM, channel_count), lambda i: (0, 0, 0))
    taps = pl.BlockSpec((3, 4, channel_count), lambda i: (0, 0, 0))
    starts = pl.BlockSpec((1, heads, width, 2 * width), lambda i: (i, 0, 0, 0))
    params = pltpu.CompilerParams(vmem_limit_bytes=48 << 20)
    keys, fresh, start, summary = pl.pallas_call(
        summary_kernel,
        grid=(steps,),
        in_specs=[
            rims, block, block, prev, prev, gates, gates, taps,
            pl.BlockSpec(masks.shape, lambda i: (0, 0, 0)),
        ],
        out_specs=[
            block, wide, starts,
            pl.BlockSpec((heads, width, 2 * width), lambda i: (0, 0, 0)),
        ],
        out_shape=[
            jax.ShapeDtypeStruct((rows, channel_count), BF16),
            jax.ShapeDtypeStruct((rows, 2 * channel_count), BF16),
            jax.ShapeDtypeStruct((steps, heads, width, 2 * width), BF16),
            jax.ShapeDtypeStruct((heads, width, 2 * width), BF16),
        ],
        scratch_shapes=[pltpu.VMEM((heads, width, 2 * width), F32)],
        compiler_params=params,
        name="summary",
    )(rim, key_raw, value_raw, key_raw, value_raw, log_decay, write_strength, conv_weight, masks)
    local, qeff = pl.pallas_call(
        local_kernel,
        grid=(steps,),
        in_specs=[rims, block, prev, block, wide, starts, gates, taps],
        out_specs=[block, block],
        out_shape=[
            jax.ShapeDtypeStruct((rows, channel_count), F32),
            jax.ShapeDtypeStruct((rows, channel_count), BF16),
        ],
        compiler_params=params,
        name="local",
    )(rim, query_raw, query_raw, keys, fresh, start, log_decay, conv_weight)
    return local, qeff, summary


def out_kernel(
    info_ref, state_ref, local_ref, qeff_ref, gate_ref, gain_ref, weight_ref, out_ref
):
    heads, width = state_ref.shape[0], state_ref.shape[1]
    rows = local_ref.shape[0]
    base = info_ref[0] + info_ref[1] * rows
    valid = base + lax.broadcasted_iota(jnp.int32, (rows, width), 0) < info_ref[2]
    gated = []
    for h in range(heads):
        sl = slice(h * width, (h + 1) * width)
        o = local_ref[:, sl] + mm(qeff_ref[:, sl], state_ref[h].astype(BF16))
        norm = lax.rsqrt(jnp.mean(o * o, axis=-1, keepdims=True) + 1e-06)
        g = gate_ref[:, sl].astype(F32)
        o = o * norm * gain_ref[...] * (g * sigmoid(g))
        gated.append(jnp.where(valid, o, 0.0).astype(BF16))
    out_ref[...] = mm(jnp.concatenate(gated, axis=1), weight_ref[...]).astype(BF16)


def passed_along(block, axis, distance):
    devices = range(lax.axis_size(axis))
    route = [(i - distance, i) for i in devices if i - distance in devices]
    return lax.ppermute(block, axis, route)


def carried_in(summary, axis):
    width = summary.shape[1]
    count = lax.axis_size(axis)
    move, own = summary[:, :, :width], summary[:, :, width:]

    def apply(a, b, s):
        return jnp.einsum("hij,hjk->hik", a, s, preferred_element_type=F32) + b.astype(F32)

    if count == 4:
        got = lax.ppermute(summary, axis, [(0, 1), (2, 3)])
        got_move, got_own = got[:, :, :width], got[:, :, width:]
        pair = apply(move, own, got_own).astype(BF16)
        near = lax.ppermute(pair, axis, [(1, 2)])
        far = lax.ppermute(pair, axis, [(1, 3)])
        return apply(got_move, got_own, far) + near.astype(F32)
    state = passed_along(own, axis, 1)
    for _ in range(count - 2):
        state = passed_along(apply(move, own, state).astype(BF16), axis, 1)
    return state.astype(F32)


def on_device(
    query_raw, key_raw, value_raw, out_gate, log_decay, write_strength,
    conv_weight, norm_gain, out_weight, history_end,
):
    rows, channel_count = query_raw.shape
    heads = log_decay.shape[0]
    width = channel_count // heads
    rim = passed_along(
        jnp.stack([query_raw[-RIM:], key_raw[-RIM:], value_raw[-RIM:]]), "seq", 1
    )
    local, qeff, summary = front(
        rim, query_raw, key_raw, value_raw, log_decay, write_strength, conv_weight
    )
    state = carried_in(summary, "seq")
    owners = lax.axis_size("head")
    mine = lax.axis_index("head")
    tile = rows // owners
    dim = out_weight.shape[1]
    start = lax.axis_index("seq") * rows
    gain = norm_gain.reshape(1, width)

    def partial(owner):
        info = jnp.stack([start, owner, history_end[0]]).astype(jnp.int32)
        tiles = pl.BlockSpec((tile, channel_count), lambda i, s: (s[1], 0))
        return pl.pallas_call(
            out_kernel,
            grid_spec=pltpu.PrefetchScalarGridSpec(
                num_scalar_prefetch=1,
                grid=(1,),
                in_specs=[
                    pl.BlockSpec((heads, width, width), lambda i, s: (0, 0, 0)),
                    tiles, tiles, tiles,
                    pl.BlockSpec((1, width), lambda i, s: (0, 0)),
                    pl.BlockSpec((channel_count, dim), lambda i, s: (0, 0)),
                ],
                out_specs=pl.BlockSpec((tile, dim), lambda i, s: (0, 0)),
            ),
            out_shape=jax.ShapeDtypeStruct((tile, dim), BF16),
            compiler_params=pltpu.CompilerParams(vmem_limit_bytes=48 << 20),
            name="outputs",
        )(info, state, local, qeff, out_gate, gain, out_weight)

    def exchange(block, bit):
        return lax.ppermute(block, "head", [(i, i ^ bit) for i in range(owners)])

    def added(a, b):
        return (a.astype(F32) + b.astype(F32)).astype(BF16)

    if owners != 4:
        blocks = jnp.concatenate([partial(o) for o in range(owners)], axis=0)
        return lax.psum_scatter(blocks, "head", scatter_dimension=0, tiled=True)
    far_in = exchange(partial(mine ^ 3), 1)
    far = added(partial(mine ^ 2), far_in)
    far_got = exchange(far, 2)
    near_in = exchange(partial(mine ^ 1), 1)
    near = partial(mine).astype(F32) + near_in.astype(F32)
    return (near + far_got.astype(F32)).astype(BF16)


def solution(mesh):
    return jax.shard_map(
        on_device,
        mesh=mesh,
        in_specs=(
            P(("parts", "seq"), "head"),
            P(("parts", "seq"), "head"),
            P(("parts", "seq"), "head"),
            P(("parts", "seq"), "head"),
            P("head", ("parts", "seq")),
            P("head", ("parts", "seq")),
            P(None, None, "head"),
            P(),
            P("head", None),
            P("parts"),
        ),
        out_specs=P(("parts", "seq", "head"), None),
        check_vma=False,
    )
```

time: 223 us -> 117 us (0.52)
  waiting for transfers between devices: 89.2 us -> 31.5 us
  Pallas kernels: 105 us -> 51.7 us
  between operations: 14.1 us -> 0.79 us
  starting transfers between devices: 3.53 us -> 14.1 us
  local copies, waits for them, and re-layouts: 9.02 us -> 12.6 us
  other arithmetic: 0.09 us -> 2.92 us
    pallas_call x2 -> x6, Pallas kernels: 105 us -> 51.7 us  [the longest x1 22.7 us: front(): pl.pallas_call(summary_kernel, grid=(steps,), in_specs=[rims, block, bloc...]
    all_gather x1 -> x0, waiting for transfers between devices: 44.9 us -> none  [on_device(): gathered = lax.all_gather(summary, 'seq')]
    reduce_scatter x1 -> x0, waiting for transfers between devices: 41.3 us -> none  [on_device(): return lax.psum_scatter(partial, 'head', scatter_dimension=0, tiled=True)]
    ppermute x0 -> x6, waiting for transfers between devices: none -> 28.5 us  [the longest x3 15.4 us: exchange(): return lax.ppermute(block, 'head', [(i, i ^ bit) for i in range(owners)])]
    ppermute x0 -> x6, starting transfers between devices: none -> 10.6 us  [the longest x1 5.19 us: carried_in(): far = lax.ppermute(pair, axis, [(1, 3)])]
    unnamed x18 -> x34, local copies, waits for them, and re-layouts: 7.48 us -> 11.1 us
    convert_element_type x0 -> x2, other arithmetic: none -> 2.6 us  [the longest x1 1.37 us: added(): return (a.astype(F32) + b.astype(F32)).astype(BF16)]
  transfers between devices with their start and end apart: 3 -> 7, of which waited for: 3 -> 3; matrix products, arithmetic and copies ran while one was open for 0% -> 1% of each run, Pallas kernels for 0% -> 20%
where the time goes in v2:
time: 117 us; the launch traced here: 116 us
  Pallas kernels  51.7 us (44%)
  waiting for transfers between devices  31.5 us (27%)
  starting transfers between devices  14.1 us (12%)
  local copies, waits for them, and re-layouts  12.6 us (11%)
  other arithmetic  2.92 us (2%)
  matrix products  2.19 us (2%)
    pallas_call x1, Pallas kernels, front(): pl.pallas_call(summary_kernel, grid=(steps,), in_specs=[rims, block, bloc...  22.7 us
    pallas_call x4, Pallas kernels, partial(): pl.pallas_call(out_kernel, grid_spec=pltpu.PrefetchScalarGridSpec(num_sca...  19.5 us
    ppermute x3, waiting for transfers between devices, exchange(): return lax.ppermute(block, 'head', [(i, i ^ bit) for i in range(owners)])  15.4 us
    ppermute x1, waiting for transfers between devices, carried_in(): got = lax.ppermute(summary, axis, [(0, 1), (2, 3)])  13.1 us
    unnamed x34, local copies, waits for them, and re-layouts  11.1 us
    pallas_call x1, Pallas kernels, front(): pl.pallas_call(local_kernel, grid=(steps,), in_specs=[rims, block, prev,...  9.59 us
    ppermute x1, starting transfers between devices, carried_in(): far = lax.ppermute(pair, axis, [(1, 3)])  5.19 us
    ppermute x1, starting transfers between devices, passed_along(): return lax.ppermute(block, axis, route)  3.48 us
  transfers between devices with their start and end apart: 7, of which 3 were waited for; matrix products, arithmetic and copies ran while one was open for 1% of the time, Pallas kernels for 20%

profile of v2, /device:TPU:8, one launch (start us, length us, event | category | flops | bytes accessed | tf_op | source)
XLA Modules:
  0.0 115.8 jit_solution(8870978468029344195)
XLA Ops:
  1.6 3.5 %collective-permute-start = (bf16[3,16,1024]{2,1,0:T(8,128)(2,1)S(1)}, bf16[3,16,1024]{2,1,0:T(8,128)(2,1)S(1)}, u32[]{:S(2)}, u32[]{:S(2)}) collective-permute-start(bf16[3,16,1024]{2,1,0:T(8,128)(2,1)S(1)} %pad_maximum_fusion), channel_id=1, source_target_pairs={{0,4},{4,8},{8,12},{1,5},{5,9},{9,13},{2,6},{6,10},{10,14},{3,7},{... | collective-permute-start | bytes 294920 | tf_op jit(solution)/shard_map/ppermute | solution.py:260
  5.1 3.0 %collective-permute-done.rim_ref = bf16[3,16,1024]{2,1,0:T(8,128)(2,1)S(1)} collective-permute-done((bf16[3,16,1024]{2,1,0:T(8,128)(2,1)S(1)}, bf16[3,16,1024]{2,1,0:T(8,128)(2,1)S(1)}, u32[]{:S(2)}, u32[]{:S(2)}) %collective-permute-start) | collective-permute-done | bytes 98336 | tf_op jit(solution)/shard_map/ppermute | solution.py:260
  8.1 1.4 %copy-done.4 = bf16[768,1024]{1,0:T(8,128)(2,1)S(1)} copy-done((bf16[768,1024]{1,0:T(8,128)(2,1)S(1)}, bf16[768,1024]{1,0:T(8,128)(2,1)}, u32[]{:S(2)}) %copy-start.4) | copy-done | bytes 1572888
  9.5 1.4 %copy-done.5 = bf16[768,1024]{1,0:T(8,128)(2,1)S(1)} copy-done((bf16[768,1024]{1,0:T(8,128)(2,1)S(1)}, bf16[768,1024]{1,0:T(8,128)(2,1)}, u32[]{:S(2)}) %copy-start.5) | copy-done | bytes 1572888
  10.9 0.9 copy-done.8
  14.1 22.7 %summary.1 = (bf16[768,1024]{1,0:T(8,128)(2,1)S(1)}, bf16[768,2048]{1,0:T(8,128)(2,1)}, bf16[6,8,128,256]{3,2,1,0:T(8,128)(2,1)}, bf16[8,128,256]{2,1,0:T(8,128)(2,1)S(1)}) custom-call(bf16[3,16,1024]{2,1,0:T(8,128)(2,1)S(1)} %collective-permute-done.rim_ref, bf16[768,1024]{1,0:T(8,128)(2,1)S(1)} %copy-done.5, bf16[768,1024]{1,0:T(8,128)(2,1)S(1)} %copy-done.4, ...), custom_call_target="tpu_custom_call" | custom-call | tf_op jit(solution)/shard_map/summary/pallas_call | solution.py:203
  36.8 1.2 %copy-done.6 = bf16[768,1024]{1,0:T(8,128)(2,1)} copy-done((bf16[768,1024]{1,0:T(8,128)(2,1)}, bf16[768,1024]{1,0:T(8,128)(2,1)S(1)}, u32[]{:S(2)}) %copy-start.6) | copy-done | bytes 1572888
  38.0 1.3 %collective-permute-start.1 = (bf16[8,128,256]{2,1,0:T(8,128)(2,1)S(1)}, bf16[8,128,256]{2,1,0:T(8,128)(2,1)S(1)}, u32[]{:S(2)}, u32[]{:S(2)}) collective-permute-start(bf16[8,128,256]{2,1,0:T(8,128)(2,1)S(1)} %get-tuple-element.11), channel_id=1, source_target_pairs={{0,4},{8,12},{1,5},{9,13},{2,6},{10,14},{3,7},{11,15},{16,20},{24,... | collective-permute-start | bytes 1572872 | tf_op jit(solution)/shard_map/ppermute | solution.py:272
  39.3 13.1 %collective-permute-done.1 = bf16[8,128,256]{2,1,0:T(8,128)(2,1)S(1)} collective-permute-done((bf16[8,128,256]{2,1,0:T(8,128)(2,1)S(1)}, bf16[8,128,256]{2,1,0:T(8,128)(2,1)S(1)}, u32[]{:S(2)}, u32[]{:S(2)}) %collective-permute-start.1) | collective-permute-done | bytes 524320 | tf_op jit(solution)/shard_map/ppermute | solution.py:272
  53.3 5.2 %collective-permute-start.2 = (bf16[8,128,128]{2,1,0:T(8,128)(2,1)}, bf16[8,128,128]{2,1,0:T(8,128)(2,1)}, u32[]{:S(2)}, u32[]{:S(2)}) collective-permute-start(bf16[8,128,128]{2,1,0:T(8,128)(2,1)} %fusion.1), channel_id=1, source_target_pairs={{4,12},{5,13},{6,14},{7,15},{20,28},{21,29},{22,30},{23,31}} | collective-permute-start | bytes 786440 | tf_op jit(solution)/shard_map/ppermute | solution.py:276
  58.5 2.0 %collective-permute-start.3 = (bf16[8,128,128]{2,1,0:T(8,128)(2,1)}, bf16[8,128,128]{2,1,0:T(8,128)(2,1)}, u32[]{:S(2)}, u32[]{:S(2)}) collective-permute-start(bf16[8,128,128]{2,1,0:T(8,128)(2,1)} %fusion.1), channel_id=1, source_target_pairs={{4,8},{5,9},{6,10},{7,11},{20,24},{21,25},{22,26},{23,27}} | collective-permute-start | bytes 786440 | tf_op jit(solution)/shard_map/ppermute | solution.py:275
  61.3 1.4 %copy-done.3 = bf16[768,1024]{1,0:T(8,128)(2,1)S(1)} copy-done((bf16[768,1024]{1,0:T(8,128)(2,1)S(1)}, bf16[768,1024]{1,0:T(8,128)(2,1)}, u32[]{:S(2)}) %copy-start.3) | copy-done | bytes 1572888
  62.7 1.4 %copy-done.7 = bf16[768,1024]{1,0:T(8,128)(2,1)S(1)} copy-done((bf16[768,1024]{1,0:T(8,128)(2,1)S(1)}, bf16[768,1024]{1,0:T(8,128)(2,1)}, u32[]{:S(2)}) %copy-start.7) | copy-done | bytes 1572888
  64.1 9.6 %local.1 = (f32[768,1024]{1,0:T(8,128)}, bf16[768,1024]{1,0:T(8,128)(2,1)S(1)}) custom-call(bf16[3,16,1024]{2,1,0:T(8,128)(2,1)S(1)} %collective-permute-done.rim_ref, bf16[768,1024]{1,0:T(8,128)(2,1)S(1)} %copy-done.3, bf16[768,1024]{1,0:T(8,128)(2,1)S(1)} %copy-done.3, bf16[768,1024]{1,0:T(8,128)(2,1)S(1)} %copy-done.7, ...), custom_call_target="tpu_custom_call" | custom-call | tf_op jit(solution)/shard_map/local/pallas_call | solution.py:224
  73.7 1.3 %fusion.state_ref = f32[8,128,128]{2,1,0:T(8,128)S(1)} fusion(bf16[8,128,128]{2,1,0:T(8,128)(2,1)} %collective-permute-done.2, bf16[8,128,128]{2,1,0:T(8,128)(2,1)} %collective-permute-done.3, bf16[8,128,256]{2,1,0:T(8,128)(2,1)S(1)} %copy-done.16), kind=kOutput, calls=%fused_computation.3 | convolution fusion | flops 34078720 | bytes 1572864 | tf_op jit(solution)/shard_map/hij,hjk->hik/dot_general | solution.py:269
  75.0 5.6 %outputs.7 = bf16[192,2304]{1,0:T(8,128)(2,1)} custom-call(s32[3]{0:T(128)S(1)} %add_add_fusion.3.info_ref, f32[8,128,128]{2,1,0:T(8,128)S(1)} %fusion.state_ref, f32[768,1024]{1,0:T(8,128)} %get-tuple-element.15.local_ref, bf16[768,1024]{1,0:T(8,128)(2,1)S(1)} %get-tuple-element.16.qeff_ref, bf16[768,1024]{1,0:T(8,128)(2,1)S(1)} %copy-done, ...), custom_call_target="tpu_custom_call" | custom-call | tf_op jit(solution)/shard_map/outputs/pallas_call | solution.py:308
  80.7 1.0 copy-done.2
  81.7 4.6 %outputs.5 = bf16[192,2304]{1,0:T(8,128)(2,1)S(1)} custom-call(s32[3]{0:T(128)S(1)} %add_add_fusion.1.info_ref, f32[8,128,128]{2,1,0:T(8,128)S(1)} %copy-done.2, f32[768,1024]{1,0:T(8,128)} %get-tuple-element.15.local_ref, bf16[768,1024]{1,0:T(8,128)(2,1)S(1)} %get-tuple-element.16.qeff_ref, bf16[768,1024]{1,0:T(8,128)(2,1)S(1)} %copy-done, ...), custom_call_target="tpu_custom_call" | custom-call | tf_op jit(solution)/shard_map/outputs/pallas_call | solution.py:308
  87.0 4.6 %outputs.6 = bf16[192,2304]{1,0:T(8,128)(2,1)S(1)} custom-call(s32[3]{0:T(128)S(1)} %add_add_fusion.2.info_ref, f32[8,128,128]{2,1,0:T(8,128)S(1)} %copy-done.2, f32[768,1024]{1,0:T(8,128)} %get-tuple-element.15.local_ref, bf16[768,1024]{1,0:T(8,128)(2,1)S(1)} %get-tuple-element.16.qeff_ref, bf16[768,1024]{1,0:T(8,128)(2,1)S(1)} %copy-done, ...), custom_call_target="tpu_custom_call" | custom-call | tf_op jit(solution)/shard_map/outputs/pallas_call | solution.py:308
  91.6 1.4 %add_convert_fusion.1 = bf16[192,2304]{1,0:T(8,128)(2,1)S(1)} fusion(bf16[192,2304]{1,0:T(8,128)(2,1)} %collective-permute-done.5, bf16[192,2304]{1,0:T(8,128)(2,1)S(1)} %outputs.6), kind=kLoop, calls=%fused_computation.1 | loop fusion | flops 1769472 | bytes 2654208 | tf_op jit(solution)/shard_map/convert_element_type | solution.py:330
  93.0 1.6 %collective-permute-start.6 = (bf16[192,2304]{1,0:T(8,128)(2,1)S(1)}, bf16[192,2304]{1,0:T(8,128)(2,1)S(1)}, u32[]{:S(2)}, u32[]{:S(2)}) collective-permute-start(bf16[192,2304]{1,0:T(8,128)(2,1)S(1)} %add_convert_fusion.1), channel_id=1, source_target_pairs={{0,2},{1,3},{2,0},{3,1},{4,6},{5,7},{6,4},{7,5},{8,10},{9,11},{10,... | collective-permute-start | bytes 2654216 | tf_op jit(solution)/shard_map/ppermute | solution.py:327
  94.6 4.6 %outputs.4 = bf16[192,2304]{1,0:T(8,128)(2,1)S(1)} custom-call(s32[3]{0:T(128)S(1)} %add_add_fusion.info_ref, f32[8,128,128]{2,1,0:T(8,128)S(1)} %copy-done.2, f32[768,1024]{1,0:T(8,128)} %get-tuple-element.15.local_ref, bf16[768,1024]{1,0:T(8,128)(2,1)S(1)} %get-tuple-element.16.qeff_ref, bf16[768,1024]{1,0:T(8,128)(2,1)S(1)} %copy-done, ...), custom_call_target="tpu_custom_call" | custom-call | tf_op jit(solution)/shard_map/outputs/pallas_call | solution.py:308
  99.3 15.4 %collective-permute-done.6 = bf16[192,2304]{1,0:T(8,128)(2,1)S(1)} collective-permute-done((bf16[192,2304]{1,0:T(8,128)(2,1)S(1)}, bf16[192,2304]{1,0:T(8,128)(2,1)S(1)}, u32[]{:S(2)}, u32[]{:S(2)}) %collective-permute-start.6) | collective-permute-done | bytes 884768 | tf_op jit(solution)/shard_map/ppermute | solution.py:327
  114.6 1.2 %add_convert_fusion = bf16[192,2304]{1,0:T(8,128)(2,1)} fusion(bf16[192,2304]{1,0:T(8,128)(2,1)S(1)} %collective-permute-done.6, bf16[192,2304]{1,0:T(8,128)(2,1)S(1)} %collective-permute-done.4, bf16[192,2304]{1,0:T(8,128)(2,1)S(1)} %outputs.4), kind=kLoop, calls=%fused_computation | loop fusion | flops 2654208 | bytes 3538944 | tf_op jit(solution)/shard_map/convert_element_type | solution.py:340
  (41 shorter events, 5.7 us)
Async XLA Ops:
  1.5 59.7 %copy-start.10 = (f32[3,4,1024]{2,1,0:T(4,128)S(1)}, f32[3,4,1024]{2,1,0:T(4,128)}, u32[]{:S(2)}) copy-start(f32[3,4,1024]{2,1,0:T(4,128)} %taps_ref.3) | copy-start | bytes 147460
  1.5 59.7 %copy-start.12 = (f32[8,768]{1,0:T(8,128)S(1)}, f32[8,768]{1,0:T(8,128)}, u32[]{:S(2)}) copy-start(f32[8,768]{1,0:T(8,128)} %dec_ref.3) | copy-start | bytes 73732
  1.6 6.5 %collective-permute-start = (bf16[3,16,1024]{2,1,0:T(8,128)(2,1)S(1)}, bf16[3,16,1024]{2,1,0:T(8,128)(2,1)S(1)}, u32[]{:S(2)}, u32[]{:S(2)}) collective-permute-start(bf16[3,16,1024]{2,1,0:T(8,128)(2,1)S(1)} %pad_maximum_fusion), channel_id=1, source_target_pairs={{0,4},{4,8},{8,12},{1,5},{5,9},{9,13},{2,6},{6,10},{10,14},{3,7},{... | collective-permute-start | bytes 294920 | tf_op jit(solution)/shard_map/ppermute | solution.py:260
  8.1 1.4 %copy-start.4 = (bf16[768,1024]{1,0:T(8,128)(2,1)S(1)}, bf16[768,1024]{1,0:T(8,128)(2,1)}, u32[]{:S(2)}) copy-start(bf16[768,1024]{1,0:T(8,128)(2,1)} %vp_ref.1) | copy-start | bytes 4718596
  9.5 1.4 %copy-start.5 = (bf16[768,1024]{1,0:T(8,128)(2,1)S(1)}, bf16[768,1024]{1,0:T(8,128)(2,1)}, u32[]{:S(2)}) copy-start(bf16[768,1024]{1,0:T(8,128)(2,1)} %kp_ref.1) | copy-start | bytes 4718596
  10.9 0.9 copy-start.8
  11.8 0.8 copy-start.9
  12.6 0.7 copy-start.11
  13.4 0.7 copy-start.13
  36.8 1.2 %copy-start.6 = (bf16[768,1024]{1,0:T(8,128)(2,1)}, bf16[768,1024]{1,0:T(8,128)(2,1)S(1)}, u32[]{:S(2)}) copy-start(bf16[768,1024]{1,0:T(8,128)(2,1)S(1)} %get-tuple-element.12.keys_ref) | copy-start | bytes 4718596
  38.0 14.4 %collective-permute-start.1 = (bf16[8,128,256]{2,1,0:T(8,128)(2,1)S(1)}, bf16[8,128,256]{2,1,0:T(8,128)(2,1)S(1)}, u32[]{:S(2)}, u32[]{:S(2)}) collective-permute-start(bf16[8,128,256]{2,1,0:T(8,128)(2,1)S(1)} %get-tuple-element.11), channel_id=1, source_target_pairs={{0,4},{8,12},{1,5},{9,13},{2,6},{10,14},{3,7},{11,15},{16,20},{24,... | collective-permute-start | bytes 1572872 | tf_op jit(solution)/shard_map/ppermute | solution.py:272
  52.4 0.9 copy-start.15
  53.3 20.4 %collective-permute-start.2 = (bf16[8,128,128]{2,1,0:T(8,128)(2,1)}, bf16[8,128,128]{2,1,0:T(8,128)(2,1)}, u32[]{:S(2)}, u32[]{:S(2)}) collective-permute-start(bf16[8,128,128]{2,1,0:T(8,128)(2,1)} %fusion.1), channel_id=1, source_target_pairs={{4,12},{5,13},{6,14},{7,15},{20,28},{21,29},{22,30},{23,31}} | collective-permute-start | bytes 786440 | tf_op jit(solution)/shard_map/ppermute | solution.py:276
  58.5 15.2 %collective-permute-start.3 = (bf16[8,128,128]{2,1,0:T(8,128)(2,1)}, bf16[8,128,128]{2,1,0:T(8,128)(2,1)}, u32[]{:S(2)}, u32[]{:S(2)}) collective-permute-start(bf16[8,128,128]{2,1,0:T(8,128)(2,1)} %fusion.1), channel_id=1, source_target_pairs={{4,8},{5,9},{6,10},{7,11},{20,24},{21,25},{22,26},{23,27}} | collective-permute-start | bytes 786440 | tf_op jit(solution)/shard_map/ppermute | solution.py:275
  61.3 1.4 %copy-start.3 = (bf16[768,1024]{1,0:T(8,128)(2,1)S(1)}, bf16[768,1024]{1,0:T(8,128)(2,1)}, u32[]{:S(2)}) copy-start(bf16[768,1024]{1,0:T(8,128)(2,1)} %qp_ref.1) | copy-start | bytes 4718596
  62.7 1.4 %copy-start.7 = (bf16[768,1024]{1,0:T(8,128)(2,1)S(1)}, bf16[768,1024]{1,0:T(8,128)(2,1)}, u32[]{:S(2)}) copy-start(bf16[768,1024]{1,0:T(8,128)(2,1)} %copy-done.6) | copy-start | bytes 4718596
  64.1 9.6 %copy-start.16 = (bf16[8,128,256]{2,1,0:T(8,128)(2,1)S(1)}, bf16[8,128,256]{2,1,0:T(8,128)(2,1)}, u32[]{:S(2)}) copy-start(bf16[8,128,256]{2,1,0:T(8,128)(2,1)} %copy-done.15) | copy-start | bytes 1572868
  64.1 10.9 %copy-start = (bf16[768,1024]{1,0:T(8,128)(2,1)S(1)}, bf16[768,1024]{1,0:T(8,128)(2,1)}, u32[]{:S(2)}) copy-start(bf16[768,1024]{1,0:T(8,128)(2,1)} %gate_ref.7) | copy-start | bytes 4718596
  64.1 10.9 %copy-start.14 = (f32[128]{0:T(128)S(1)}, f32[128]{0:T(128)}, u32[]{:S(2)}) copy-start(f32[128]{0:T(128)} %param.18) | copy-start | bytes 1540
  74.9 5.6 %copy-start.1 = (f32[8,128,128]{2,1,0:T(8,128)}, f32[8,128,128]{2,1,0:T(8,128)S(1)}, u32[]{:S(2)}) copy-start(f32[8,128,128]{2,1,0:T(8,128)S(1)} %fusion.state_ref) | copy-start | bytes 1572868
  80.5 11.1 %collective-permute-start.5 = (bf16[192,2304]{1,0:T(8,128)(2,1)}, bf16[192,2304]{1,0:T(8,128)(2,1)}, u32[]{:S(2)}, u32[]{:S(2)}) collective-permute-start(bf16[192,2304]{1,0:T(8,128)(2,1)} %outputs.7), channel_id=1, source_target_pairs={{0,1},{1,0},{2,3},{3,2},{4,5},{5,4},{6,7},{7,6},{8,9},{9,8},{10,11... | collective-permute-start | bytes 2654216 | tf_op jit(solution)/shard_map/ppermute | solution.py:327
  80.7 1.0 copy-start.2
  86.4 12.9 %collective-permute-start.4 = (bf16[192,2304]{1,0:T(8,128)(2,1)S(1)}, bf16[192,2304]{1,0:T(8,128)(2,1)S(1)}, u32[]{:S(2)}, u32[]{:S(2)}) collective-permute-start(bf16[192,2304]{1,0:T(8,128)(2,1)S(1)} %outputs.5), channel_id=1, source_target_pairs={{0,1},{1,0},{2,3},{3,2},{4,5},{5,4},{6,7},{7,6},{8,9},{9,8},{10,11... | collective-permute-start | bytes 2654216 | tf_op jit(solution)/shard_map/ppermute | solution.py:327
  93.0 21.6 %collective-permute-start.6 = (bf16[192,2304]{1,0:T(8,128)(2,1)S(1)}, bf16[192,2304]{1,0:T(8,128)(2,1)S(1)}, u32[]{:S(2)}, u32[]{:S(2)}) collective-permute-start(bf16[192,2304]{1,0:T(8,128)(2,1)S(1)} %add_convert_fusion.1), channel_id=1, source_target_pairs={{0,2},{1,3},{2,0},{3,1},{4,6},{5,7},{6,4},{7,5},{8,10},{9,11},{10,... | collective-permute-start | bytes 2654216 | tf_op jit(solution)/shard_map/ppermute | solution.py:327

commit v3 on v2

--- a/solution.py
+++ b/solution.py
@@ -1,3 +1,5 @@
+import functools
+
 import jax
 import jax.numpy as jnp
 import numpy as np
@@ -9,6 +11,8 @@
 CHUNK = 128
 RIM = 16
 GROUP = 8
+SUBS = 2
+PIECES = 1
 F32 = jnp.float32
 BF16 = jnp.bfloat16
 NN = (((1,), (0,)), ((), ()))
@@ -43,6 +47,10 @@
     return (x * (lax.rsqrt(jnp.sum(x * x, axis=-1, keepdims=True) + 1e-06) * scale)).astype(BF16)
 
 
+def placed(*arrays):
+    return [pltpu.with_memory_space_constraint(x, pltpu.HBM) for x in arrays]
+
+
 def positions(c):
     return (
         lax.broadcasted_iota(jnp.int32, (c, c), 0),
@@ -61,7 +69,8 @@
     keys_ref, fresh_ref, start_ref, summary_ref, state_ref,
 ):
     step = pl.program_id(0)
-    c = k_ref.shape[0]
+    c = CHUNK
+    subs = k_ref.shape[0] // c
     heads = dec_ref.shape[0]
     width = k_ref.shape[1] // heads
 
@@ -76,60 +85,74 @@
     ri, ci = positions(c)
     tril = jnp.where(ci <= ri, 1.0, 0.0).astype(F32)
     eye = jnp.where(ci == ri, 1.0, 0.0).astype(F32)
-    dec = dec_ref[...]
-    wr = wr_ref[...]
-    cum_row = exact(dec, tril, NT)
-    cum_col = exact(tril, dec, NT)
-    wr_col = exact(eye, wr, NT)
-    last = cum_row[:, c - 1 : c]
-    wg_row = wr * jnp.exp(cum_row)
-    kout_row = jnp.exp(last - cum_row)
-    last_decay = jnp.exp(last)
     first = step == 0
-
-    for g in range(0, heads, GROUP):
-        hs = range(g, g + GROUP)
-        sls = [slice(h * width, (h + 1) * width) for h in hs]
-        n = range(GROUP)
-        k = [unit(channels(rim_ref, k_ref, kp_ref, taps_ref, 1, sl, first), 1.0) for sl in sls]
-        for i in n:
-            keys_ref[:, sls[i]] = k[i]
-        gram = [mm(x, x, NT) for x in k]
-        low = []
-        for i in n:
-            h = hs[i]
-            gap = cum_col[:, h : h + 1] - cum_row[h : h + 1, :]
-            decay = jnp.exp(jnp.minimum(gap, 0.0)) * wr_col[:, h : h + 1]
-            low.append(jnp.where(ci < ri, gram[i] * decay, 0.0).astype(BF16))
-        inv = [eye - (x * mask_ref[0]).astype(F32) for x in low]
-        level = 1
-        while (1 << level) < c:
-            mask = mask_ref[level]
-            invb = [x.astype(BF16) for x in inv]
-            inner = [mm(low[i] * mask, invb[i]).astype(BF16) for i in n]
-            inv = [inv[i] - mm(invb[i], inner[i]) for i in n]
-            level += 1
-        v = [channels(rim_ref, v_ref, vp_ref, taps_ref, 2, sl, first).astype(BF16) for sl in sls]
-        key_mix = [mm((inv[i] * wg_row[hs[i] : hs[i] + 1, :]).astype(BF16), k[i]).astype(BF16) for i in n]
-        value_mix = [mm((inv[i] * wr[hs[i] : hs[i] + 1, :]).astype(BF16), v[i]) for i in n]
-        k_out = [(k[i].astype(F32).T * kout_row[hs[i] : hs[i] + 1, :]).astype(BF16) for i in n]
-        start = [state_ref[h].astype(BF16) for h in hs]
-        for i in n:
-            start_ref[0, hs[i]] = start[i]
-        read = [mm(key_mix[i], start[i]) for i in n]
+    dec = [dec_ref[:, s * c : (s + 1) * c] for s in range(subs)]
+    wr = [wr_ref[:, s * c : (s + 1) * c] for s in range(subs)]
+    cum_row = [exact(x, tril, NT) for x in dec]
+    cum_col = [exact(tril, x, NT) for x in dec]
+    wr_col = [exact(eye, x, NT) for x in wr]
+    last = [x[:, c - 1 : c] for x in cum_row]
+    wg_row = [wr[s] * jnp.exp(cum_row[s]) for s in range(subs)]
+    kout_row = [jnp.exp(last[s] - cum_row[s]) for s in range(subs)]
+    last_decay = [jnp.exp(x) for x in last]
+
+    units = [(s, h) for s in range(subs) for h in range(heads)]
+    n = range(len(units))
+
+    def lanes(h):
+        return slice(h * width, (h + 1) * width)
+
+    def row(x, i):
+        s, h = units[i]
+        return x[s][h : h + 1, :]
+
+    def col(x, i):
+        s, h = units[i]
+        return x[s][:, h : h + 1]
+
+    def split(x):
+        return {(s, h): x[h][s * c : (s + 1) * c] for s, h in units}
+
+    k_all = [unit(channels(rim_ref, k_ref, kp_ref, taps_ref, 1, lanes(h), first), 1.0) for h in range(heads)]
+    for h in range(heads):
+        keys_ref[:, lanes(h)] = k_all[h]
+    k = [k_all[h][s * c : (s + 1) * c] for s, h in units]
+    gram = [mm(x, x, NT) for x in k]
+    low = []
+    for i in n:
+        gap = col(cum_col, i) - row(cum_row, i)
+        decay = jnp.exp(jnp.minimum(gap, 0.0)) * col(wr_col, i)
+        low.append(jnp.where(ci < ri, gram[i] * decay, 0.0).astype(BF16))
+    inv = [eye - (x * mask_ref[0]).astype(F32) for x in low]
+    level = 1
+    while (1 << level) < c:
+        mask = mask_ref[level]
+        invb = [x.astype(BF16) for x in inv]
+        inner = [mm(low[i] * mask, invb[i]).astype(BF16) for i in n]
+        inv = [inv[i] - mm(invb[i], inner[i]) for i in n]
+        level += 1
+    v_all = [channels(rim_ref, v_ref, vp_ref, taps_ref, 2, lanes(h), first).astype(BF16) for h in range(heads)]
+    v = [v_all[h][s * c : (s + 1) * c] for s, h in units]
+    key_mix = [mm((inv[i] * row(wg_row, i)).astype(BF16), k[i]).astype(BF16) for i in n]
+    value_mix = [mm((inv[i] * row(wr, i)).astype(BF16), v[i]) for i in n]
+    k_out = [(k[i].astype(F32).T * row(kout_row, i)).astype(BF16) for i in n]
+    for s in range(subs):
+        at = s * heads
+        start = [state_ref[h].astype(BF16) for h in range(heads)]
+        for h in range(heads):
+            start_ref[s, h] = start[h]
+        read = [mm(key_mix[at + h], start[h]) for h in range(heads)]
         fresh = [
             jnp.concatenate(
-                [-read[i][:, :width], value_mix[i] - read[i][:, width:]], axis=1
+                [-read[h][:, :width], value_mix[at + h] - read[h][:, width:]], axis=1
             ).astype(BF16)
-            for i in n
+            for h in range(heads)
         ]
-        for i in n:
-            h = hs[i]
-            fresh_ref[:, 2 * h * width : 2 * (h + 1) * width] = fresh[i]
-        both = [mm(k_out[i], fresh[i]) for i in n]
-        for i in n:
-            h = hs[i]
-            state_ref[h] = last_decay[h : h + 1, :] * state_ref[h] + both[i]
+        for h in range(heads):
+            fresh_ref[s * c : (s + 1) * c, 2 * h * width : 2 * (h + 1) * width] = fresh[h]
+        both = [mm(k_out[at + h], fresh[h]) for h in range(heads)]
+        for h in range(heads):
+            state_ref[h] = last_decay[s][h : h + 1, :] * state_ref[h] + both[h]
 
     @pl.when(step == pl.num_programs(0) - 1)
     def _():
@@ -137,10 +160,10 @@
 
 
 def local_kernel(
-    rim_ref, q_ref, qp_ref, keys_ref, fresh_ref, start_ref, dec_ref, taps_ref,
-    local_ref, qeff_ref,
+    begin, rim_ref, q_ref, qp_ref, keys_ref, fresh_ref, start_ref, dec_ref, taps_ref, *rest
 ):
-    step = pl.program_id(0)
+    local_ref, qeff_ref = rest[-2:]
+    step = pl.program_id(0) + begin
     c = q_ref.shape[0]
     heads = dec_ref.shape[0]
     width = q_ref.shape[1] // heads
@@ -200,40 +223,63 @@
     taps = pl.BlockSpec((3, 4, channel_count), lambda i: (0, 0, 0))
     starts = pl.BlockSpec((1, heads, width, 2 * width), lambda i: (i, 0, 0, 0))
     params = pltpu.CompilerParams(vmem_limit_bytes=48 << 20)
+    subs = SUBS if steps % SUBS == 0 else 1
+    big = pl.BlockSpec((subs * c, channel_count), lambda i: (i, 0))
     keys, fresh, start, summary = pl.pallas_call(
         summary_kernel,
-        grid=(steps,),
+        grid=(steps // subs,),
         in_specs=[
-            rims, block, block, prev, prev, gates, gates, taps,
+            rims, big, big,
+            pl.BlockSpec((RIM, channel_count), lambda i: (jnp.maximum(i * per * subs - 1, 0), 0)),
+            pl.BlockSpec((RIM, channel_count), lambda i: (jnp.maximum(i * per * subs - 1, 0), 0)),
+            pl.BlockSpec((heads, subs * c), lambda i: (0, i)),
+            pl.BlockSpec((heads, subs * c), lambda i: (0, i)), taps,
             pl.BlockSpec(masks.shape, lambda i: (0, 0, 0)),
         ],
         out_specs=[
-            block, wide, starts,
+            big,
+            pl.BlockSpec((subs * c, 2 * channel_count), lambda i: (i, 0)),
+            pl.BlockSpec((subs, heads, width, 2 * width), lambda i: (i, 0, 0, 0)),
             pl.BlockSpec((heads, width, 2 * width), lambda i: (0, 0, 0)),
         ],
         out_shape=[
-            jax.ShapeDtypeStruct((rows, channel_count), BF16),
-            jax.ShapeDtypeStruct((rows, 2 * channel_count), BF16),
-            jax.ShapeDtypeStruct((steps, heads, width, 2 * width), BF16),
+            pltpu.HBM((rows, channel_count), BF16),
+            pltpu.HBM((rows, 2 * channel_count), BF16),
+            pltpu.HBM((steps, heads, width, 2 * width), BF16),
             jax.ShapeDtypeStruct((heads, width, 2 * width), BF16),
         ],
         scratch_shapes=[pltpu.VMEM((heads, width, 2 * width), F32)],
         compiler_params=params,
         name="summary",
-    )(rim, key_raw, value_raw, key_raw, value_raw, log_decay, write_strength, conv_weight, masks)
-    local, qeff = pl.pallas_call(
-        local_kernel,
-        grid=(steps,),
-        in_specs=[rims, block, prev, block, wide, starts, gates, taps],
-        out_specs=[block, block],
-        out_shape=[
-            jax.ShapeDtypeStruct((rows, channel_count), F32),
-            jax.ShapeDtypeStruct((rows, channel_count), BF16),
-        ],
-        compiler_params=params,
-        name="local",
-    )(rim, query_raw, query_raw, keys, fresh, start, log_decay, conv_weight)
-    return local, qeff, summary
+    )(rim, *placed(key_raw, value_raw, key_raw, value_raw, log_decay, write_strength, conv_weight, masks))
+    first = steps // 2
+
+    def local_part(begin, count, done, rim, keys, fresh, start):
+        def at(spec):
+            return pl.BlockSpec(spec.block_shape, lambda i: spec.index_map(i + begin))
+
+        return pl.pallas_call(
+            functools.partial(local_kernel, begin),
+            grid=(count,),
+            in_specs=[rims, *map(at, (block, prev, block, wide, starts, gates)), taps]
+            + [pl.BlockSpec(memory_space=pl.ANY)] * len(done),
+            out_specs=[at(block), at(block)],
+            out_shape=[
+                pltpu.HBM((rows, channel_count), F32),
+                pltpu.HBM((rows, channel_count), BF16),
+            ],
+            input_output_aliases={8 + i: i for i in range(len(done))},
+            compiler_params=params,
+            name="local",
+        )(rim, *placed(query_raw, query_raw, keys, fresh, start, log_decay, conv_weight, *done))
+
+    def early():
+        return local_part(0, first, (), rim, keys, fresh, start)
+
+    def late(done):
+        return local_part(first, steps - first, done, rim, keys, fresh, start)
+
+    return early, late, summary
 
 
 def out_kernel(
@@ -251,7 +297,8 @@
         g = gate_ref[:, sl].astype(F32)
         o = o * norm * gain_ref[...] * (g * sigmoid(g))
         gated.append(jnp.where(valid, o, 0.0).astype(BF16))
-    out_ref[...] = mm(jnp.concatenate(gated, axis=1), weight_ref[...]).astype(BF16)
+    gated = jnp.concatenate(gated, axis=1)
+    out_ref[...] = mm(gated, weight_ref[...]).astype(BF16)
 
 
 def passed_along(block, axis, distance):
@@ -260,7 +307,7 @@
     return lax.ppermute(block, axis, route)
 
 
-def carried_in(summary, axis):
+def carried_in(summary, axis, early, late):
     width = summary.shape[1]
     count = lax.axis_size(axis)
     move, own = summary[:, :, :width], summary[:, :, width:]
@@ -269,16 +316,20 @@
         return jnp.einsum("hij,hjk->hik", a, s, preferred_element_type=F32) + b.astype(F32)
 
     if count == 4:
-        got = lax.ppermute(summary, axis, [(0, 1), (2, 3)])
-        got_move, got_own = got[:, :, :width], got[:, :, width:]
+        got_own = lax.ppermute(own, axis, [(0, 1), (2, 3)])
+        done = early()
+        got_own, done = lax.optimization_barrier((got_own, done))
         pair = apply(move, own, got_own).astype(BF16)
+        far = lax.ppermute(pair, axis, [(1, 3)])
         near = lax.ppermute(pair, axis, [(1, 2)])
-        far = lax.ppermute(pair, axis, [(1, 3)])
-        return apply(got_move, got_own, far) + near.astype(F32)
+        move, done, pair = lax.optimization_barrier((move, done, pair))
+        got_move = lax.ppermute(move, axis, [(2, 3)])
+        done = late(done)
+        return apply(got_move, got_own, far) + near.astype(F32), *done
     state = passed_along(own, axis, 1)
     for _ in range(count - 2):
         state = passed_along(apply(move, own, state).astype(BF16), axis, 1)
-    return state.astype(F32)
+    return state.astype(F32), *late(early())
 
 
 def on_device(
@@ -291,20 +342,23 @@
     rim = passed_along(
         jnp.stack([query_raw[-RIM:], key_raw[-RIM:], value_raw[-RIM:]]), "seq", 1
     )
-    local, qeff, summary = front(
+    early, late, summary = front(
         rim, query_raw, key_raw, value_raw, log_decay, write_strength, conv_weight
     )
-    state = carried_in(summary, "seq")
+    state, local, qeff = carried_in(summary, "seq", early, late)
     owners = lax.axis_size("head")
     mine = lax.axis_index("head")
-    tile = rows // owners
     dim = out_weight.shape[1]
     start = lax.axis_index("seq") * rows
     gain = norm_gain.reshape(1, width)
 
-    def partial(owner):
-        info = jnp.stack([start, owner, history_end[0]]).astype(jnp.int32)
+    def partial(owner, piece=0, pieces=1, after=None, resident=False):
+        tile = rows // owners // pieces
+        info = jnp.stack([start, owner * pieces + piece, history_end[0]]).astype(jnp.int32)
+        if after is not None:
+            info, after = lax.optimization_barrier((info, after))
         tiles = pl.BlockSpec((tile, channel_count), lambda i, s: (s[1], 0))
+        weight = out_weight if resident else placed(out_weight)[0]
         return pl.pallas_call(
             out_kernel,
             grid_spec=pltpu.PrefetchScalarGridSpec(
@@ -314,14 +368,16 @@
                     pl.BlockSpec((heads, width, width), lambda i, s: (0, 0, 0)),
                     tiles, tiles, tiles,
                     pl.BlockSpec((1, width), lambda i, s: (0, 0)),
-                    pl.BlockSpec((channel_count, dim), lambda i, s: (0, 0)),
+                    pl.BlockSpec(memory_space=pltpu.VMEM)
+                    if resident
+                    else pl.BlockSpec((channel_count, dim), lambda i, s: (0, 0)),
                 ],
                 out_specs=pl.BlockSpec((tile, dim), lambda i, s: (0, 0)),
             ),
             out_shape=jax.ShapeDtypeStruct((tile, dim), BF16),
-            compiler_params=pltpu.CompilerParams(vmem_limit_bytes=48 << 20),
+            compiler_params=pltpu.CompilerParams(vmem_limit_bytes=24 << 20),
             name="outputs",
-        )(info, state, local, qeff, out_gate, gain, out_weight)
+        )(info, state, *placed(local, qeff, out_gate, gain), weight)
 
     def exchange(block, bit):
         return lax.ppermute(block, "head", [(i, i ^ bit) for i in range(owners)])
@@ -332,12 +388,22 @@
     if owners != 4:
         blocks = jnp.concatenate([partial(o) for o in range(owners)], axis=0)
         return lax.psum_scatter(blocks, "head", scatter_dimension=0, tiled=True)
-    far_in = exchange(partial(mine ^ 3), 1)
-    far = added(partial(mine ^ 2), far_in)
-    far_got = exchange(far, 2)
-    near_in = exchange(partial(mine ^ 1), 1)
-    near = partial(mine).astype(F32) + near_in.astype(F32)
-    return (near + far_got.astype(F32)).astype(BF16)
+    far, far_got = None, []
+    for piece in range(PIECES):
+        sent = partial(mine ^ 3, piece, PIECES, far, resident=piece == 0)
+        far_in = exchange(sent, 1)
+        far = added(partial(mine ^ 2, piece, PIECES, sent), far_in)
+        far_got.append(exchange(far, 2))
+    near_in = exchange(partial(mine ^ 1, after=far), 1)
+    near = partial(mine, after=far).astype(F32) + near_in.astype(F32)
+    tile = near.shape[0] // PIECES
+    return jnp.concatenate(
+        [
+            (near[i * tile : (i + 1) * tile] + got.astype(F32)).astype(BF16)
+            for i, got in enumerate(far_got)
+        ],
+        axis=0,
+    )
 
 
 def solution(mesh):

time: 117 us -> 85.5 us (0.73)
  waiting for transfers between devices: 31.5 us -> 14.6 us
  local copies, waits for them, and re-layouts: 12.6 us -> 1.68 us
  matrix products: 2.19 us -> 0.44 us
  other arithmetic: 2.92 us -> 1.69 us
  Pallas kernels: 51.7 us -> 50.5 us
    ppermute x1 -> x2, waiting for transfers between devices: 13.1 us -> 1.16 us  [the longest x1 1.15 us: carried_in(): got_own = lax.ppermute(own, axis, [(0, 1), (2, 3)])]
    unnamed x34 -> x4, local copies, waits for them, and re-layouts: 11.1 us -> 0.01 us
    ppermute x3, waiting for transfers between devices: 15.4 us -> 10.4 us  [exchange(): return lax.ppermute(block, 'head', [(i, i ^ bit) for i in range(owners)])]
    dot_general x2, matrix products: 2.19 us -> 0.44 us  [apply(): jnp.einsum('hij,hjk->hik', a, s, preferred_element_type=F32) + b.astype(F32)]
    pallas_call x4, Pallas kernels: 19.5 us -> 18.2 us  [partial(): pl.pallas_call(out_kernel, grid_spec=pltpu.PrefetchScalarGridSpec(num_sca...]
    pallas_call x2 -> x3, Pallas kernels: 32.3 us -> 32.3 us  [the longest x1 19.5 us: front(): pl.pallas_call(summary_kernel, grid=(steps // subs,), in_specs=[rims, big...]
  transfers between devices with their start and end apart: 7 -> 8, of which waited for: 3 -> 3; matrix products, arithmetic and copies ran while one was open for 1% -> 0% of each run, Pallas kernels for 20% -> 33%
where the time goes in v3:
time: 85.5 us; the launch traced here: 84.3 us
  Pallas kernels  50.5 us (59%)
  waiting for transfers between devices  14.6 us (17%)
  starting transfers between devices  14.5 us (17%)
  other arithmetic  1.69 us (2%)
  local copies, waits for them, and re-layouts  1.68 us (2%)
    pallas_call x1, Pallas kernels, front(): pl.pallas_call(summary_kernel, grid=(steps // subs,), in_specs=[rims, big...  19.5 us
    pallas_call x4, Pallas kernels, partial(): pl.pallas_call(out_kernel, grid_spec=pltpu.PrefetchScalarGridSpec(num_sca...  18.2 us
    pallas_call x2, Pallas kernels, local_part(): pl.pallas_call(functools.partial(local_kernel, begin), grid=(count,), in_...  12.8 us
    ppermute x3, waiting for transfers between devices, exchange(): return lax.ppermute(block, 'head', [(i, i ^ bit) for i in range(owners)])  10.4 us
    ppermute x1, starting transfers between devices, carried_in(): far = lax.ppermute(pair, axis, [(1, 3)])  5.13 us
    ppermute x1, starting transfers between devices, passed_along(): return lax.ppermute(block, axis, route)  3.48 us
    ppermute x1, waiting for transfers between devices, passed_along(): return lax.ppermute(block, axis, route)  3.02 us
    ppermute x1, starting transfers between devices, carried_in(): near = lax.ppermute(pair, axis, [(1, 2)])  2.05 us
  transfers between devices with their start and end apart: 8, of which 3 were waited for; matrix products, arithmetic and copies ran while one was open for 0% of the time, Pallas kernels for 33%

profile of v3, /device:TPU:8, one launch (start us, length us, event | category | flops | bytes accessed | tf_op | source)
XLA Modules:
  0.0 84.3 jit_solution(4102174278715236975)
XLA Ops:
  0.0 0.8 slice_bitcast_fusion.2
  0.8 0.8 slice_bitcast_fusion
  1.6 3.5 %collective-permute-start = (bf16[3,16,1024]{2,1,0:T(8,128)(2,1)S(1)}, bf16[3,16,1024]{2,1,0:T(8,128)(2,1)S(1)}, u32[]{:S(2)}, u32[]{:S(2)}) collective-permute-start(bf16[3,16,1024]{2,1,0:T(8,128)(2,1)S(1)} %pad_maximum_fusion), channel_id=1, source_target_pairs={{0,4},{4,8},{8,12},{1,5},{5,9},{9,13},{2,6},{6,10},{10,14},{3,7},{... | collective-permute-start | bytes 294920 | tf_op jit(solution)/shard_map/ppermute | solution.py:307
  5.0 3.0 %collective-permute-done.rim_ref = bf16[3,16,1024]{2,1,0:T(8,128)(2,1)S(1)} collective-permute-done((bf16[3,16,1024]{2,1,0:T(8,128)(2,1)S(1)}, bf16[3,16,1024]{2,1,0:T(8,128)(2,1)S(1)}, u32[]{:S(2)}, u32[]{:S(2)}) %collective-permute-start) | collective-permute-done | bytes 98336 | tf_op jit(solution)/shard_map/ppermute | solution.py:307
  8.1 19.5 %summary.1 = (bf16[768,1024]{1,0:T(8,128)(2,1)}, bf16[768,2048]{1,0:T(8,128)(2,1)}, bf16[6,8,128,256]{3,2,1,0:T(8,128)(2,1)}, bf16[8,128,256]{2,1,0:T(8,128)(2,1)S(1)}) custom-call(bf16[3,16,1024]{2,1,0:T(8,128)(2,1)S(1)} %collective-permute-done.rim_ref, bf16[768,1024]{1,0:T(8,128)(2,1)} %kp_ref.1, bf16[768,1024]{1,0:T(8,128)(2,1)} %vp_ref.1, ...), custom_call_target="tpu_custom_call" | custom-call | tf_op jit(solution)/shard_map/summary/pallas_call | solution.py:228
  27.6 0.1 fusion.3
  27.7 1.3 %collective-permute-start.1 = (bf16[8,128,128]{2,1,0:T(8,128)(2,1)S(1)}, bf16[8,128,128]{2,1,0:T(8,128)(2,1)S(1)}, u32[]{:S(2)}, u32[]{:S(2)}) collective-permute-start(bf16[8,128,128]{2,1,0:T(8,128)(2,1)S(1)} %get-tuple-element.39), channel_id=1, source_target_pairs={{0,4},{8,12},{1,5},{9,13},{2,6},{10,14},{3,7},{11,15},{16,20},{24,... | collective-permute-start | bytes 786440 | tf_op jit(solution)/shard_map/ppermute | solution.py:319
  29.0 6.3 %local.2 = (f32[768,1024]{1,0:T(8,128)}, bf16[768,1024]{1,0:T(8,128)(2,1)}) custom-call(bf16[3,16,1024]{2,1,0:T(8,128)(2,1)S(1)} %collective-permute-done.rim_ref, bf16[768,1024]{1,0:T(8,128)(2,1)} %qp_ref.3, bf16[768,1024]{1,0:T(8,128)(2,1)} %qp_ref.3, bf16[768,1024]{1,0:T(8,128)(2,1)} %get-tuple-element.23.keys_ref, ...), custom_call_target="tpu_custom_call" | custom-call | tf_op jit(solution)/shard_map/local/pallas_call | solution.py:261
  35.3 1.2 %collective-permute-done.1 = bf16[8,128,128]{2,1,0:T(8,128)(2,1)S(1)} collective-permute-done((bf16[8,128,128]{2,1,0:T(8,128)(2,1)S(1)}, bf16[8,128,128]{2,1,0:T(8,128)(2,1)S(1)}, u32[]{:S(2)}, u32[]{:S(2)}) %collective-permute-start.1) | collective-permute-done | bytes 262176 | tf_op jit(solution)/shard_map/ppermute | solution.py:319
  36.5 0.2 fusion.1
  36.7 0.7 collective-permute-start.2
  37.4 5.1 %collective-permute-start.3 = (bf16[8,128,128]{2,1,0:T(8,128)(2,1)S(1)}, bf16[8,128,128]{2,1,0:T(8,128)(2,1)S(1)}, u32[]{:S(2)}, u32[]{:S(2)}) collective-permute-start(bf16[8,128,128]{2,1,0:T(8,128)(2,1)S(1)} %fusion.1), channel_id=1, source_target_pairs={{4,12},{5,13},{6,14},{7,15},{20,28},{21,29},{22,30},{23,31}} | collective-permute-start | bytes 786440 | tf_op jit(solution)/shard_map/ppermute | solution.py:323
  42.5 2.0 %collective-permute-start.4 = (bf16[8,128,128]{2,1,0:T(8,128)(2,1)S(1)}, bf16[8,128,128]{2,1,0:T(8,128)(2,1)S(1)}, u32[]{:S(2)}, u32[]{:S(2)}) collective-permute-start(bf16[8,128,128]{2,1,0:T(8,128)(2,1)S(1)} %fusion.1), channel_id=1, source_target_pairs={{4,8},{5,9},{6,10},{7,11},{20,24},{21,25},{22,26},{23,27}} | collective-permute-start | bytes 786440 | tf_op jit(solution)/shard_map/ppermute | solution.py:324
  45.3 6.4 %local.3 = (f32[768,1024]{1,0:T(8,128)}, bf16[768,1024]{1,0:T(8,128)(2,1)}) custom-call(bf16[3,16,1024]{2,1,0:T(8,128)(2,1)S(1)} %collective-permute-done.rim_ref, bf16[768,1024]{1,0:T(8,128)(2,1)} %qp_ref.3, bf16[768,1024]{1,0:T(8,128)(2,1)} %qp_ref.3, bf16[768,1024]{1,0:T(8,128)(2,1)} %get-tuple-element.23.keys_ref, ...), custom_call_target="tpu_custom_call", output_to_operand_aliasing={{0}: (8, {}), {1}: (9, {})} | custom-call | tf_op jit(solution)/shard_map/local/pallas_call | solution.py:261
  51.8 0.2 fusion.state_ref
  52.1 3.4 %outputs.4 = bf16[192,2304]{1,0:T(8,128)(2,1)S(1)} custom-call(s32[3]{0:T(128)S(1)} %add_add_fusion.2.info_ref, f32[8,128,128]{2,1,0:T(8,128)S(1)} %fusion.state_ref, f32[768,1024]{1,0:T(8,128)} %get-tuple-element.34.local_ref, bf16[768,1024]{1,0:T(8,128)(2,1)} %get-tuple-element.35.qeff_ref, bf16[768,1024]{1,0:T(8,128)(2,1)} %gate_ref.7, ...), custom_call_target="tpu_custom_call" | custom-call | tf_op jit(solution)/shard_map/outputs/pallas_call | solution.py:362
  55.7 4.9 %outputs.5 = bf16[192,2304]{1,0:T(8,128)(2,1)S(1)} custom-call(s32[3]{0:T(128)S(1)} %add_add_fusion.1.info_ref, f32[8,128,128]{2,1,0:T(8,128)S(1)} %fusion.state_ref, f32[768,1024]{1,0:T(8,128)} %get-tuple-element.34.local_ref, bf16[768,1024]{1,0:T(8,128)(2,1)} %get-tuple-element.35.qeff_ref, bf16[768,1024]{1,0:T(8,128)(2,1)} %gate_ref.7, ...), custom_call_target="tpu_custom_call" | custom-call | tf_op jit(solution)/shard_map/outputs/pallas_call | solution.py:362
  60.7 0.2 add_convert_fusion.1
  60.9 1.6 %collective-permute-start.7 = (bf16[192,2304]{1,0:T(8,128)(2,1)S(1)}, bf16[192,2304]{1,0:T(8,128)(2,1)S(1)}, u32[]{:S(2)}, u32[]{:S(2)}) collective-permute-start(bf16[192,2304]{1,0:T(8,128)(2,1)S(1)} %add_convert_fusion.1), channel_id=1, source_target_pairs={{0,2},{1,3},{2,0},{3,1},{4,6},{5,7},{6,4},{7,5},{8,10},{9,11},{10,... | collective-permute-start | bytes 2654216 | tf_op jit(solution)/shard_map/ppermute | solution.py:383
  62.5 4.9 %outputs.7 = bf16[192,2304]{1,0:T(8,128)(2,1)S(1)} custom-call(s32[3]{0:T(128)S(1)} %get-tuple-element.38.info_ref, f32[8,128,128]{2,1,0:T(8,128)S(1)} %fusion.state_ref, f32[768,1024]{1,0:T(8,128)} %get-tuple-element.34.local_ref, bf16[768,1024]{1,0:T(8,128)(2,1)} %get-tuple-element.35.qeff_ref, bf16[768,1024]{1,0:T(8,128)(2,1)} %gate_ref.7, ...), custom_call_target="tpu_custom_call" | custom-call | tf_op jit(solution)/shard_map/outputs/pallas_call | solution.py:362
  67.4 0.3 collective-permute-start.6
  67.7 4.9 %outputs.6 = bf16[192,2304]{1,0:T(8,128)(2,1)S(1)} custom-call(s32[3]{0:T(128)S(1)} %get-tuple-element.37.info_ref, f32[8,128,128]{2,1,0:T(8,128)S(1)} %fusion.state_ref, f32[768,1024]{1,0:T(8,128)} %get-tuple-element.34.local_ref, bf16[768,1024]{1,0:T(8,128)(2,1)} %get-tuple-element.35.qeff_ref, bf16[768,1024]{1,0:T(8,128)(2,1)} %gate_ref.7, ...), custom_call_target="tpu_custom_call" | custom-call | tf_op jit(solution)/shard_map/outputs/pallas_call | solution.py:362
  72.6 10.4 %collective-permute-done.7 = bf16[192,2304]{1,0:T(8,128)(2,1)S(1)} collective-permute-done((bf16[192,2304]{1,0:T(8,128)(2,1)S(1)}, bf16[192,2304]{1,0:T(8,128)(2,1)S(1)}, u32[]{:S(2)}, u32[]{:S(2)}) %collective-permute-start.7) | collective-permute-done | bytes 884768 | tf_op jit(solution)/shard_map/ppermute | solution.py:383
  83.0 1.2 %add_convert_fusion = bf16[192,2304]{1,0:T(8,128)(2,1)} fusion(bf16[192,2304]{1,0:T(8,128)(2,1)S(1)} %collective-permute-done.7, bf16[192,2304]{1,0:T(8,128)(2,1)S(1)} %collective-permute-done.6, bf16[192,2304]{1,0:T(8,128)(2,1)S(1)} %outputs.6), kind=kLoop, calls=%fused_computation | loop fusion | flops 2654208 | bytes 3538944 | tf_op jit(solution)/shard_map/convert_element_type | solution.py:402
  (15 shorter events, 0.3 us)
Async XLA Ops:
  1.6 6.5 %collective-permute-start = (bf16[3,16,1024]{2,1,0:T(8,128)(2,1)S(1)}, bf16[3,16,1024]{2,1,0:T(8,128)(2,1)S(1)}, u32[]{:S(2)}, u32[]{:S(2)}) collective-permute-start(bf16[3,16,1024]{2,1,0:T(8,128)(2,1)S(1)} %pad_maximum_fusion), channel_id=1, source_target_pairs={{0,4},{4,8},{8,12},{1,5},{5,9},{9,13},{2,6},{6,10},{10,14},{3,7},{... | collective-permute-start | bytes 294920 | tf_op jit(solution)/shard_map/ppermute | solution.py:307
  27.7 8.8 %collective-permute-start.1 = (bf16[8,128,128]{2,1,0:T(8,128)(2,1)S(1)}, bf16[8,128,128]{2,1,0:T(8,128)(2,1)S(1)}, u32[]{:S(2)}, u32[]{:S(2)}) collective-permute-start(bf16[8,128,128]{2,1,0:T(8,128)(2,1)S(1)} %get-tuple-element.39), channel_id=1, source_target_pairs={{0,4},{8,12},{1,5},{9,13},{2,6},{10,14},{3,7},{11,15},{16,20},{24,... | collective-permute-start | bytes 786440 | tf_op jit(solution)/shard_map/ppermute | solution.py:319
  36.7 15.1 %collective-permute-start.2 = (bf16[8,128,128]{2,1,0:T(8,128)(2,1)S(1)}, bf16[8,128,128]{2,1,0:T(8,128)(2,1)S(1)}, u32[]{:S(2)}, u32[]{:S(2)}) collective-permute-start(bf16[8,128,128]{2,1,0:T(8,128)(2,1)S(1)} %get-tuple-element.31), channel_id=1, source_target_pairs={{8,12},{9,13},{10,14},{11,15},{24,28},{25,29},{26,30},{27,31}} | collective-permute-start | bytes 786440 | tf_op jit(solution)/shard_map/ppermute | solution.py:326
  37.4 14.4 %collective-permute-start.3 = (bf16[8,128,128]{2,1,0:T(8,128)(2,1)S(1)}, bf16[8,128,128]{2,1,0:T(8,128)(2,1)S(1)}, u32[]{:S(2)}, u32[]{:S(2)}) collective-permute-start(bf16[8,128,128]{2,1,0:T(8,128)(2,1)S(1)} %fusion.1), channel_id=1, source_target_pairs={{4,12},{5,13},{6,14},{7,15},{20,28},{21,29},{22,30},{23,31}} | collective-permute-start | bytes 786440 | tf_op jit(solution)/shard_map/ppermute | solution.py:323
  42.5 9.3 %collective-permute-start.4 = (bf16[8,128,128]{2,1,0:T(8,128)(2,1)S(1)}, bf16[8,128,128]{2,1,0:T(8,128)(2,1)S(1)}, u32[]{:S(2)}, u32[]{:S(2)}) collective-permute-start(bf16[8,128,128]{2,1,0:T(8,128)(2,1)S(1)} %fusion.1), channel_id=1, source_target_pairs={{4,8},{5,9},{6,10},{7,11},{20,24},{21,25},{22,26},{23,27}} | collective-permute-start | bytes 786440 | tf_op jit(solution)/shard_map/ppermute | solution.py:324
  45.2 6.8 %slice-start = ((s8[4718592]{0:T(1024)(128)(4,1)}), s8[4194304]{0:T(1024)(128)(4,1)S(1)}, s32[]{:S(2)}) async-start(s8[4718592]{0:T(1024)(128)(4,1)} %bitcast.15), calls=%async_computation | async-start | bytes 8388608
  45.3 6.7 %slice-start.1 = ((s8[4718592]{0:T(1024)(128)(4,1)}), s8[524288]{0:T(1024)(128)(4,1)S(1)}, s32[]{:S(2)}) async-start(s8[4718592]{0:T(1024)(128)(4,1)} %bitcast.15), calls=%async_computation.1 | async-start | bytes 1048576
  55.5 5.2 %collective-permute-start.5 = (bf16[192,2304]{1,0:T(8,128)(2,1)S(1)}, bf16[192,2304]{1,0:T(8,128)(2,1)S(1)}, u32[]{:S(2)}, u32[]{:S(2)}) collective-permute-start(bf16[192,2304]{1,0:T(8,128)(2,1)S(1)} %outputs.4), channel_id=1, source_target_pairs={{0,1},{1,0},{2,3},{3,2},{4,5},{5,4},{6,7},{7,6},{8,9},{9,8},{10,11... | collective-permute-start | bytes 2654216 | tf_op jit(solution)/shard_map/ppermute | solution.py:383
  60.9 22.1 %collective-permute-start.7 = (bf16[192,2304]{1,0:T(8,128)(2,1)S(1)}, bf16[192,2304]{1,0:T(8,128)(2,1)S(1)}, u32[]{:S(2)}, u32[]{:S(2)}) collective-permute-start(bf16[192,2304]{1,0:T(8,128)(2,1)S(1)} %add_convert_fusion.1), channel_id=1, source_target_pairs={{0,2},{1,3},{2,0},{3,1},{4,6},{5,7},{6,4},{7,5},{8,10},{9,11},{10,... | collective-permute-start | bytes 2654216 | tf_op jit(solution)/shard_map/ppermute | solution.py:383
  67.4 15.6 %collective-permute-start.6 = (bf16[192,2304]{1,0:T(8,128)(2,1)S(1)}, bf16[192,2304]{1,0:T(8,128)(2,1)S(1)}, u32[]{:S(2)}, u32[]{:S(2)}) collective-permute-start(bf16[192,2304]{1,0:T(8,128)(2,1)S(1)} %outputs.7), channel_id=1, source_target_pairs={{0,1},{1,0},{2,3},{3,2},{4,5},{5,4},{6,7},{7,6},{8,9},{9,8},{10,11... | collective-permute-start | bytes 2654216 | tf_op jit(solution)/shard_map/ppermute | solution.py:383

commit v4 on v3

--- a/solution.py
+++ b/solution.py
@@ -30,16 +30,15 @@
 
 
 def sigmoid(x):
-    return 1.0 / (1.0 + jnp.exp(-x))
+    return 0.5 + 0.5 * jnp.tanh(0.5 * x)
 
 
 def conv_silu(raw, rim, taps):
-    rows = raw.shape[0]
+    rows, n = raw.shape[0], rim.shape[0]
     padded = jnp.concatenate([rim, raw], axis=0)
-    n = rim.shape[0]
-    total = taps[3:4] * raw
-    for j in range(3):
-        total = total + taps[j : j + 1] * padded[n - 3 + j : n - 3 + j + rows]
+    before = pltpu.roll(padded, 1, 0)
+    old = pltpu.roll(taps[1:2] * padded + taps[0:1] * before, 2, 0)
+    total = (taps[3:4] * padded + taps[2:3] * before + old)[n:]
     return total * sigmoid(total)
 
 
@@ -92,7 +91,8 @@
     cum_col = [exact(tril, x, NT) for x in dec]
     wr_col = [exact(eye, x, NT) for x in wr]
     last = [x[:, c - 1 : c] for x in cum_row]
-    wg_row = [wr[s] * jnp.exp(cum_row[s]) for s in range(subs)]
+    log_col = [cum_col[s] + jnp.log(wr_col[s]) for s in range(subs)]
+    drop_col = [-wr_col[s] * jnp.exp(cum_col[s]) for s in range(subs)]
     kout_row = [jnp.exp(last[s] - cum_row[s]) for s in range(subs)]
     last_decay = [jnp.exp(x) for x in last]
 
@@ -120,31 +120,39 @@
     gram = [mm(x, x, NT) for x in k]
     low = []
     for i in n:
-        gap = col(cum_col, i) - row(cum_row, i)
-        decay = jnp.exp(jnp.minimum(gap, 0.0)) * col(wr_col, i)
+        decay = jnp.exp(col(log_col, i) - row(cum_row, i))
         low.append(jnp.where(ci < ri, gram[i] * decay, 0.0).astype(BF16))
-    inv = [eye - (x * mask_ref[0]).astype(F32) for x in low]
+    inv = [eye.astype(BF16) - x * mask_ref[0] for x in low]
     level = 1
     while (1 << level) < c:
         mask = mask_ref[level]
-        invb = [x.astype(BF16) for x in inv]
-        inner = [mm(low[i] * mask, invb[i]).astype(BF16) for i in n]
-        inv = [inv[i] - mm(invb[i], inner[i]) for i in n]
+        inner = [mm(low[i] * mask, inv[i]).astype(BF16) for i in n]
+        inv = [inv[i] - mm(inv[i], inner[i]).astype(BF16) for i in n]
         level += 1
     v_all = [channels(rim_ref, v_ref, vp_ref, taps_ref, 2, lanes(h), first).astype(BF16) for h in range(heads)]
     v = [v_all[h][s * c : (s + 1) * c] for s, h in units]
-    key_mix = [mm((inv[i] * row(wg_row, i)).astype(BF16), k[i]).astype(BF16) for i in n]
-    value_mix = [mm((inv[i] * row(wr, i)).astype(BF16), v[i]) for i in n]
-    k_out = [(k[i].astype(F32).T * row(kout_row, i)).astype(BF16) for i in n]
+    kf = [x.astype(F32) for x in k]
+    sides = [
+        jnp.concatenate(
+            [
+                (kf[i] * col(drop_col, i)).astype(BF16),
+                (v[i].astype(F32) * col(wr_col, i)).astype(BF16),
+            ],
+            axis=1,
+        )
+        for i in n
+    ]
+    mixed = [mm(inv[i], sides[i]) for i in n]
+    k_out = [(kf[i].T * row(kout_row, i)).astype(BF16) for i in n]
     for s in range(subs):
         at = s * heads
         start = [state_ref[h].astype(BF16) for h in range(heads)]
         for h in range(heads):
             start_ref[s, h] = start[h]
-        read = [mm(key_mix[at + h], start[h]) for h in range(heads)]
+        read = [mm(mixed[at + h][:, :width].astype(BF16), start[h]) for h in range(heads)]
         fresh = [
             jnp.concatenate(
-                [-read[h][:, :width], value_mix[at + h] - read[h][:, width:]], axis=1
+                [read[h][:, :width], mixed[at + h][:, width:] + read[h][:, width:]], axis=1
             ).astype(BF16)
             for h in range(heads)
         ]
@@ -183,7 +191,7 @@
         for i in n:
             h = hs[i]
             gap = cum_col[:, h : h + 1] - cum_row[h : h + 1, :]
-            scores = jnp.where(ci <= ri, gram[i] * jnp.exp(jnp.minimum(gap, 0.0)), 0.0).astype(BF16)
+            scores = jnp.where(ci <= ri, gram[i] * jnp.exp(gap), 0.0).astype(BF16)
             q_in = (q[i].astype(F32) * gamma_col[:, h : h + 1]).astype(BF16)
             out = mm(
                 jnp.concatenate([q_in, scores], axis=1),
@@ -252,7 +260,7 @@
         compiler_params=params,
         name="summary",
     )(rim, *placed(key_raw, value_raw, key_raw, value_raw, log_decay, write_strength, conv_weight, masks))
-    first = steps // 2
+    first = steps // 3
 
     def local_part(begin, count, done, rim, keys, fresh, start):
         def at(spec):
@@ -321,11 +329,13 @@
         got_own, done = lax.optimization_barrier((got_own, done))
         pair = apply(move, own, got_own).astype(BF16)
         far = lax.ppermute(pair, axis, [(1, 3)])
-        near = lax.ppermute(pair, axis, [(1, 2)])
-        move, done, pair = lax.optimization_barrier((move, done, pair))
-        got_move = lax.ppermute(move, axis, [(2, 3)])
+        place = lax.axis_index(axis)
+        next_in = lax.ppermute(jnp.where(place == 1, pair, move), axis, [(1, 2), (2, 3)])
+        done, pair = lax.optimization_barrier((done, pair))
         done = late(done)
-        return apply(got_move, got_own, far) + near.astype(F32), *done
+        got_move = jnp.where(place == 3, next_in, jnp.zeros_like(next_in))
+        near = jnp.where(place == 2, next_in.astype(F32), 0.0)
+        return apply(got_move, got_own, far) + near, *done
     state = passed_along(own, axis, 1)
     for _ in range(count - 2):
         state = passed_along(apply(move, own, state).astype(BF16), axis, 1)

time: 85.5 us -> 81.7 us (0.956)
  Pallas kernels: 50.5 us -> 47.4 us
  starting transfers between devices: 14.5 us -> 12.7 us
  waiting for transfers between devices: 14.6 us -> 16.3 us
    pallas_call x1, Pallas kernels: 19.5 us -> 17.1 us  [front(): pl.pallas_call(summary_kernel, grid=(steps // subs,), in_specs=[rims, big...]
    ppermute x1, waiting for transfers between devices: 1.15 us -> 2.83 us  [carried_in(): got_own = lax.ppermute(own, axis, [(0, 1), (2, 3)])]
    ppermute x2 -> x1, starting transfers between devices: 2.73 us -> 1.49 us  [carried_in(): lax.ppermute(jnp.where(place == 1, pair, move), axis, [(1, 2), (2, 3)])]
  transfers between devices with their start and end apart: 8 -> 7, of which waited for: 3 -> 3; matrix products, arithmetic and copies ran while one was open for 0% -> 0% of each run, Pallas kernels for 33% -> 33%
where the time goes in v4:
time: 81.7 us; the launch traced here: 80.9 us
  Pallas kernels  47.4 us (58%)
  waiting for transfers between devices  16.3 us (20%)
  starting transfers between devices  12.7 us (16%)
  other arithmetic  1.69 us (2%)
  local copies, waits for them, and re-layouts  1.6 us (2%)
  between operations  0.83 us (1%)
    pallas_call x4, Pallas kernels, partial(): pl.pallas_call(out_kernel, grid_spec=pltpu.PrefetchScalarGridSpec(num_sca...  18.1 us
    pallas_call x1, Pallas kernels, front(): pl.pallas_call(summary_kernel, grid=(steps // subs,), in_specs=[rims, big...  17.1 us
    pallas_call x2, Pallas kernels, local_part(): pl.pallas_call(functools.partial(local_kernel, begin), grid=(count,), in_...  12.1 us
    ppermute x3, waiting for transfers between devices, exchange(): return lax.ppermute(block, 'head', [(i, i ^ bit) for i in range(owners)])  10.5 us
    ppermute x1, starting transfers between devices, carried_in(): far = lax.ppermute(pair, axis, [(1, 3)])  4.5 us
    ppermute x1, starting transfers between devices, passed_along(): return lax.ppermute(block, axis, route)  3.48 us
    ppermute x1, waiting for transfers between devices, passed_along(): return lax.ppermute(block, axis, route)  3.02 us
    ppermute x1, waiting for transfers between devices, carried_in(): got_own = lax.ppermute(own, axis, [(0, 1), (2, 3)])  2.83 us
  transfers between devices with their start and end apart: 7, of which 3 were waited for; matrix products, arithmetic and copies ran while one was open for 0% of the time, Pallas kernels for 33%

profile of v4, /device:TPU:8, one launch (start us, length us, event | category | flops | bytes accessed | tf_op | source)
XLA Modules:
  0.0 80.9 jit_solution(9066543517911962294)
XLA Ops:
  0.0 0.8 slice_bitcast_fusion.2
  0.8 0.8 slice_bitcast_fusion
  1.6 3.5 %collective-permute-start = (bf16[3,16,1024]{2,1,0:T(8,128)(2,1)S(1)}, bf16[3,16,1024]{2,1,0:T(8,128)(2,1)S(1)}, u32[]{:S(2)}, u32[]{:S(2)}) collective-permute-start(bf16[3,16,1024]{2,1,0:T(8,128)(2,1)S(1)} %pad_maximum_fusion), channel_id=1, source_target_pairs={{0,4},{4,8},{8,12},{1,5},{5,9},{9,13},{2,6},{6,10},{10,14},{3,7},{... | collective-permute-start | bytes 294920 | tf_op jit(solution)/shard_map/ppermute | solution.py:315
  5.0 3.0 %collective-permute-done.rim_ref = bf16[3,16,1024]{2,1,0:T(8,128)(2,1)S(1)} collective-permute-done((bf16[3,16,1024]{2,1,0:T(8,128)(2,1)S(1)}, bf16[3,16,1024]{2,1,0:T(8,128)(2,1)S(1)}, u32[]{:S(2)}, u32[]{:S(2)}) %collective-permute-start) | collective-permute-done | bytes 98336 | tf_op jit(solution)/shard_map/ppermute | solution.py:315
  8.1 17.1 %summary.1 = (bf16[768,1024]{1,0:T(8,128)(2,1)}, bf16[768,2048]{1,0:T(8,128)(2,1)}, bf16[6,8,128,256]{3,2,1,0:T(8,128)(2,1)}, bf16[8,128,256]{2,1,0:T(8,128)(2,1)S(1)}) custom-call(bf16[3,16,1024]{2,1,0:T(8,128)(2,1)S(1)} %collective-permute-done.rim_ref, bf16[768,1024]{1,0:T(8,128)(2,1)} %kp_ref.1, bf16[768,1024]{1,0:T(8,128)(2,1)} %vp_ref.1, ...), custom_call_target="tpu_custom_call" | custom-call | tf_op jit(solution)/shard_map/summary/pallas_call | solution.py:236
  25.2 1.3 %collective-permute-start.1 = (bf16[8,128,128]{2,1,0:T(8,128)(2,1)S(1)}, bf16[8,128,128]{2,1,0:T(8,128)(2,1)S(1)}, u32[]{:S(2)}, u32[]{:S(2)}) collective-permute-start(bf16[8,128,128]{2,1,0:T(8,128)(2,1)S(1)} %slice.19), channel_id=1, source_target_pairs={{0,4},{8,12},{1,5},{9,13},{2,6},{10,14},{3,7},{11,15},{16,20},{24,... | collective-permute-start | bytes 786440 | tf_op jit(solution)/shard_map/ppermute | solution.py:327
  26.5 4.7 %local.2 = (f32[768,1024]{1,0:T(8,128)}, bf16[768,1024]{1,0:T(8,128)(2,1)}) custom-call(bf16[3,16,1024]{2,1,0:T(8,128)(2,1)S(1)} %collective-permute-done.rim_ref, bf16[768,1024]{1,0:T(8,128)(2,1)} %qp_ref.3, bf16[768,1024]{1,0:T(8,128)(2,1)} %qp_ref.3, bf16[768,1024]{1,0:T(8,128)(2,1)} %get-tuple-element.22.keys_ref, ...), custom_call_target="tpu_custom_call" | custom-call | tf_op jit(solution)/shard_map/local/pallas_call | solution.py:269
  31.2 2.8 %collective-permute-done.1 = bf16[8,128,128]{2,1,0:T(8,128)(2,1)S(1)} collective-permute-done((bf16[8,128,128]{2,1,0:T(8,128)(2,1)S(1)}, bf16[8,128,128]{2,1,0:T(8,128)(2,1)S(1)}, u32[]{:S(2)}, u32[]{:S(2)}) %collective-permute-start.1) | collective-permute-done | bytes 262176 | tf_op jit(solution)/shard_map/ppermute | solution.py:327
  34.0 0.2 broadcast_select_fusion
  34.3 4.5 %collective-permute-start.3 = (bf16[8,128,128]{2,1,0:T(8,128)(2,1)S(1)}, bf16[8,128,128]{2,1,0:T(8,128)(2,1)S(1)}, u32[]{:S(2)}, u32[]{:S(2)}) collective-permute-start(bf16[8,128,128]{2,1,0:T(8,128)(2,1)S(1)} %get-tuple-element.38), channel_id=1, source_target_pairs={{4,12},{5,13},{6,14},{7,15},{20,28},{21,29},{22,30},{23,31}} | collective-permute-start | bytes 786440 | tf_op jit(solution)/shard_map/ppermute | solution.py:331
  38.8 1.5 %collective-permute-start.2 = (bf16[8,128,128]{2,1,0:T(8,128)(2,1)S(1)}, bf16[8,128,128]{2,1,0:T(8,128)(2,1)S(1)}, u32[]{:S(2)}, u32[]{:S(2)}) collective-permute-start(bf16[8,128,128]{2,1,0:T(8,128)(2,1)S(1)} %get-tuple-element.37), channel_id=1, source_target_pairs={{4,8},{8,12},{5,9},{9,13},{6,10},{10,14},{7,11},{11,15},{20,24},{2... | collective-permute-start | bytes 786440 | tf_op jit(solution)/shard_map/ppermute | solution.py:333
  41.0 0.1 add_add_fusion.2.info_ref
  41.0 7.5 %local.3 = (f32[768,1024]{1,0:T(8,128)}, bf16[768,1024]{1,0:T(8,128)(2,1)}) custom-call(bf16[3,16,1024]{2,1,0:T(8,128)(2,1)S(1)} %collective-permute-done.rim_ref, bf16[768,1024]{1,0:T(8,128)(2,1)} %qp_ref.3, bf16[768,1024]{1,0:T(8,128)(2,1)} %qp_ref.3, bf16[768,1024]{1,0:T(8,128)(2,1)} %get-tuple-element.22.keys_ref, ...), custom_call_target="tpu_custom_call", output_to_operand_aliasing={{0}: (8, {}), {1}: (9, {})} | custom-call | tf_op jit(solution)/shard_map/local/pallas_call | solution.py:269
  48.5 0.2 fusion.state_ref
  48.8 3.4 %outputs.4 = bf16[192,2304]{1,0:T(8,128)(2,1)S(1)} custom-call(s32[3]{0:T(128)S(1)} %add_add_fusion.2.info_ref, f32[8,128,128]{2,1,0:T(8,128)S(1)} %fusion.state_ref, f32[768,1024]{1,0:T(8,128)} %get-tuple-element.32.local_ref, bf16[768,1024]{1,0:T(8,128)(2,1)} %get-tuple-element.33.qeff_ref, bf16[768,1024]{1,0:T(8,128)(2,1)} %gate_ref.7, ...), custom_call_target="tpu_custom_call" | custom-call | tf_op jit(solution)/shard_map/outputs/pallas_call | solution.py:372
  52.3 0.1 add_add_fusion.1.info_ref
  52.5 4.9 %outputs.5 = bf16[192,2304]{1,0:T(8,128)(2,1)S(1)} custom-call(s32[3]{0:T(128)S(1)} %add_add_fusion.1.info_ref, f32[8,128,128]{2,1,0:T(8,128)S(1)} %fusion.state_ref, f32[768,1024]{1,0:T(8,128)} %get-tuple-element.32.local_ref, bf16[768,1024]{1,0:T(8,128)(2,1)} %get-tuple-element.33.qeff_ref, bf16[768,1024]{1,0:T(8,128)(2,1)} %gate_ref.7, ...), custom_call_target="tpu_custom_call" | custom-call | tf_op jit(solution)/shard_map/outputs/pallas_call | solution.py:372
  57.4 0.2 add_convert_fusion.1
  57.6 1.6 %collective-permute-start.6 = (bf16[192,2304]{1,0:T(8,128)(2,1)S(1)}, bf16[192,2304]{1,0:T(8,128)(2,1)S(1)}, u32[]{:S(2)}, u32[]{:S(2)}) collective-permute-start(bf16[192,2304]{1,0:T(8,128)(2,1)S(1)} %add_convert_fusion.1), channel_id=1, source_target_pairs={{0,2},{1,3},{2,0},{3,1},{4,6},{5,7},{6,4},{7,5},{8,10},{9,11},{10,... | collective-permute-start | bytes 2654216 | tf_op jit(solution)/shard_map/ppermute | solution.py:393
  59.2 4.9 %outputs.7 = bf16[192,2304]{1,0:T(8,128)(2,1)S(1)} custom-call(s32[3]{0:T(128)S(1)} %get-tuple-element.36.info_ref, f32[8,128,128]{2,1,0:T(8,128)S(1)} %fusion.state_ref, f32[768,1024]{1,0:T(8,128)} %get-tuple-element.32.local_ref, bf16[768,1024]{1,0:T(8,128)(2,1)} %get-tuple-element.33.qeff_ref, bf16[768,1024]{1,0:T(8,128)(2,1)} %gate_ref.7, ...), custom_call_target="tpu_custom_call" | custom-call | tf_op jit(solution)/shard_map/outputs/pallas_call | solution.py:372
  64.1 0.3 collective-permute-start.5
  64.3 4.9 %outputs.6 = bf16[192,2304]{1,0:T(8,128)(2,1)S(1)} custom-call(s32[3]{0:T(128)S(1)} %get-tuple-element.35.info_ref, f32[8,128,128]{2,1,0:T(8,128)S(1)} %fusion.state_ref, f32[768,1024]{1,0:T(8,128)} %get-tuple-element.32.local_ref, bf16[768,1024]{1,0:T(8,128)(2,1)} %get-tuple-element.33.qeff_ref, bf16[768,1024]{1,0:T(8,128)(2,1)} %gate_ref.7, ...), custom_call_target="tpu_custom_call" | custom-call | tf_op jit(solution)/shard_map/outputs/pallas_call | solution.py:372
  69.3 10.5 %collective-permute-done.6 = bf16[192,2304]{1,0:T(8,128)(2,1)S(1)} collective-permute-done((bf16[192,2304]{1,0:T(8,128)(2,1)S(1)}, bf16[192,2304]{1,0:T(8,128)(2,1)S(1)}, u32[]{:S(2)}, u32[]{:S(2)}) %collective-permute-start.6) | collective-permute-done | bytes 884768 | tf_op jit(solution)/shard_map/ppermute | solution.py:393
  79.7 1.2 %add_convert_fusion = bf16[192,2304]{1,0:T(8,128)(2,1)} fusion(bf16[192,2304]{1,0:T(8,128)(2,1)S(1)} %collective-permute-done.6, bf16[192,2304]{1,0:T(8,128)(2,1)S(1)} %collective-permute-done.5, bf16[192,2304]{1,0:T(8,128)(2,1)S(1)} %outputs.6), kind=kLoop, calls=%fused_computation | loop fusion | flops 2654208 | bytes 3538944 | tf_op jit(solution)/shard_map/convert_element_type | solution.py:412
  (13 shorter events, 0.2 us)
Async XLA Ops:
  1.6 6.5 %collective-permute-start = (bf16[3,16,1024]{2,1,0:T(8,128)(2,1)S(1)}, bf16[3,16,1024]{2,1,0:T(8,128)(2,1)S(1)}, u32[]{:S(2)}, u32[]{:S(2)}) collective-permute-start(bf16[3,16,1024]{2,1,0:T(8,128)(2,1)S(1)} %pad_maximum_fusion), channel_id=1, source_target_pairs={{0,4},{4,8},{8,12},{1,5},{5,9},{9,13},{2,6},{6,10},{10,14},{3,7},{... | collective-permute-start | bytes 294920 | tf_op jit(solution)/shard_map/ppermute | solution.py:315
  25.2 8.8 %collective-permute-start.1 = (bf16[8,128,128]{2,1,0:T(8,128)(2,1)S(1)}, bf16[8,128,128]{2,1,0:T(8,128)(2,1)S(1)}, u32[]{:S(2)}, u32[]{:S(2)}) collective-permute-start(bf16[8,128,128]{2,1,0:T(8,128)(2,1)S(1)} %slice.19), channel_id=1, source_target_pairs={{0,4},{8,12},{1,5},{9,13},{2,6},{10,14},{3,7},{11,15},{16,20},{24,... | collective-permute-start | bytes 786440 | tf_op jit(solution)/shard_map/ppermute | solution.py:327
  34.3 14.2 %collective-permute-start.3 = (bf16[8,128,128]{2,1,0:T(8,128)(2,1)S(1)}, bf16[8,128,128]{2,1,0:T(8,128)(2,1)S(1)}, u32[]{:S(2)}, u32[]{:S(2)}) collective-permute-start(bf16[8,128,128]{2,1,0:T(8,128)(2,1)S(1)} %get-tuple-element.38), channel_id=1, source_target_pairs={{4,12},{5,13},{6,14},{7,15},{20,28},{21,29},{22,30},{23,31}} | collective-permute-start | bytes 786440 | tf_op jit(solution)/shard_map/ppermute | solution.py:331
  38.8 9.7 %collective-permute-start.2 = (bf16[8,128,128]{2,1,0:T(8,128)(2,1)S(1)}, bf16[8,128,128]{2,1,0:T(8,128)(2,1)S(1)}, u32[]{:S(2)}, u32[]{:S(2)}) collective-permute-start(bf16[8,128,128]{2,1,0:T(8,128)(2,1)S(1)} %get-tuple-element.37), channel_id=1, source_target_pairs={{4,8},{8,12},{5,9},{9,13},{6,10},{10,14},{7,11},{11,15},{20,24},{2... | collective-permute-start | bytes 786440 | tf_op jit(solution)/shard_map/ppermute | solution.py:333
  40.9 7.8 %slice-start = ((s8[4718592]{0:T(1024)(128)(4,1)}), s8[4194304]{0:T(1024)(128)(4,1)S(1)}, s32[]{:S(2)}) async-start(s8[4718592]{0:T(1024)(128)(4,1)} %bitcast.14), calls=%async_computation | async-start | bytes 8388608
  41.0 7.7 %slice-start.1 = ((s8[4718592]{0:T(1024)(128)(4,1)}), s8[524288]{0:T(1024)(128)(4,1)S(1)}, s32[]{:S(2)}) async-start(s8[4718592]{0:T(1024)(128)(4,1)} %bitcast.14), calls=%async_computation.1 | async-start | bytes 1048576
  52.2 5.2 %collective-permute-start.4 = (bf16[192,2304]{1,0:T(8,128)(2,1)S(1)}, bf16[192,2304]{1,0:T(8,128)(2,1)S(1)}, u32[]{:S(2)}, u32[]{:S(2)}) collective-permute-start(bf16[192,2304]{1,0:T(8,128)(2,1)S(1)} %outputs.4), channel_id=1, source_target_pairs={{0,1},{1,0},{2,3},{3,2},{4,5},{5,4},{6,7},{7,6},{8,9},{9,8},{10,11... | collective-permute-start | bytes 2654216 | tf_op jit(solution)/shard_map/ppermute | solution.py:393
  57.6 22.1 %collective-permute-start.6 = (bf16[192,2304]{1,0:T(8,128)(2,1)S(1)}, bf16[192,2304]{1,0:T(8,128)(2,1)S(1)}, u32[]{:S(2)}, u32[]{:S(2)}) collective-permute-start(bf16[192,2304]{1,0:T(8,128)(2,1)S(1)} %add_convert_fusion.1), channel_id=1, source_target_pairs={{0,2},{1,3},{2,0},{3,1},{4,6},{5,7},{6,4},{7,5},{8,10},{9,11},{10,... | collective-permute-start | bytes 2654216 | tf_op jit(solution)/shard_map/ppermute | solution.py:393
  64.1 15.6 %collective-permute-start.5 = (bf16[192,2304]{1,0:T(8,128)(2,1)S(1)}, bf16[192,2304]{1,0:T(8,128)(2,1)S(1)}, u32[]{:S(2)}, u32[]{:S(2)}) collective-permute-start(bf16[192,2304]{1,0:T(8,128)(2,1)S(1)} %outputs.7), channel_id=1, source_target_pairs={{0,1},{1,0},{2,3},{3,2},{4,5},{5,4},{6,7},{7,6},{8,9},{9,8},{10,11... | collective-permute-start | bytes 2654216 | tf_op jit(solution)/shard_map/ppermute | solution.py:393

commit v5 on v4

--- a/solution.py
+++ b/solution.py
@@ -12,7 +12,6 @@
 RIM = 16
 GROUP = 8
 SUBS = 2
-PIECES = 1
 F32 = jnp.float32
 BF16 = jnp.bfloat16
 NN = (((1,), (0,)), ((), ()))
@@ -200,7 +199,7 @@
                 ),
             )
             qeff_ref[:, sls[i]] = out[:, :width].astype(BF16)
-            local_ref[:, sls[i]] = out[:, width:]
+            local_ref[:, sls[i]] = out[:, width:].astype(BF16)
 
 
 def level_masks(c):
@@ -273,7 +272,7 @@
             + [pl.BlockSpec(memory_space=pl.ANY)] * len(done),
             out_specs=[at(block), at(block)],
             out_shape=[
-                pltpu.HBM((rows, channel_count), F32),
+                pltpu.HBM((rows, channel_count), BF16),
                 pltpu.HBM((rows, channel_count), BF16),
             ],
             input_output_aliases={8 + i: i for i in range(len(done))},
@@ -291,28 +290,52 @@
 
 
 def out_kernel(
-    info_ref, state_ref, local_ref, qeff_ref, gate_ref, gain_ref, weight_ref, out_ref
+    info_ref, state_ref, local_ref, qeff_ref, gate_ref, gain_ref, weight_ref, *out_refs
 ):
+    step = pl.program_id(0)
     heads, width = state_ref.shape[0], state_ref.shape[1]
     rows = local_ref.shape[0]
-    base = info_ref[0] + info_ref[1] * rows
-    valid = base + lax.broadcasted_iota(jnp.int32, (rows, width), 0) < info_ref[2]
+    base = info_ref[0] + info_ref[2 + step] * rows
+    valid = base + lax.broadcasted_iota(jnp.int32, (rows, width), 0) < info_ref[1]
     gated = []
     for h in range(heads):
         sl = slice(h * width, (h + 1) * width)
-        o = local_ref[:, sl] + mm(qeff_ref[:, sl], state_ref[h].astype(BF16))
+        o = local_ref[:, sl].astype(F32) + mm(qeff_ref[:, sl], state_ref[h])
         norm = lax.rsqrt(jnp.mean(o * o, axis=-1, keepdims=True) + 1e-06)
         g = gate_ref[:, sl].astype(F32)
         o = o * norm * gain_ref[...] * (g * sigmoid(g))
         gated.append(jnp.where(valid, o, 0.0).astype(BF16))
-    gated = jnp.concatenate(gated, axis=1)
-    out_ref[...] = mm(gated, weight_ref[...]).astype(BF16)
+    result = mm(jnp.concatenate(gated, axis=1), weight_ref[...]).astype(BF16)
+    for i, out_ref in enumerate(out_refs):
+
+        @pl.when(step == i)
+        def _(out_ref=out_ref):
+            out_ref[...] = result
 
 
 def passed_along(block, axis, distance):
     devices = range(lax.axis_size(axis))
     route = [(i - distance, i) for i in devices if i - distance in devices]
     return lax.ppermute(block, axis, route)
+
+
+def ends_kernel(q_ref, k_ref, v_ref, out_ref):
+    out_ref[0] = q_ref[...]
+    out_ref[1] = k_ref[...]
+    out_ref[2] = v_ref[...]
+
+
+def ends(*arrays):
+    rows, channel_count = arrays[0].shape
+    last = rows // RIM - 1
+    return pl.pallas_call(
+        ends_kernel,
+        grid=(1,),
+        in_specs=[pl.BlockSpec((RIM, channel_count), lambda i: (last, 0))] * 3,
+        out_specs=pl.BlockSpec((3, RIM, channel_count), lambda i: (0, 0, 0)),
+        out_shape=jax.ShapeDtypeStruct((3, RIM, channel_count), BF16),
+        name="ends",
+    )(*placed(*arrays))
 
 
 def carried_in(summary, axis, early, late):
@@ -335,11 +358,11 @@
         done = late(done)
         got_move = jnp.where(place == 3, next_in, jnp.zeros_like(next_in))
         near = jnp.where(place == 2, next_in.astype(F32), 0.0)
-        return apply(got_move, got_own, far) + near, *done
+        return (apply(got_move, got_own, far) + near).astype(BF16), *done
     state = passed_along(own, axis, 1)
     for _ in range(count - 2):
         state = passed_along(apply(move, own, state).astype(BF16), axis, 1)
-    return state.astype(F32), *late(early())
+    return state, *late(early())
 
 
 def on_device(
@@ -349,9 +372,7 @@
     rows, channel_count = query_raw.shape
     heads = log_decay.shape[0]
     width = channel_count // heads
-    rim = passed_along(
-        jnp.stack([query_raw[-RIM:], key_raw[-RIM:], value_raw[-RIM:]]), "seq", 1
-    )
+    rim = passed_along(ends(query_raw, key_raw, value_raw), "seq", 1)
     early, late, summary = front(
         rim, query_raw, key_raw, value_raw, log_decay, write_strength, conv_weight
     )
@@ -362,18 +383,18 @@
     start = lax.axis_index("seq") * rows
     gain = norm_gain.reshape(1, width)
 
-    def partial(owner, piece=0, pieces=1, after=None, resident=False):
-        tile = rows // owners // pieces
-        info = jnp.stack([start, owner * pieces + piece, history_end[0]]).astype(jnp.int32)
+    def partial(*blocks, after=None, resident=False):
+        tile = rows // owners
+        info = jnp.stack([start, history_end[0], *blocks]).astype(jnp.int32)
         if after is not None:
             info, after = lax.optimization_barrier((info, after))
-        tiles = pl.BlockSpec((tile, channel_count), lambda i, s: (s[1], 0))
+        tiles = pl.BlockSpec((tile, channel_count), lambda i, s: (s[2 + i], 0))
         weight = out_weight if resident else placed(out_weight)[0]
         return pl.pallas_call(
             out_kernel,
             grid_spec=pltpu.PrefetchScalarGridSpec(
                 num_scalar_prefetch=1,
-                grid=(1,),
+                grid=(len(blocks),),
                 in_specs=[
                     pl.BlockSpec((heads, width, width), lambda i, s: (0, 0, 0)),
                     tiles, tiles, tiles,
@@ -382,9 +403,9 @@
                     if resident
                     else pl.BlockSpec((channel_count, dim), lambda i, s: (0, 0)),
                 ],
-                out_specs=pl.BlockSpec((tile, dim), lambda i, s: (0, 0)),
+                out_specs=[pl.BlockSpec((tile, dim), lambda i, s: (0, 0))] * len(blocks),
             ),
-            out_shape=jax.ShapeDtypeStruct((tile, dim), BF16),
+            out_shape=[jax.ShapeDtypeStruct((tile, dim), BF16)] * len(blocks),
             compiler_params=pltpu.CompilerParams(vmem_limit_bytes=24 << 20),
             name="outputs",
         )(info, state, *placed(local, qeff, out_gate, gain), weight)
@@ -396,24 +417,14 @@
         return (a.astype(F32) + b.astype(F32)).astype(BF16)
 
     if owners != 4:
-        blocks = jnp.concatenate([partial(o) for o in range(owners)], axis=0)
+        blocks = jnp.concatenate(partial(*range(owners)), axis=0)
         return lax.psum_scatter(blocks, "head", scatter_dimension=0, tiled=True)
-    far, far_got = None, []
-    for piece in range(PIECES):
-        sent = partial(mine ^ 3, piece, PIECES, far, resident=piece == 0)
-        far_in = exchange(sent, 1)
-        far = added(partial(mine ^ 2, piece, PIECES, sent), far_in)
-        far_got.append(exchange(far, 2))
-    near_in = exchange(partial(mine ^ 1, after=far), 1)
-    near = partial(mine, after=far).astype(F32) + near_in.astype(F32)
-    tile = near.shape[0] // PIECES
-    return jnp.concatenate(
-        [
-            (near[i * tile : (i + 1) * tile] + got.astype(F32)).astype(BF16)
-            for i, got in enumerate(far_got)
-        ],
-        axis=0,
-    )
+    sent, kept = partial(mine ^ 3, mine ^ 2, resident=True)
+    far = added(kept, exchange(sent, 1))
+    far_got = exchange(far, 2)
+    sent, kept = partial(mine ^ 1, mine, after=far)
+    near = kept.astype(F32) + exchange(sent, 1).astype(F32)
+    return (near + far_got.astype(F32)).astype(BF16)
 
 
 def solution(mesh):

time: 81.7 us -> 80.3 us (0.983)
  waiting for transfers between devices: 16.3 us -> 21.8 us
  Pallas kernels: 47.4 us -> 42.3 us
  local copies, waits for them, and re-layouts: 1.6 us -> 0.06 us
    pallas_call x4 -> x2, Pallas kernels: 18.1 us -> 11.9 us  [partial(): pl.pallas_call(out_kernel, grid_spec=pltpu.PrefetchScalarGridSpec(num_sca...]
    ppermute x3, waiting for transfers between devices: 10.5 us -> 15.7 us  [exchange(): return lax.ppermute(block, 'head', [(i, i ^ bit) for i in range(owners)])]
    another operation x2 -> x0, local copies, waits for them, and re-layouts: 1.54 us -> none  [on_device(): jnp.stack([query_raw[-RIM:], key_raw[-RIM:], value_raw[-RIM:]])]
    pallas_call x0 -> x1, Pallas kernels: none -> 1.44 us  [ends(): pl.pallas_call(ends_kernel, grid=(1,), in_specs=[pl.BlockSpec((RIM, chann...]
  transfers between devices with their start and end apart: 7 -> 7, of which waited for: 3 -> 4; matrix products, arithmetic and copies ran while one was open for 0% -> 0% of each run, Pallas kernels for 33% -> 24%
where the time goes in v5:
time: 80.3 us; the launch traced here: 79.3 us
  Pallas kernels  42.3 us (53%)
  waiting for transfers between devices  21.8 us (27%)
  starting transfers between devices  12.3 us (15%)
  other arithmetic  1.63 us (2%)
  between operations  0.81 us (1%)
    pallas_call x1, Pallas kernels, front(): pl.pallas_call(summary_kernel, grid=(steps // subs,), in_specs=[rims, big...  17.1 us
    ppermute x3, waiting for transfers between devices, exchange(): return lax.ppermute(block, 'head', [(i, i ^ bit) for i in range(owners)])  15.7 us
    pallas_call x2, Pallas kernels, partial(): pl.pallas_call(out_kernel, grid_spec=pltpu.PrefetchScalarGridSpec(num_sca...  11.9 us
    pallas_call x2, Pallas kernels, local_part(): pl.pallas_call(functools.partial(local_kernel, begin), grid=(count,), in_...  11.9 us
    ppermute x1, starting transfers between devices, carried_in(): far = lax.ppermute(pair, axis, [(1, 3)])  4.5 us
    ppermute x1, starting transfers between devices, passed_along(): return lax.ppermute(block, axis, route)  3.47 us
    ppermute x1, waiting for transfers between devices, passed_along(): return lax.ppermute(block, axis, route)  3.23 us
    ppermute x1, waiting for transfers between devices, carried_in(): got_own = lax.ppermute(own, axis, [(0, 1), (2, 3)])  2.89 us
  transfers between devices with their start and end apart: 7, of which 4 were waited for; matrix products, arithmetic and copies ran while one was open for 0% of the time, Pallas kernels for 24%

profile of v5, /device:TPU:8, one launch (start us, length us, event | category | flops | bytes accessed | tf_op | source)
XLA Modules:
  0.0 79.3 jit_solution(13469143300881952787)
XLA Ops:
  0.0 1.4 %ends.1 = bf16[3,16,1024]{2,1,0:T(8,128)(2,1)} custom-call(bf16[768,1024]{1,0:T(8,128)(2,1)} %qp_ref.3, bf16[768,1024]{1,0:T(8,128)(2,1)} %kp_ref.1, bf16[768,1024]{1,0:T(8,128)(2,1)} %vp_ref.1), custom_call_target="tpu_custom_call" | custom-call | tf_op jit(solution)/shard_map/ends/pallas_call | solution.py:331
  1.4 3.5 %collective-permute-start = (bf16[3,16,1024]{2,1,0:T(8,128)(2,1)}, bf16[3,16,1024]{2,1,0:T(8,128)(2,1)S(1)}, u32[]{:S(2)}, u32[]{:S(2)}) collective-permute-start(bf16[3,16,1024]{2,1,0:T(8,128)(2,1)} %ends.1), channel_id=1, source_target_pairs={{0,4},{4,8},{8,12},{1,5},{5,9},{9,13},{2,6},{6,10},{10,14},{3,7},{... | collective-permute-start | bytes 294920 | tf_op jit(solution)/shard_map/ppermute | solution.py:319
  4.9 3.2 %collective-permute-done.rim_ref = bf16[3,16,1024]{2,1,0:T(8,128)(2,1)S(1)} collective-permute-done((bf16[3,16,1024]{2,1,0:T(8,128)(2,1)}, bf16[3,16,1024]{2,1,0:T(8,128)(2,1)S(1)}, u32[]{:S(2)}, u32[]{:S(2)}) %collective-permute-start) | collective-permute-done | bytes 98336 | tf_op jit(solution)/shard_map/ppermute | solution.py:319
  8.1 17.1 %summary.1 = (bf16[768,1024]{1,0:T(8,128)(2,1)}, bf16[768,2048]{1,0:T(8,128)(2,1)}, bf16[6,8,128,256]{3,2,1,0:T(8,128)(2,1)}, bf16[8,128,256]{2,1,0:T(8,128)(2,1)S(1)}) custom-call(bf16[3,16,1024]{2,1,0:T(8,128)(2,1)S(1)} %collective-permute-done.rim_ref, bf16[768,1024]{1,0:T(8,128)(2,1)} %kp_ref.1, bf16[768,1024]{1,0:T(8,128)(2,1)} %vp_ref.1, ...), custom_call_target="tpu_custom_call" | custom-call | tf_op jit(solution)/shard_map/summary/pallas_call | solution.py:235
  25.3 1.3 %collective-permute-start.1 = (bf16[8,128,128]{2,1,0:T(8,128)(2,1)S(1)}, bf16[8,128,128]{2,1,0:T(8,128)(2,1)S(1)}, u32[]{:S(2)}, u32[]{:S(2)}) collective-permute-start(bf16[8,128,128]{2,1,0:T(8,128)(2,1)S(1)} %slice.7), channel_id=1, source_target_pairs={{0,4},{8,12},{1,5},{9,13},{2,6},{10,14},{3,7},{11,15},{16,20},{24,... | collective-permute-start | bytes 786440 | tf_op jit(solution)/shard_map/ppermute | solution.py:350
  26.6 4.6 %local.2 = (bf16[768,1024]{1,0:T(8,128)(2,1)}, bf16[768,1024]{1,0:T(8,128)(2,1)}) custom-call(bf16[3,16,1024]{2,1,0:T(8,128)(2,1)S(1)} %collective-permute-done.rim_ref, bf16[768,1024]{1,0:T(8,128)(2,1)} %qp_ref.3, bf16[768,1024]{1,0:T(8,128)(2,1)} %qp_ref.3, bf16[768,1024]{1,0:T(8,128)(2,1)} %get-tuple-element.24.keys_ref, ...), custom_call_target="tpu_custom_call" | custom-call | tf_op jit(solution)/shard_map/local/pallas_call | solution.py:268
  31.2 2.9 %collective-permute-done.1 = bf16[8,128,128]{2,1,0:T(8,128)(2,1)S(1)} collective-permute-done((bf16[8,128,128]{2,1,0:T(8,128)(2,1)S(1)}, bf16[8,128,128]{2,1,0:T(8,128)(2,1)S(1)}, u32[]{:S(2)}, u32[]{:S(2)}) %collective-permute-start.1) | collective-permute-done | bytes 262176 | tf_op jit(solution)/shard_map/ppermute | solution.py:350
  34.0 0.2 broadcast_select_fusion
  34.3 4.5 %collective-permute-start.3 = (bf16[8,128,128]{2,1,0:T(8,128)(2,1)S(1)}, bf16[8,128,128]{2,1,0:T(8,128)(2,1)S(1)}, u32[]{:S(2)}, u32[]{:S(2)}) collective-permute-start(bf16[8,128,128]{2,1,0:T(8,128)(2,1)S(1)} %get-tuple-element.42), channel_id=1, source_target_pairs={{4,12},{5,13},{6,14},{7,15},{20,28},{21,29},{22,30},{23,31}} | collective-permute-start | bytes 786440 | tf_op jit(solution)/shard_map/ppermute | solution.py:354
  38.8 1.3 %collective-permute-start.2 = (bf16[8,128,128]{2,1,0:T(8,128)(2,1)S(1)}, bf16[8,128,128]{2,1,0:T(8,128)(2,1)S(1)}, u32[]{:S(2)}, u32[]{:S(2)}) collective-permute-start(bf16[8,128,128]{2,1,0:T(8,128)(2,1)S(1)} %get-tuple-element.41), channel_id=1, source_target_pairs={{4,8},{8,12},{5,9},{9,13},{6,10},{10,14},{7,11},{11,15},{20,24},{2... | collective-permute-start | bytes 786440 | tf_op jit(solution)/shard_map/ppermute | solution.py:356
  40.8 0.0 slice-start
  40.8 0.1 pad_add_fusion.2.info_ref
  40.9 7.3 %local.3 = (bf16[768,1024]{1,0:T(8,128)(2,1)}, bf16[768,1024]{1,0:T(8,128)(2,1)}) custom-call(bf16[3,16,1024]{2,1,0:T(8,128)(2,1)S(1)} %collective-permute-done.rim_ref, bf16[768,1024]{1,0:T(8,128)(2,1)} %qp_ref.3, bf16[768,1024]{1,0:T(8,128)(2,1)} %qp_ref.3, ...), custom_call_target="tpu_custom_call", output_to_operand_aliasing={{0}: (8, {}), {1}: (9, {})} | custom-call | tf_op jit(solution)/shard_map/local/pallas_call | solution.py:268
  48.2 0.2 fusion.1.state_ref
  48.4 5.1 %outputs.2 = (bf16[192,2304]{1,0:T(8,128)(2,1)S(1)}, bf16[192,2304]{1,0:T(8,128)(2,1)S(1)}) custom-call(s32[4]{0:T(128)S(1)} %pad_add_fusion.2.info_ref, bf16[8,128,128]{2,1,0:T(8,128)(2,1)S(1)} %fusion.1.state_ref, bf16[768,1024]{1,0:T(8,128)(2,1)} %get-tuple-element.34.local_ref, bf16[768,1024]{1,0:T(8,128)(2,1)} %get-tuple-element.35.qeff_ref, ...), custom_call_target="tpu_custom_call" | custom-call | tf_op jit(solution)/shard_map/outputs/pallas_call | solution.py:393
  53.6 0.1 collective-permute-start.4
  53.7 0.1 pad_add_fusion.info_ref
  53.8 2.3 %collective-permute-done.4 = bf16[192,2304]{1,0:T(8,128)(2,1)S(1)} collective-permute-done((bf16[192,2304]{1,0:T(8,128)(2,1)S(1)}, bf16[192,2304]{1,0:T(8,128)(2,1)S(1)}, u32[]{:S(2)}, u32[]{:S(2)}) %collective-permute-start.4) | collective-permute-done | bytes 884768 | tf_op jit(solution)/shard_map/ppermute | solution.py:414
  56.1 0.2 add_convert_fusion.1
  56.3 1.6 %collective-permute-start.6 = (bf16[192,2304]{1,0:T(8,128)(2,1)S(1)}, bf16[192,2304]{1,0:T(8,128)(2,1)S(1)}, u32[]{:S(2)}, u32[]{:S(2)}) collective-permute-start(bf16[192,2304]{1,0:T(8,128)(2,1)S(1)} %add_convert_fusion.1), channel_id=1, source_target_pairs={{0,2},{1,3},{2,0},{3,1},{4,6},{5,7},{6,4},{7,5},{8,10},{9,11},{10,... | collective-permute-start | bytes 2654216 | tf_op jit(solution)/shard_map/ppermute | solution.py:414
  57.9 6.8 %outputs.3 = (bf16[192,2304]{1,0:T(8,128)(2,1)S(1)}, bf16[192,2304]{1,0:T(8,128)(2,1)S(1)}) custom-call(s32[4]{0:T(128)S(1)} %pad_add_fusion.info_ref, bf16[8,128,128]{2,1,0:T(8,128)(2,1)S(1)} %fusion.1.state_ref, bf16[768,1024]{1,0:T(8,128)(2,1)} %get-tuple-element.34.local_ref, bf16[768,1024]{1,0:T(8,128)(2,1)} %get-tuple-element.35.qeff_ref, ...), custom_call_target="tpu_custom_call" | custom-call | tf_op jit(solution)/shard_map/outputs/pallas_call | solution.py:393
  64.6 0.1 collective-permute-start.5
  64.7 13.3 %collective-permute-done.6 = bf16[192,2304]{1,0:T(8,128)(2,1)S(1)} collective-permute-done((bf16[192,2304]{1,0:T(8,128)(2,1)S(1)}, bf16[192,2304]{1,0:T(8,128)(2,1)S(1)}, u32[]{:S(2)}, u32[]{:S(2)}) %collective-permute-start.6) | collective-permute-done | bytes 884768 | tf_op jit(solution)/shard_map/ppermute | solution.py:414
  78.0 1.3 %add_convert_fusion = bf16[192,2304]{1,0:T(8,128)(2,1)} fusion(bf16[192,2304]{1,0:T(8,128)(2,1)S(1)} %collective-permute-done.6, bf16[192,2304]{1,0:T(8,128)(2,1)S(1)} %collective-permute-done.5, bf16[192,2304]{1,0:T(8,128)(2,1)S(1)} %get-tuple-element.39), kind=kLoop, calls=%fused_computation | loop fusion | flops 2654208 | bytes 3538944 | tf_op jit(solution)/shard_map/convert_element_type | solution.py:427
  (8 shorter events, 0.1 us)
Async XLA Ops:
  1.4 6.7 %collective-permute-start = (bf16[3,16,1024]{2,1,0:T(8,128)(2,1)}, bf16[3,16,1024]{2,1,0:T(8,128)(2,1)S(1)}, u32[]{:S(2)}, u32[]{:S(2)}) collective-permute-start(bf16[3,16,1024]{2,1,0:T(8,128)(2,1)} %ends.1), channel_id=1, source_target_pairs={{0,4},{4,8},{8,12},{1,5},{5,9},{9,13},{2,6},{6,10},{10,14},{3,7},{... | collective-permute-start | bytes 294920 | tf_op jit(solution)/shard_map/ppermute | solution.py:319
  25.3 8.8 %collective-permute-start.1 = (bf16[8,128,128]{2,1,0:T(8,128)(2,1)S(1)}, bf16[8,128,128]{2,1,0:T(8,128)(2,1)S(1)}, u32[]{:S(2)}, u32[]{:S(2)}) collective-permute-start(bf16[8,128,128]{2,1,0:T(8,128)(2,1)S(1)} %slice.7), channel_id=1, source_target_pairs={{0,4},{8,12},{1,5},{9,13},{2,6},{10,14},{3,7},{11,15},{16,20},{24,... | collective-permute-start | bytes 786440 | tf_op jit(solution)/shard_map/ppermute | solution.py:350
  34.3 13.9 %collective-permute-start.3 = (bf16[8,128,128]{2,1,0:T(8,128)(2,1)S(1)}, bf16[8,128,128]{2,1,0:T(8,128)(2,1)S(1)}, u32[]{:S(2)}, u32[]{:S(2)}) collective-permute-start(bf16[8,128,128]{2,1,0:T(8,128)(2,1)S(1)} %get-tuple-element.42), channel_id=1, source_target_pairs={{4,12},{5,13},{6,14},{7,15},{20,28},{21,29},{22,30},{23,31}} | collective-permute-start | bytes 786440 | tf_op jit(solution)/shard_map/ppermute | solution.py:354
  38.8 9.4 %collective-permute-start.2 = (bf16[8,128,128]{2,1,0:T(8,128)(2,1)S(1)}, bf16[8,128,128]{2,1,0:T(8,128)(2,1)S(1)}, u32[]{:S(2)}, u32[]{:S(2)}) collective-permute-start(bf16[8,128,128]{2,1,0:T(8,128)(2,1)S(1)} %get-tuple-element.41), channel_id=1, source_target_pairs={{4,8},{8,12},{5,9},{9,13},{6,10},{10,14},{7,11},{11,15},{20,24},{2... | collective-permute-start | bytes 786440 | tf_op jit(solution)/shard_map/ppermute | solution.py:356
  40.8 7.6 %slice-start = ((s8[4718592]{0:T(1024)(128)(4,1)}), s8[4194304]{0:T(1024)(128)(4,1)S(1)}, s32[]{:S(2)}) async-start(s8[4718592]{0:T(1024)(128)(4,1)} %bitcast.8), calls=%async_computation | async-start | bytes 8388608
  40.9 7.6 %slice-start.1 = ((s8[4718592]{0:T(1024)(128)(4,1)}), s8[524288]{0:T(1024)(128)(4,1)S(1)}, s32[]{:S(2)}) async-start(s8[4718592]{0:T(1024)(128)(4,1)} %bitcast.8), calls=%async_computation.1 | async-start | bytes 1048576
  53.6 2.5 %collective-permute-start.4 = (bf16[192,2304]{1,0:T(8,128)(2,1)S(1)}, bf16[192,2304]{1,0:T(8,128)(2,1)S(1)}, u32[]{:S(2)}, u32[]{:S(2)}) collective-permute-start(bf16[192,2304]{1,0:T(8,128)(2,1)S(1)} %get-tuple-element.37), channel_id=1, source_target_pairs={{0,1},{1,0},{2,3},{3,2},{4,5},{5,4},{6,7},{7,6},{8,9},{9,8},{10,11... | collective-permute-start | bytes 2654216 | tf_op jit(solution)/shard_map/ppermute | solution.py:414
  56.3 21.8 %collective-permute-start.6 = (bf16[192,2304]{1,0:T(8,128)(2,1)S(1)}, bf16[192,2304]{1,0:T(8,128)(2,1)S(1)}, u32[]{:S(2)}, u32[]{:S(2)}) collective-permute-start(bf16[192,2304]{1,0:T(8,128)(2,1)S(1)} %add_convert_fusion.1), channel_id=1, source_target_pairs={{0,2},{1,3},{2,0},{3,1},{4,6},{5,7},{6,4},{7,5},{8,10},{9,11},{10,... | collective-permute-start | bytes 2654216 | tf_op jit(solution)/shard_map/ppermute | solution.py:414
  64.6 13.4 %collective-permute-start.5 = (bf16[192,2304]{1,0:T(8,128)(2,1)S(1)}, bf16[192,2304]{1,0:T(8,128)(2,1)S(1)}, u32[]{:S(2)}, u32[]{:S(2)}) collective-permute-start(bf16[192,2304]{1,0:T(8,128)(2,1)S(1)} %get-tuple-element.40), channel_id=1, source_target_pairs={{0,1},{1,0},{2,3},{3,2},{4,5},{5,4},{6,7},{7,6},{8,9},{9,8},{10,11... | collective-permute-start | bytes 2654216 | tf_op jit(solution)/shard_map/ppermute | solution.py:414

commit v6 on v5

--- a/solution.py
+++ b/solution.py
@@ -347,18 +347,17 @@
         return jnp.einsum("hij,hjk->hik", a, s, preferred_element_type=F32) + b.astype(F32)
 
     if count == 4:
-        got_own = lax.ppermute(own, axis, [(0, 1), (2, 3)])
+        first = lax.ppermute(own, axis, [(0, 1)])
+        third = lax.ppermute(summary, axis, [(2, 3)])
         done = early()
-        got_own, done = lax.optimization_barrier((got_own, done))
-        pair = apply(move, own, got_own).astype(BF16)
+        first, done = lax.optimization_barrier((first, done))
+        pair = apply(move, own, first).astype(BF16)
         far = lax.ppermute(pair, axis, [(1, 3)])
-        place = lax.axis_index(axis)
-        next_in = lax.ppermute(jnp.where(place == 1, pair, move), axis, [(1, 2), (2, 3)])
+        near = lax.ppermute(pair, axis, [(1, 2)])
         done, pair = lax.optimization_barrier((done, pair))
         done = late(done)
-        got_move = jnp.where(place == 3, next_in, jnp.zeros_like(next_in))
-        near = jnp.where(place == 2, next_in.astype(F32), 0.0)
-        return (apply(got_move, got_own, far) + near).astype(BF16), *done
+        state = apply(third[:, :, :width], third[:, :, width:], far)
+        return (state + near.astype(F32) + first.astype(F32)).astype(BF16), *done
     state = passed_along(own, axis, 1)
     for _ in range(count - 2):
         state = passed_along(apply(move, own, state).astype(BF16), axis, 1)

time: 80.3 us -> 79.1 us (0.985)
  starting transfers between devices: 12.3 us -> 11.3 us
    ppermute x1, starting transfers between devices: 4.5 us -> 2.3 us  [carried_in(): far = lax.ppermute(pair, axis, [(1, 3)])]
    ppermute x2 -> x3, starting transfers between devices: 2.6 us -> 3.87 us  [the longest x1 1.88 us: carried_in(): near = lax.ppermute(pair, axis, [(1, 2)])]
    ppermute x2 -> x3, waiting for transfers between devices: 2.89 us -> 2.3 us  [the longest x1 2.2 us: carried_in(): first = lax.ppermute(own, axis, [(0, 1)])]
  transfers between devices with their start and end apart: 7 -> 8, of which waited for: 4 -> 5; matrix products, arithmetic and copies ran while one was open for 0% -> 0% of each run, Pallas kernels for 24% -> 24%
where the time goes in v6:
time: 79.1 us; the launch traced here: 77.8 us
  Pallas kernels  42.3 us (53%)
  waiting for transfers between devices  21.2 us (27%)
  starting transfers between devices  11.3 us (14%)
  other arithmetic  1.63 us (2%)
  between operations  0.8 us (1%)
    pallas_call x1, Pallas kernels, front(): pl.pallas_call(summary_kernel, grid=(steps // subs,), in_specs=[rims, big...  17.1 us
    ppermute x3, waiting for transfers between devices, exchange(): return lax.ppermute(block, 'head', [(i, i ^ bit) for i in range(owners)])  15.7 us
    pallas_call x2, Pallas kernels, partial(): pl.pallas_call(out_kernel, grid_spec=pltpu.PrefetchScalarGridSpec(num_sca...  11.9 us
    pallas_call x2, Pallas kernels, local_part(): pl.pallas_call(functools.partial(local_kernel, begin), grid=(count,), in_...  11.9 us
    ppermute x1, starting transfers between devices, passed_along(): return lax.ppermute(block, axis, route)  3.47 us
    ppermute x1, waiting for transfers between devices, passed_along(): return lax.ppermute(block, axis, route)  3.23 us
    ppermute x1, starting transfers between devices, carried_in(): far = lax.ppermute(pair, axis, [(1, 3)])  2.3 us
    ppermute x1, waiting for transfers between devices, carried_in(): first = lax.ppermute(own, axis, [(0, 1)])  2.2 us
  transfers between devices with their start and end apart: 8, of which 5 were waited for; matrix products, arithmetic and copies ran while one was open for 0% of the time, Pallas kernels for 24%

profile of v6, /device:TPU:8, one launch (start us, length us, event | category | flops | bytes accessed | tf_op | source)
XLA Modules:
  0.0 77.8 jit_solution(133487462541485696)
XLA Ops:
  0.0 1.4 %ends.1 = bf16[3,16,1024]{2,1,0:T(8,128)(2,1)} custom-call(bf16[768,1024]{1,0:T(8,128)(2,1)} %qp_ref.3, bf16[768,1024]{1,0:T(8,128)(2,1)} %kp_ref.1, bf16[768,1024]{1,0:T(8,128)(2,1)} %vp_ref.1), custom_call_target="tpu_custom_call" | custom-call | tf_op jit(solution)/shard_map/ends/pallas_call | solution.py:331
  1.4 3.5 %collective-permute-start = (bf16[3,16,1024]{2,1,0:T(8,128)(2,1)}, bf16[3,16,1024]{2,1,0:T(8,128)(2,1)S(1)}, u32[]{:S(2)}, u32[]{:S(2)}) collective-permute-start(bf16[3,16,1024]{2,1,0:T(8,128)(2,1)} %ends.1), channel_id=1, source_target_pairs={{0,4},{4,8},{8,12},{1,5},{5,9},{9,13},{2,6},{6,10},{10,14},{3,7},{... | collective-permute-start | bytes 294920 | tf_op jit(solution)/shard_map/ppermute | solution.py:319
  4.9 3.2 %collective-permute-done.rim_ref = bf16[3,16,1024]{2,1,0:T(8,128)(2,1)S(1)} collective-permute-done((bf16[3,16,1024]{2,1,0:T(8,128)(2,1)}, bf16[3,16,1024]{2,1,0:T(8,128)(2,1)S(1)}, u32[]{:S(2)}, u32[]{:S(2)}) %collective-permute-start) | collective-permute-done | bytes 98336 | tf_op jit(solution)/shard_map/ppermute | solution.py:319
  8.1 17.1 %summary.1 = (bf16[768,1024]{1,0:T(8,128)(2,1)}, bf16[768,2048]{1,0:T(8,128)(2,1)}, bf16[6,8,128,256]{3,2,1,0:T(8,128)(2,1)}, bf16[8,128,256]{2,1,0:T(8,128)(2,1)S(1)}) custom-call(bf16[3,16,1024]{2,1,0:T(8,128)(2,1)S(1)} %collective-permute-done.rim_ref, bf16[768,1024]{1,0:T(8,128)(2,1)} %kp_ref.1, bf16[768,1024]{1,0:T(8,128)(2,1)} %vp_ref.1, ...), custom_call_target="tpu_custom_call" | custom-call | tf_op jit(solution)/shard_map/summary/pallas_call | solution.py:235
  25.3 1.3 %collective-permute-start.2 = (bf16[8,128,128]{2,1,0:T(8,128)(2,1)S(1)}, bf16[8,128,128]{2,1,0:T(8,128)(2,1)S(1)}, u32[]{:S(2)}, u32[]{:S(2)}) collective-permute-start(bf16[8,128,128]{2,1,0:T(8,128)(2,1)S(1)} %slice.14), channel_id=1, source_target_pairs={{0,4},{1,5},{2,6},{3,7},{16,20},{17,21},{18,22},{19,23}} | collective-permute-start | bytes 786440 | tf_op jit(solution)/shard_map/ppermute | solution.py:350
  26.6 0.7 collective-permute-start.1
  27.3 4.6 %local.2 = (bf16[768,1024]{1,0:T(8,128)(2,1)}, bf16[768,1024]{1,0:T(8,128)(2,1)}) custom-call(bf16[3,16,1024]{2,1,0:T(8,128)(2,1)S(1)} %collective-permute-done.rim_ref, bf16[768,1024]{1,0:T(8,128)(2,1)} %qp_ref.3, bf16[768,1024]{1,0:T(8,128)(2,1)} %qp_ref.3, bf16[768,1024]{1,0:T(8,128)(2,1)} %get-tuple-element.24.keys_ref, ...), custom_call_target="tpu_custom_call" | custom-call | tf_op jit(solution)/shard_map/local/pallas_call | solution.py:268
  31.8 2.2 %collective-permute-done.2 = bf16[8,128,128]{2,1,0:T(8,128)(2,1)S(1)} collective-permute-done((bf16[8,128,128]{2,1,0:T(8,128)(2,1)S(1)}, bf16[8,128,128]{2,1,0:T(8,128)(2,1)S(1)}, u32[]{:S(2)}, u32[]{:S(2)}) %collective-permute-start.2) | collective-permute-done | bytes 262176 | tf_op jit(solution)/shard_map/ppermute | solution.py:350
  34.0 0.2 fusion.3
  34.3 2.3 %collective-permute-start.3 = (bf16[8,128,128]{2,1,0:T(8,128)(2,1)S(1)}, bf16[8,128,128]{2,1,0:T(8,128)(2,1)S(1)}, u32[]{:S(2)}, u32[]{:S(2)}) collective-permute-start(bf16[8,128,128]{2,1,0:T(8,128)(2,1)S(1)} %fusion.3), channel_id=1, source_target_pairs={{4,12},{5,13},{6,14},{7,15},{20,28},{21,29},{22,30},{23,31}} | collective-permute-start | bytes 786440 | tf_op jit(solution)/shard_map/ppermute | solution.py:355
  36.6 1.9 %collective-permute-start.4 = (bf16[8,128,128]{2,1,0:T(8,128)(2,1)S(1)}, bf16[8,128,128]{2,1,0:T(8,128)(2,1)S(1)}, u32[]{:S(2)}, u32[]{:S(2)}) collective-permute-start(bf16[8,128,128]{2,1,0:T(8,128)(2,1)S(1)} %fusion.3), channel_id=1, source_target_pairs={{4,8},{5,9},{6,10},{7,11},{20,24},{21,25},{22,26},{23,27}} | collective-permute-start | bytes 786440 | tf_op jit(solution)/shard_map/ppermute | solution.py:356
  39.1 0.1 pad_add_fusion.2.info_ref
  39.2 7.3 %local.3 = (bf16[768,1024]{1,0:T(8,128)(2,1)}, bf16[768,1024]{1,0:T(8,128)(2,1)}) custom-call(bf16[3,16,1024]{2,1,0:T(8,128)(2,1)S(1)} %collective-permute-done.rim_ref, bf16[768,1024]{1,0:T(8,128)(2,1)} %qp_ref.3, bf16[768,1024]{1,0:T(8,128)(2,1)} %qp_ref.3, ...), custom_call_target="tpu_custom_call", output_to_operand_aliasing={{0}: (8, {}), {1}: (9, {})} | custom-call | tf_op jit(solution)/shard_map/local/pallas_call | solution.py:268
  46.5 0.1 collective-permute-done.4
  46.6 0.3 fusion.2.state_ref
  46.9 5.1 %outputs.2 = (bf16[192,2304]{1,0:T(8,128)(2,1)S(1)}, bf16[192,2304]{1,0:T(8,128)(2,1)S(1)}) custom-call(s32[4]{0:T(128)S(1)} %pad_add_fusion.2.info_ref, bf16[8,128,128]{2,1,0:T(8,128)(2,1)S(1)} %fusion.2.state_ref, bf16[768,1024]{1,0:T(8,128)(2,1)} %get-tuple-element.34.local_ref, bf16[768,1024]{1,0:T(8,128)(2,1)} %get-tuple-element.35.qeff_ref, ...), custom_call_target="tpu_custom_call" | custom-call | tf_op jit(solution)/shard_map/outputs/pallas_call | solution.py:392
  52.1 0.1 collective-permute-start.5
  52.1 0.1 pad_add_fusion.info_ref
  52.2 2.3 %collective-permute-done.5 = bf16[192,2304]{1,0:T(8,128)(2,1)S(1)} collective-permute-done((bf16[192,2304]{1,0:T(8,128)(2,1)S(1)}, bf16[192,2304]{1,0:T(8,128)(2,1)S(1)}, u32[]{:S(2)}, u32[]{:S(2)}) %collective-permute-start.5) | collective-permute-done | bytes 884768 | tf_op jit(solution)/shard_map/ppermute | solution.py:413
  54.5 0.2 add_convert_fusion.1
  54.8 1.6 %collective-permute-start.7 = (bf16[192,2304]{1,0:T(8,128)(2,1)S(1)}, bf16[192,2304]{1,0:T(8,128)(2,1)S(1)}, u32[]{:S(2)}, u32[]{:S(2)}) collective-permute-start(bf16[192,2304]{1,0:T(8,128)(2,1)S(1)} %add_convert_fusion.1), channel_id=1, source_target_pairs={{0,2},{1,3},{2,0},{3,1},{4,6},{5,7},{6,4},{7,5},{8,10},{9,11},{10,... | collective-permute-start | bytes 2654216 | tf_op jit(solution)/shard_map/ppermute | solution.py:413
  56.3 6.8 %outputs.3 = (bf16[192,2304]{1,0:T(8,128)(2,1)S(1)}, bf16[192,2304]{1,0:T(8,128)(2,1)S(1)}) custom-call(s32[4]{0:T(128)S(1)} %pad_add_fusion.info_ref, bf16[8,128,128]{2,1,0:T(8,128)(2,1)S(1)} %fusion.2.state_ref, bf16[768,1024]{1,0:T(8,128)(2,1)} %get-tuple-element.34.local_ref, bf16[768,1024]{1,0:T(8,128)(2,1)} %get-tuple-element.35.qeff_ref, ...), custom_call_target="tpu_custom_call" | custom-call | tf_op jit(solution)/shard_map/outputs/pallas_call | solution.py:392
  63.2 13.3 %collective-permute-done.7 = bf16[192,2304]{1,0:T(8,128)(2,1)S(1)} collective-permute-done((bf16[192,2304]{1,0:T(8,128)(2,1)S(1)}, bf16[192,2304]{1,0:T(8,128)(2,1)S(1)}, u32[]{:S(2)}, u32[]{:S(2)}) %collective-permute-start.7) | collective-permute-done | bytes 884768 | tf_op jit(solution)/shard_map/ppermute | solution.py:413
  76.5 1.3 %add_convert_fusion = bf16[192,2304]{1,0:T(8,128)(2,1)} fusion(bf16[192,2304]{1,0:T(8,128)(2,1)S(1)} %collective-permute-done.7, bf16[192,2304]{1,0:T(8,128)(2,1)S(1)} %collective-permute-done.6, bf16[192,2304]{1,0:T(8,128)(2,1)S(1)} %get-tuple-element.39), kind=kLoop, calls=%fused_computation | loop fusion | flops 2654208 | bytes 3538944 | tf_op jit(solution)/shard_map/convert_element_type | solution.py:426
  (10 shorter events, 0.1 us)
Async XLA Ops:
  1.4 6.7 %collective-permute-start = (bf16[3,16,1024]{2,1,0:T(8,128)(2,1)}, bf16[3,16,1024]{2,1,0:T(8,128)(2,1)S(1)}, u32[]{:S(2)}, u32[]{:S(2)}) collective-permute-start(bf16[3,16,1024]{2,1,0:T(8,128)(2,1)} %ends.1), channel_id=1, source_target_pairs={{0,4},{4,8},{8,12},{1,5},{5,9},{9,13},{2,6},{6,10},{10,14},{3,7},{... | collective-permute-start | bytes 294920 | tf_op jit(solution)/shard_map/ppermute | solution.py:319
  25.3 8.8 %collective-permute-start.2 = (bf16[8,128,128]{2,1,0:T(8,128)(2,1)S(1)}, bf16[8,128,128]{2,1,0:T(8,128)(2,1)S(1)}, u32[]{:S(2)}, u32[]{:S(2)}) collective-permute-start(bf16[8,128,128]{2,1,0:T(8,128)(2,1)S(1)} %slice.14), channel_id=1, source_target_pairs={{0,4},{1,5},{2,6},{3,7},{16,20},{17,21},{18,22},{19,23}} | collective-permute-start | bytes 786440 | tf_op jit(solution)/shard_map/ppermute | solution.py:350
  26.6 20.1 %collective-permute-start.1 = (bf16[8,128,256]{2,1,0:T(8,128)(2,1)S(1)}, bf16[8,128,256]{2,1,0:T(8,128)(2,1)S(1)}, u32[]{:S(2)}, u32[]{:S(2)}) collective-permute-start(bf16[8,128,256]{2,1,0:T(8,128)(2,1)S(1)} %get-tuple-element.23), channel_id=1, source_target_pairs={{8,12},{9,13},{10,14},{11,15},{24,28},{25,29},{26,30},{27,31}} | collective-permute-start | bytes 1572872 | tf_op jit(solution)/shard_map/ppermute | solution.py:351
  34.3 12.2 %collective-permute-start.3 = (bf16[8,128,128]{2,1,0:T(8,128)(2,1)S(1)}, bf16[8,128,128]{2,1,0:T(8,128)(2,1)S(1)}, u32[]{:S(2)}, u32[]{:S(2)}) collective-permute-start(bf16[8,128,128]{2,1,0:T(8,128)(2,1)S(1)} %fusion.3), channel_id=1, source_target_pairs={{4,12},{5,13},{6,14},{7,15},{20,28},{21,29},{22,30},{23,31}} | collective-permute-start | bytes 786440 | tf_op jit(solution)/shard_map/ppermute | solution.py:355
  36.6 10.0 %collective-permute-start.4 = (bf16[8,128,128]{2,1,0:T(8,128)(2,1)S(1)}, bf16[8,128,128]{2,1,0:T(8,128)(2,1)S(1)}, u32[]{:S(2)}, u32[]{:S(2)}) collective-permute-start(bf16[8,128,128]{2,1,0:T(8,128)(2,1)S(1)} %fusion.3), channel_id=1, source_target_pairs={{4,8},{5,9},{6,10},{7,11},{20,24},{21,25},{22,26},{23,27}} | collective-permute-start | bytes 786440 | tf_op jit(solution)/shard_map/ppermute | solution.py:356
  39.1 7.8 %slice-start = ((s8[4718592]{0:T(1024)(128)(4,1)}), s8[4194304]{0:T(1024)(128)(4,1)S(1)}, s32[]{:S(2)}) async-start(s8[4718592]{0:T(1024)(128)(4,1)} %bitcast.8), calls=%async_computation | async-start | bytes 8388608
  39.2 7.7 %slice-start.1 = ((s8[4718592]{0:T(1024)(128)(4,1)}), s8[524288]{0:T(1024)(128)(4,1)S(1)}, s32[]{:S(2)}) async-start(s8[4718592]{0:T(1024)(128)(4,1)} %bitcast.8), calls=%async_computation.1 | async-start | bytes 1048576
  52.1 2.5 %collective-permute-start.5 = (bf16[192,2304]{1,0:T(8,128)(2,1)S(1)}, bf16[192,2304]{1,0:T(8,128)(2,1)S(1)}, u32[]{:S(2)}, u32[]{:S(2)}) collective-permute-start(bf16[192,2304]{1,0:T(8,128)(2,1)S(1)} %get-tuple-element.37), channel_id=1, source_target_pairs={{0,1},{1,0},{2,3},{3,2},{4,5},{5,4},{6,7},{7,6},{8,9},{9,8},{10,11... | collective-permute-start | bytes 2654216 | tf_op jit(solution)/shard_map/ppermute | solution.py:413
  54.8 21.8 %collective-permute-start.7 = (bf16[192,2304]{1,0:T(8,128)(2,1)S(1)}, bf16[192,2304]{1,0:T(8,128)(2,1)S(1)}, u32[]{:S(2)}, u32[]{:S(2)}) collective-permute-start(bf16[192,2304]{1,0:T(8,128)(2,1)S(1)} %add_convert_fusion.1), channel_id=1, source_target_pairs={{0,2},{1,3},{2,0},{3,1},{4,6},{5,7},{6,4},{7,5},{8,10},{9,11},{10,... | collective-permute-start | bytes 2654216 | tf_op jit(solution)/shard_map/ppermute | solution.py:413
  63.1 13.4 %collective-permute-start.6 = (bf16[192,2304]{1,0:T(8,128)(2,1)S(1)}, bf16[192,2304]{1,0:T(8,128)(2,1)S(1)}, u32[]{:S(2)}, u32[]{:S(2)}) collective-permute-start(bf16[192,2304]{1,0:T(8,128)(2,1)S(1)} %get-tuple-element.40), channel_id=1, source_target_pairs={{0,1},{1,0},{2,3},{3,2},{4,5},{5,4},{6,7},{7,6},{8,9},{9,8},{10,11... | collective-permute-start | bytes 2654216 | tf_op jit(solution)/shard_map/ppermute | solution.py:413

commit v7 on v6

--- a/solution.py
+++ b/solution.py
@@ -352,8 +352,8 @@
         done = early()
         first, done = lax.optimization_barrier((first, done))
         pair = apply(move, own, first).astype(BF16)
+        near = lax.ppermute(pair, axis, [(1, 2)])
         far = lax.ppermute(pair, axis, [(1, 3)])
-        near = lax.ppermute(pair, axis, [(1, 2)])
         done, pair = lax.optimization_barrier((done, pair))
         done = late(done)
         state = apply(third[:, :, :width], third[:, :, width:], far)

time: 79.1 us -> 79.1 us (level)
  no operation moved by 1% of the time
where the time goes in v7:
time: 79.1 us; the launch traced here: 77.8 us
  Pallas kernels  42.3 us (53%)
  waiting for transfers between devices  21.2 us (27%)
  starting transfers between devices  11.3 us (14%)
  other arithmetic  1.63 us (2%)
  between operations  0.8 us (1%)
    pallas_call x1, Pallas kernels, front(): pl.pallas_call(summary_kernel, grid=(steps // subs,), in_specs=[rims, big...  17.1 us
    ppermute x3, waiting for transfers between devices, exchange(): return lax.ppermute(block, 'head', [(i, i ^ bit) for i in range(owners)])  15.7 us
    pallas_call x2, Pallas kernels, partial(): pl.pallas_call(out_kernel, grid_spec=pltpu.PrefetchScalarGridSpec(num_sca...  11.9 us
    pallas_call x2, Pallas kernels, local_part(): pl.pallas_call(functools.partial(local_kernel, begin), grid=(count,), in_...  11.9 us
    ppermute x1, starting transfers between devices, passed_along(): return lax.ppermute(block, axis, route)  3.47 us
    ppermute x1, waiting for transfers between devices, passed_along(): return lax.ppermute(block, axis, route)  3.23 us
    ppermute x1, starting transfers between devices, carried_in(): far = lax.ppermute(pair, axis, [(1, 3)])  2.3 us
    ppermute x1, waiting for transfers between devices, carried_in(): first = lax.ppermute(own, axis, [(0, 1)])  2.2 us
  transfers between devices with their start and end apart: 8, of which 5 were waited for; matrix products, arithmetic and copies ran while one was open for 0% of the time, Pallas kernels for 24%

profile of v7, /device:TPU:8, one launch (start us, length us, event | category | flops | bytes accessed | tf_op | source)
XLA Modules:
  0.0 77.8 jit_solution(133487462541485696)
XLA Ops:
  0.0 1.4 %ends.1 = bf16[3,16,1024]{2,1,0:T(8,128)(2,1)} custom-call(bf16[768,1024]{1,0:T(8,128)(2,1)} %qp_ref.3, bf16[768,1024]{1,0:T(8,128)(2,1)} %kp_ref.1, bf16[768,1024]{1,0:T(8,128)(2,1)} %vp_ref.1), custom_call_target="tpu_custom_call" | custom-call | tf_op jit(solution)/shard_map/ends/pallas_call | solution.py:331
  1.4 3.5 %collective-permute-start = (bf16[3,16,1024]{2,1,0:T(8,128)(2,1)}, bf16[3,16,1024]{2,1,0:T(8,128)(2,1)S(1)}, u32[]{:S(2)}, u32[]{:S(2)}) collective-permute-start(bf16[3,16,1024]{2,1,0:T(8,128)(2,1)} %ends.1), channel_id=1, source_target_pairs={{0,4},{4,8},{8,12},{1,5},{5,9},{9,13},{2,6},{6,10},{10,14},{3,7},{... | collective-permute-start | bytes 294920 | tf_op jit(solution)/shard_map/ppermute | solution.py:319
  4.9 3.2 %collective-permute-done.rim_ref = bf16[3,16,1024]{2,1,0:T(8,128)(2,1)S(1)} collective-permute-done((bf16[3,16,1024]{2,1,0:T(8,128)(2,1)}, bf16[3,16,1024]{2,1,0:T(8,128)(2,1)S(1)}, u32[]{:S(2)}, u32[]{:S(2)}) %collective-permute-start) | collective-permute-done | bytes 98336 | tf_op jit(solution)/shard_map/ppermute | solution.py:319
  8.1 17.1 %summary.1 = (bf16[768,1024]{1,0:T(8,128)(2,1)}, bf16[768,2048]{1,0:T(8,128)(2,1)}, bf16[6,8,128,256]{3,2,1,0:T(8,128)(2,1)}, bf16[8,128,256]{2,1,0:T(8,128)(2,1)S(1)}) custom-call(bf16[3,16,1024]{2,1,0:T(8,128)(2,1)S(1)} %collective-permute-done.rim_ref, bf16[768,1024]{1,0:T(8,128)(2,1)} %kp_ref.1, bf16[768,1024]{1,0:T(8,128)(2,1)} %vp_ref.1, ...), custom_call_target="tpu_custom_call" | custom-call | tf_op jit(solution)/shard_map/summary/pallas_call | solution.py:235
  25.3 1.3 %collective-permute-start.2 = (bf16[8,128,128]{2,1,0:T(8,128)(2,1)S(1)}, bf16[8,128,128]{2,1,0:T(8,128)(2,1)S(1)}, u32[]{:S(2)}, u32[]{:S(2)}) collective-permute-start(bf16[8,128,128]{2,1,0:T(8,128)(2,1)S(1)} %slice.14), channel_id=1, source_target_pairs={{0,4},{1,5},{2,6},{3,7},{16,20},{17,21},{18,22},{19,23}} | collective-permute-start | bytes 786440 | tf_op jit(solution)/shard_map/ppermute | solution.py:350
  26.6 0.7 collective-permute-start.1
  27.3 4.6 %local.2 = (bf16[768,1024]{1,0:T(8,128)(2,1)}, bf16[768,1024]{1,0:T(8,128)(2,1)}) custom-call(bf16[3,16,1024]{2,1,0:T(8,128)(2,1)S(1)} %collective-permute-done.rim_ref, bf16[768,1024]{1,0:T(8,128)(2,1)} %qp_ref.3, bf16[768,1024]{1,0:T(8,128)(2,1)} %qp_ref.3, bf16[768,1024]{1,0:T(8,128)(2,1)} %get-tuple-element.24.keys_ref, ...), custom_call_target="tpu_custom_call" | custom-call | tf_op jit(solution)/shard_map/local/pallas_call | solution.py:268
  31.8 2.2 %collective-permute-done.2 = bf16[8,128,128]{2,1,0:T(8,128)(2,1)S(1)} collective-permute-done((bf16[8,128,128]{2,1,0:T(8,128)(2,1)S(1)}, bf16[8,128,128]{2,1,0:T(8,128)(2,1)S(1)}, u32[]{:S(2)}, u32[]{:S(2)}) %collective-permute-start.2) | collective-permute-done | bytes 262176 | tf_op jit(solution)/shard_map/ppermute | solution.py:350
  34.0 0.2 fusion.3
  34.3 2.3 %collective-permute-start.3 = (bf16[8,128,128]{2,1,0:T(8,128)(2,1)S(1)}, bf16[8,128,128]{2,1,0:T(8,128)(2,1)S(1)}, u32[]{:S(2)}, u32[]{:S(2)}) collective-permute-start(bf16[8,128,128]{2,1,0:T(8,128)(2,1)S(1)} %fusion.3), channel_id=1, source_target_pairs={{4,12},{5,13},{6,14},{7,15},{20,28},{21,29},{22,30},{23,31}} | collective-permute-start | bytes 786440 | tf_op jit(solution)/shard_map/ppermute | solution.py:356
  36.6 1.9 %collective-permute-start.4 = (bf16[8,128,128]{2,1,0:T(8,128)(2,1)S(1)}, bf16[8,128,128]{2,1,0:T(8,128)(2,1)S(1)}, u32[]{:S(2)}, u32[]{:S(2)}) collective-permute-start(bf16[8,128,128]{2,1,0:T(8,128)(2,1)S(1)} %fusion.3), channel_id=1, source_target_pairs={{4,8},{5,9},{6,10},{7,11},{20,24},{21,25},{22,26},{23,27}} | collective-permute-start | bytes 786440 | tf_op jit(solution)/shard_map/ppermute | solution.py:355
  39.1 0.1 pad_add_fusion.2.info_ref
  39.2 7.3 %local.3 = (bf16[768,1024]{1,0:T(8,128)(2,1)}, bf16[768,1024]{1,0:T(8,128)(2,1)}) custom-call(bf16[3,16,1024]{2,1,0:T(8,128)(2,1)S(1)} %collective-permute-done.rim_ref, bf16[768,1024]{1,0:T(8,128)(2,1)} %qp_ref.3, bf16[768,1024]{1,0:T(8,128)(2,1)} %qp_ref.3, ...), custom_call_target="tpu_custom_call", output_to_operand_aliasing={{0}: (8, {}), {1}: (9, {})} | custom-call | tf_op jit(solution)/shard_map/local/pallas_call | solution.py:268
  46.5 0.1 collective-permute-done.4
  46.6 0.3 fusion.2.state_ref
  46.9 5.1 %outputs.2 = (bf16[192,2304]{1,0:T(8,128)(2,1)S(1)}, bf16[192,2304]{1,0:T(8,128)(2,1)S(1)}) custom-call(s32[4]{0:T(128)S(1)} %pad_add_fusion.2.info_ref, bf16[8,128,128]{2,1,0:T(8,128)(2,1)S(1)} %fusion.2.state_ref, bf16[768,1024]{1,0:T(8,128)(2,1)} %get-tuple-element.34.local_ref, bf16[768,1024]{1,0:T(8,128)(2,1)} %get-tuple-element.35.qeff_ref, ...), custom_call_target="tpu_custom_call" | custom-call | tf_op jit(solution)/shard_map/outputs/pallas_call | solution.py:392
  52.1 0.1 collective-permute-start.5
  52.1 0.1 pad_add_fusion.info_ref
  52.2 2.3 %collective-permute-done.5 = bf16[192,2304]{1,0:T(8,128)(2,1)S(1)} collective-permute-done((bf16[192,2304]{1,0:T(8,128)(2,1)S(1)}, bf16[192,2304]{1,0:T(8,128)(2,1)S(1)}, u32[]{:S(2)}, u32[]{:S(2)}) %collective-permute-start.5) | collective-permute-done | bytes 884768 | tf_op jit(solution)/shard_map/ppermute | solution.py:413
  54.5 0.2 add_convert_fusion.1
  54.8 1.6 %collective-permute-start.7 = (bf16[192,2304]{1,0:T(8,128)(2,1)S(1)}, bf16[192,2304]{1,0:T(8,128)(2,1)S(1)}, u32[]{:S(2)}, u32[]{:S(2)}) collective-permute-start(bf16[192,2304]{1,0:T(8,128)(2,1)S(1)} %add_convert_fusion.1), channel_id=1, source_target_pairs={{0,2},{1,3},{2,0},{3,1},{4,6},{5,7},{6,4},{7,5},{8,10},{9,11},{10,... | collective-permute-start | bytes 2654216 | tf_op jit(solution)/shard_map/ppermute | solution.py:413
  56.3 6.8 %outputs.3 = (bf16[192,2304]{1,0:T(8,128)(2,1)S(1)}, bf16[192,2304]{1,0:T(8,128)(2,1)S(1)}) custom-call(s32[4]{0:T(128)S(1)} %pad_add_fusion.info_ref, bf16[8,128,128]{2,1,0:T(8,128)(2,1)S(1)} %fusion.2.state_ref, bf16[768,1024]{1,0:T(8,128)(2,1)} %get-tuple-element.34.local_ref, bf16[768,1024]{1,0:T(8,128)(2,1)} %get-tuple-element.35.qeff_ref, ...), custom_call_target="tpu_custom_call" | custom-call | tf_op jit(solution)/shard_map/outputs/pallas_call | solution.py:392
  63.2 13.3 %collective-permute-done.7 = bf16[192,2304]{1,0:T(8,128)(2,1)S(1)} collective-permute-done((bf16[192,2304]{1,0:T(8,128)(2,1)S(1)}, bf16[192,2304]{1,0:T(8,128)(2,1)S(1)}, u32[]{:S(2)}, u32[]{:S(2)}) %collective-permute-start.7) | collective-permute-done | bytes 884768 | tf_op jit(solution)/shard_map/ppermute | solution.py:413
  76.5 1.3 %add_convert_fusion = bf16[192,2304]{1,0:T(8,128)(2,1)} fusion(bf16[192,2304]{1,0:T(8,128)(2,1)S(1)} %collective-permute-done.7, bf16[192,2304]{1,0:T(8,128)(2,1)S(1)} %collective-permute-done.6, bf16[192,2304]{1,0:T(8,128)(2,1)S(1)} %get-tuple-element.39), kind=kLoop, calls=%fused_computation | loop fusion | flops 2654208 | bytes 3538944 | tf_op jit(solution)/shard_map/convert_element_type | solution.py:426
  (10 shorter events, 0.1 us)
Async XLA Ops:
  1.4 6.7 %collective-permute-start = (bf16[3,16,1024]{2,1,0:T(8,128)(2,1)}, bf16[3,16,1024]{2,1,0:T(8,128)(2,1)S(1)}, u32[]{:S(2)}, u32[]{:S(2)}) collective-permute-start(bf16[3,16,1024]{2,1,0:T(8,128)(2,1)} %ends.1), channel_id=1, source_target_pairs={{0,4},{4,8},{8,12},{1,5},{5,9},{9,13},{2,6},{6,10},{10,14},{3,7},{... | collective-permute-start | bytes 294920 | tf_op jit(solution)/shard_map/ppermute | solution.py:319
  25.3 8.8 %collective-permute-start.2 = (bf16[8,128,128]{2,1,0:T(8,128)(2,1)S(1)}, bf16[8,128,128]{2,1,0:T(8,128)(2,1)S(1)}, u32[]{:S(2)}, u32[]{:S(2)}) collective-permute-start(bf16[8,128,128]{2,1,0:T(8,128)(2,1)S(1)} %slice.14), channel_id=1, source_target_pairs={{0,4},{1,5},{2,6},{3,7},{16,20},{17,21},{18,22},{19,23}} | collective-permute-start | bytes 786440 | tf_op jit(solution)/shard_map/ppermute | solution.py:350
  26.6 20.1 %collective-permute-start.1 = (bf16[8,128,256]{2,1,0:T(8,128)(2,1)S(1)}, bf16[8,128,256]{2,1,0:T(8,128)(2,1)S(1)}, u32[]{:S(2)}, u32[]{:S(2)}) collective-permute-start(bf16[8,128,256]{2,1,0:T(8,128)(2,1)S(1)} %get-tuple-element.23), channel_id=1, source_target_pairs={{8,12},{9,13},{10,14},{11,15},{24,28},{25,29},{26,30},{27,31}} | collective-permute-start | bytes 1572872 | tf_op jit(solution)/shard_map/ppermute | solution.py:351
  34.3 12.2 %collective-permute-start.3 = (bf16[8,128,128]{2,1,0:T(8,128)(2,1)S(1)}, bf16[8,128,128]{2,1,0:T(8,128)(2,1)S(1)}, u32[]{:S(2)}, u32[]{:S(2)}) collective-permute-start(bf16[8,128,128]{2,1,0:T(8,128)(2,1)S(1)} %fusion.3), channel_id=1, source_target_pairs={{4,12},{5,13},{6,14},{7,15},{20,28},{21,29},{22,30},{23,31}} | collective-permute-start | bytes 786440 | tf_op jit(solution)/shard_map/ppermute | solution.py:356
  36.6 10.0 %collective-permute-start.4 = (bf16[8,128,128]{2,1,0:T(8,128)(2,1)S(1)}, bf16[8,128,128]{2,1,0:T(8,128)(2,1)S(1)}, u32[]{:S(2)}, u32[]{:S(2)}) collective-permute-start(bf16[8,128,128]{2,1,0:T(8,128)(2,1)S(1)} %fusion.3), channel_id=1, source_target_pairs={{4,8},{5,9},{6,10},{7,11},{20,24},{21,25},{22,26},{23,27}} | collective-permute-start | bytes 786440 | tf_op jit(solution)/shard_map/ppermute | solution.py:355
  39.1 7.8 %slice-start = ((s8[4718592]{0:T(1024)(128)(4,1)}), s8[4194304]{0:T(1024)(128)(4,1)S(1)}, s32[]{:S(2)}) async-start(s8[4718592]{0:T(1024)(128)(4,1)} %bitcast.8), calls=%async_computation | async-start | bytes 8388608
  39.2 7.7 %slice-start.1 = ((s8[4718592]{0:T(1024)(128)(4,1)}), s8[524288]{0:T(1024)(128)(4,1)S(1)}, s32[]{:S(2)}) async-start(s8[4718592]{0:T(1024)(128)(4,1)} %bitcast.8), calls=%async_computation.1 | async-start | bytes 1048576
  52.1 2.5 %collective-permute-start.5 = (bf16[192,2304]{1,0:T(8,128)(2,1)S(1)}, bf16[192,2304]{1,0:T(8,128)(2,1)S(1)}, u32[]{:S(2)}, u32[]{:S(2)}) collective-permute-start(bf16[192,2304]{1,0:T(8,128)(2,1)S(1)} %get-tuple-element.37), channel_id=1, source_target_pairs={{0,1},{1,0},{2,3},{3,2},{4,5},{5,4},{6,7},{7,6},{8,9},{9,8},{10,11... | collective-permute-start | bytes 2654216 | tf_op jit(solution)/shard_map/ppermute | solution.py:413
  54.8 21.8 %collective-permute-start.7 = (bf16[192,2304]{1,0:T(8,128)(2,1)S(1)}, bf16[192,2304]{1,0:T(8,128)(2,1)S(1)}, u32[]{:S(2)}, u32[]{:S(2)}) collective-permute-start(bf16[192,2304]{1,0:T(8,128)(2,1)S(1)} %add_convert_fusion.1), channel_id=1, source_target_pairs={{0,2},{1,3},{2,0},{3,1},{4,6},{5,7},{6,4},{7,5},{8,10},{9,11},{10,... | collective-permute-start | bytes 2654216 | tf_op jit(solution)/shard_map/ppermute | solution.py:413
  63.1 13.4 %collective-permute-start.6 = (bf16[192,2304]{1,0:T(8,128)(2,1)S(1)}, bf16[192,2304]{1,0:T(8,128)(2,1)S(1)}, u32[]{:S(2)}, u32[]{:S(2)}) collective-permute-start(bf16[192,2304]{1,0:T(8,128)(2,1)S(1)} %get-tuple-element.40), channel_id=1, source_target_pairs={{0,1},{1,0},{2,3},{3,2},{4,5},{5,4},{6,7},{7,6},{8,9},{9,8},{10,11... | collective-permute-start | bytes 2654216 | tf_op jit(solution)/shard_map/ppermute | solution.py:413

commit v8 on v6

--- a/solution.py
+++ b/solution.py
@@ -142,7 +142,7 @@
         for i in n
     ]
     mixed = [mm(inv[i], sides[i]) for i in n]
-    k_out = [(kf[i].T * row(kout_row, i)).astype(BF16) for i in n]
+    k_out = [(k[i].T.astype(F32) * row(kout_row, i)).astype(BF16) for i in n]
     for s in range(subs):
         at = s * heads
         start = [state_ref[h].astype(BF16) for h in range(heads)]

time: 79.1 us -> 78.9 us (level)
  no operation moved by 1% of the time
where the time goes in v8:
time: 78.9 us; the launch traced here: 77.6 us
  Pallas kernels  42.1 us (53%)
  waiting for transfers between devices  21.2 us (27%)
  starting transfers between devices  11.4 us (14%)
  other arithmetic  1.63 us (2%)
  between operations  0.8 us (1%)
    pallas_call x1, Pallas kernels, front(): pl.pallas_call(summary_kernel, grid=(steps // subs,), in_specs=[rims, big...  16.9 us
    ppermute x3, waiting for transfers between devices, exchange(): return lax.ppermute(block, 'head', [(i, i ^ bit) for i in range(owners)])  15.7 us
    pallas_call x2, Pallas kernels, partial(): pl.pallas_call(out_kernel, grid_spec=pltpu.PrefetchScalarGridSpec(num_sca...  11.9 us
    pallas_call x2, Pallas kernels, local_part(): pl.pallas_call(functools.partial(local_kernel, begin), grid=(count,), in_...  11.9 us
    ppermute x1, starting transfers between devices, passed_along(): return lax.ppermute(block, axis, route)  3.47 us
    ppermute x1, waiting for transfers between devices, passed_along(): return lax.ppermute(block, axis, route)  3.23 us
    ppermute x1, starting transfers between devices, carried_in(): far = lax.ppermute(pair, axis, [(1, 3)])  2.31 us
    ppermute x1, waiting for transfers between devices, carried_in(): first = lax.ppermute(own, axis, [(0, 1)])  2.2 us
  transfers between devices with their start and end apart: 8, of which 5 were waited for; matrix products, arithmetic and copies ran while one was open for 0% of the time, Pallas kernels for 24%

profile of v8, /device:TPU:8, one launch (start us, length us, event | category | flops | bytes accessed | tf_op | source)
XLA Modules:
  0.0 77.6 jit_solution(3340182282838316501)
XLA Ops:
  0.0 1.4 %ends.1 = bf16[3,16,1024]{2,1,0:T(8,128)(2,1)} custom-call(bf16[768,1024]{1,0:T(8,128)(2,1)} %qp_ref.3, bf16[768,1024]{1,0:T(8,128)(2,1)} %kp_ref.1, bf16[768,1024]{1,0:T(8,128)(2,1)} %vp_ref.1), custom_call_target="tpu_custom_call" | custom-call | tf_op jit(solution)/shard_map/ends/pallas_call | solution.py:331
  1.4 3.5 %collective-permute-start = (bf16[3,16,1024]{2,1,0:T(8,128)(2,1)}, bf16[3,16,1024]{2,1,0:T(8,128)(2,1)S(1)}, u32[]{:S(2)}, u32[]{:S(2)}) collective-permute-start(bf16[3,16,1024]{2,1,0:T(8,128)(2,1)} %ends.1), channel_id=1, source_target_pairs={{0,4},{4,8},{8,12},{1,5},{5,9},{9,13},{2,6},{6,10},{10,14},{3,7},{... | collective-permute-start | bytes 294920 | tf_op jit(solution)/shard_map/ppermute | solution.py:319
  4.9 3.2 %collective-permute-done.rim_ref = bf16[3,16,1024]{2,1,0:T(8,128)(2,1)S(1)} collective-permute-done((bf16[3,16,1024]{2,1,0:T(8,128)(2,1)}, bf16[3,16,1024]{2,1,0:T(8,128)(2,1)S(1)}, u32[]{:S(2)}, u32[]{:S(2)}) %collective-permute-start) | collective-permute-done | bytes 98336 | tf_op jit(solution)/shard_map/ppermute | solution.py:319
  8.1 16.9 %summary.1 = (bf16[768,1024]{1,0:T(8,128)(2,1)}, bf16[768,2048]{1,0:T(8,128)(2,1)}, bf16[6,8,128,256]{3,2,1,0:T(8,128)(2,1)}, bf16[8,128,256]{2,1,0:T(8,128)(2,1)S(1)}) custom-call(bf16[3,16,1024]{2,1,0:T(8,128)(2,1)S(1)} %collective-permute-done.rim_ref, bf16[768,1024]{1,0:T(8,128)(2,1)} %kp_ref.1, bf16[768,1024]{1,0:T(8,128)(2,1)} %vp_ref.1, ...), custom_call_target="tpu_custom_call" | custom-call | tf_op jit(solution)/shard_map/summary/pallas_call | solution.py:235
  25.1 1.3 %collective-permute-start.2 = (bf16[8,128,128]{2,1,0:T(8,128)(2,1)S(1)}, bf16[8,128,128]{2,1,0:T(8,128)(2,1)S(1)}, u32[]{:S(2)}, u32[]{:S(2)}) collective-permute-start(bf16[8,128,128]{2,1,0:T(8,128)(2,1)S(1)} %slice.14), channel_id=1, source_target_pairs={{0,4},{1,5},{2,6},{3,7},{16,20},{17,21},{18,22},{19,23}} | collective-permute-start | bytes 786440 | tf_op jit(solution)/shard_map/ppermute | solution.py:350
  26.4 0.7 collective-permute-start.1
  27.1 4.6 %local.2 = (bf16[768,1024]{1,0:T(8,128)(2,1)}, bf16[768,1024]{1,0:T(8,128)(2,1)}) custom-call(bf16[3,16,1024]{2,1,0:T(8,128)(2,1)S(1)} %collective-permute-done.rim_ref, bf16[768,1024]{1,0:T(8,128)(2,1)} %qp_ref.3, bf16[768,1024]{1,0:T(8,128)(2,1)} %qp_ref.3, bf16[768,1024]{1,0:T(8,128)(2,1)} %get-tuple-element.24.keys_ref, ...), custom_call_target="tpu_custom_call" | custom-call | tf_op jit(solution)/shard_map/local/pallas_call | solution.py:268
  31.7 2.2 %collective-permute-done.2 = bf16[8,128,128]{2,1,0:T(8,128)(2,1)S(1)} collective-permute-done((bf16[8,128,128]{2,1,0:T(8,128)(2,1)S(1)}, bf16[8,128,128]{2,1,0:T(8,128)(2,1)S(1)}, u32[]{:S(2)}, u32[]{:S(2)}) %collective-permute-start.2) | collective-permute-done | bytes 262176 | tf_op jit(solution)/shard_map/ppermute | solution.py:350
  33.9 0.2 fusion.3
  34.1 2.3 %collective-permute-start.3 = (bf16[8,128,128]{2,1,0:T(8,128)(2,1)S(1)}, bf16[8,128,128]{2,1,0:T(8,128)(2,1)S(1)}, u32[]{:S(2)}, u32[]{:S(2)}) collective-permute-start(bf16[8,128,128]{2,1,0:T(8,128)(2,1)S(1)} %fusion.3), channel_id=1, source_target_pairs={{4,12},{5,13},{6,14},{7,15},{20,28},{21,29},{22,30},{23,31}} | collective-permute-start | bytes 786440 | tf_op jit(solution)/shard_map/ppermute | solution.py:355
  36.4 1.9 %collective-permute-start.4 = (bf16[8,128,128]{2,1,0:T(8,128)(2,1)S(1)}, bf16[8,128,128]{2,1,0:T(8,128)(2,1)S(1)}, u32[]{:S(2)}, u32[]{:S(2)}) collective-permute-start(bf16[8,128,128]{2,1,0:T(8,128)(2,1)S(1)} %fusion.3), channel_id=1, source_target_pairs={{4,8},{5,9},{6,10},{7,11},{20,24},{21,25},{22,26},{23,27}} | collective-permute-start | bytes 786440 | tf_op jit(solution)/shard_map/ppermute | solution.py:356
  39.0 0.1 pad_add_fusion.2.info_ref
  39.1 7.3 %local.3 = (bf16[768,1024]{1,0:T(8,128)(2,1)}, bf16[768,1024]{1,0:T(8,128)(2,1)}) custom-call(bf16[3,16,1024]{2,1,0:T(8,128)(2,1)S(1)} %collective-permute-done.rim_ref, bf16[768,1024]{1,0:T(8,128)(2,1)} %qp_ref.3, bf16[768,1024]{1,0:T(8,128)(2,1)} %qp_ref.3, ...), custom_call_target="tpu_custom_call", output_to_operand_aliasing={{0}: (8, {}), {1}: (9, {})} | custom-call | tf_op jit(solution)/shard_map/local/pallas_call | solution.py:268
  46.4 0.1 collective-permute-done.4
  46.5 0.3 fusion.2.state_ref
  46.8 5.1 %outputs.2 = (bf16[192,2304]{1,0:T(8,128)(2,1)S(1)}, bf16[192,2304]{1,0:T(8,128)(2,1)S(1)}) custom-call(s32[4]{0:T(128)S(1)} %pad_add_fusion.2.info_ref, bf16[8,128,128]{2,1,0:T(8,128)(2,1)S(1)} %fusion.2.state_ref, bf16[768,1024]{1,0:T(8,128)(2,1)} %get-tuple-element.34.local_ref, bf16[768,1024]{1,0:T(8,128)(2,1)} %get-tuple-element.35.qeff_ref, ...), custom_call_target="tpu_custom_call" | custom-call | tf_op jit(solution)/shard_map/outputs/pallas_call | solution.py:392
  52.0 0.1 pad_add_fusion.info_ref
  52.1 2.3 %collective-permute-done.5 = bf16[192,2304]{1,0:T(8,128)(2,1)S(1)} collective-permute-done((bf16[192,2304]{1,0:T(8,128)(2,1)S(1)}, bf16[192,2304]{1,0:T(8,128)(2,1)S(1)}, u32[]{:S(2)}, u32[]{:S(2)}) %collective-permute-start.5) | collective-permute-done | bytes 884768 | tf_op jit(solution)/shard_map/ppermute | solution.py:413
  54.4 0.2 add_convert_fusion.1
  54.6 1.6 %collective-permute-start.7 = (bf16[192,2304]{1,0:T(8,128)(2,1)S(1)}, bf16[192,2304]{1,0:T(8,128)(2,1)S(1)}, u32[]{:S(2)}, u32[]{:S(2)}) collective-permute-start(bf16[192,2304]{1,0:T(8,128)(2,1)S(1)} %add_convert_fusion.1), channel_id=1, source_target_pairs={{0,2},{1,3},{2,0},{3,1},{4,6},{5,7},{6,4},{7,5},{8,10},{9,11},{10,... | collective-permute-start | bytes 2654216 | tf_op jit(solution)/shard_map/ppermute | solution.py:413
  56.2 6.8 %outputs.3 = (bf16[192,2304]{1,0:T(8,128)(2,1)S(1)}, bf16[192,2304]{1,0:T(8,128)(2,1)S(1)}) custom-call(s32[4]{0:T(128)S(1)} %pad_add_fusion.info_ref, bf16[8,128,128]{2,1,0:T(8,128)(2,1)S(1)} %fusion.2.state_ref, bf16[768,1024]{1,0:T(8,128)(2,1)} %get-tuple-element.34.local_ref, bf16[768,1024]{1,0:T(8,128)(2,1)} %get-tuple-element.35.qeff_ref, ...), custom_call_target="tpu_custom_call" | custom-call | tf_op jit(solution)/shard_map/outputs/pallas_call | solution.py:392
  62.9 0.1 collective-permute-start.6
  63.0 13.4 %collective-permute-done.7 = bf16[192,2304]{1,0:T(8,128)(2,1)S(1)} collective-permute-done((bf16[192,2304]{1,0:T(8,128)(2,1)S(1)}, bf16[192,2304]{1,0:T(8,128)(2,1)S(1)}, u32[]{:S(2)}, u32[]{:S(2)}) %collective-permute-start.7) | collective-permute-done | bytes 884768 | tf_op jit(solution)/shard_map/ppermute | solution.py:413
  76.4 1.3 %add_convert_fusion = bf16[192,2304]{1,0:T(8,128)(2,1)} fusion(bf16[192,2304]{1,0:T(8,128)(2,1)S(1)} %collective-permute-done.7, bf16[192,2304]{1,0:T(8,128)(2,1)S(1)} %collective-permute-done.6, bf16[192,2304]{1,0:T(8,128)(2,1)S(1)} %get-tuple-element.39), kind=kLoop, calls=%fused_computation | loop fusion | flops 2654208 | bytes 3538944 | tf_op jit(solution)/shard_map/convert_element_type | solution.py:426
  (10 shorter events, 0.1 us)
Async XLA Ops:
  1.4 6.7 %collective-permute-start = (bf16[3,16,1024]{2,1,0:T(8,128)(2,1)}, bf16[3,16,1024]{2,1,0:T(8,128)(2,1)S(1)}, u32[]{:S(2)}, u32[]{:S(2)}) collective-permute-start(bf16[3,16,1024]{2,1,0:T(8,128)(2,1)} %ends.1), channel_id=1, source_target_pairs={{0,4},{4,8},{8,12},{1,5},{5,9},{9,13},{2,6},{6,10},{10,14},{3,7},{... | collective-permute-start | bytes 294920 | tf_op jit(solution)/shard_map/ppermute | solution.py:319
  25.1 8.8 %collective-permute-start.2 = (bf16[8,128,128]{2,1,0:T(8,128)(2,1)S(1)}, bf16[8,128,128]{2,1,0:T(8,128)(2,1)S(1)}, u32[]{:S(2)}, u32[]{:S(2)}) collective-permute-start(bf16[8,128,128]{2,1,0:T(8,128)(2,1)S(1)} %slice.14), channel_id=1, source_target_pairs={{0,4},{1,5},{2,6},{3,7},{16,20},{17,21},{18,22},{19,23}} | collective-permute-start | bytes 786440 | tf_op jit(solution)/shard_map/ppermute | solution.py:350
  26.4 20.1 %collective-permute-start.1 = (bf16[8,128,256]{2,1,0:T(8,128)(2,1)S(1)}, bf16[8,128,256]{2,1,0:T(8,128)(2,1)S(1)}, u32[]{:S(2)}, u32[]{:S(2)}) collective-permute-start(bf16[8,128,256]{2,1,0:T(8,128)(2,1)S(1)} %get-tuple-element.23), channel_id=1, source_target_pairs={{8,12},{9,13},{10,14},{11,15},{24,28},{25,29},{26,30},{27,31}} | collective-permute-start | bytes 1572872 | tf_op jit(solution)/shard_map/ppermute | solution.py:351
  34.1 12.3 %collective-permute-start.3 = (bf16[8,128,128]{2,1,0:T(8,128)(2,1)S(1)}, bf16[8,128,128]{2,1,0:T(8,128)(2,1)S(1)}, u32[]{:S(2)}, u32[]{:S(2)}) collective-permute-start(bf16[8,128,128]{2,1,0:T(8,128)(2,1)S(1)} %fusion.3), channel_id=1, source_target_pairs={{4,12},{5,13},{6,14},{7,15},{20,28},{21,29},{22,30},{23,31}} | collective-permute-start | bytes 786440 | tf_op jit(solution)/shard_map/ppermute | solution.py:355
  36.4 10.0 %collective-permute-start.4 = (bf16[8,128,128]{2,1,0:T(8,128)(2,1)S(1)}, bf16[8,128,128]{2,1,0:T(8,128)(2,1)S(1)}, u32[]{:S(2)}, u32[]{:S(2)}) collective-permute-start(bf16[8,128,128]{2,1,0:T(8,128)(2,1)S(1)} %fusion.3), channel_id=1, source_target_pairs={{4,8},{5,9},{6,10},{7,11},{20,24},{21,25},{22,26},{23,27}} | collective-permute-start | bytes 786440 | tf_op jit(solution)/shard_map/ppermute | solution.py:356
  39.0 7.8 %slice-start = ((s8[4718592]{0:T(1024)(128)(4,1)}), s8[4194304]{0:T(1024)(128)(4,1)S(1)}, s32[]{:S(2)}) async-start(s8[4718592]{0:T(1024)(128)(4,1)} %bitcast.8), calls=%async_computation | async-start | bytes 8388608
  39.1 7.7 %slice-start.1 = ((s8[4718592]{0:T(1024)(128)(4,1)}), s8[524288]{0:T(1024)(128)(4,1)S(1)}, s32[]{:S(2)}) async-start(s8[4718592]{0:T(1024)(128)(4,1)} %bitcast.8), calls=%async_computation.1 | async-start | bytes 1048576
  51.9 2.5 %collective-permute-start.5 = (bf16[192,2304]{1,0:T(8,128)(2,1)S(1)}, bf16[192,2304]{1,0:T(8,128)(2,1)S(1)}, u32[]{:S(2)}, u32[]{:S(2)}) collective-permute-start(bf16[192,2304]{1,0:T(8,128)(2,1)S(1)} %get-tuple-element.37), channel_id=1, source_target_pairs={{0,1},{1,0},{2,3},{3,2},{4,5},{5,4},{6,7},{7,6},{8,9},{9,8},{10,11... | collective-permute-start | bytes 2654216 | tf_op jit(solution)/shard_map/ppermute | solution.py:413
  54.6 21.8 %collective-permute-start.7 = (bf16[192,2304]{1,0:T(8,128)(2,1)S(1)}, bf16[192,2304]{1,0:T(8,128)(2,1)S(1)}, u32[]{:S(2)}, u32[]{:S(2)}) collective-permute-start(bf16[192,2304]{1,0:T(8,128)(2,1)S(1)} %add_convert_fusion.1), channel_id=1, source_target_pairs={{0,2},{1,3},{2,0},{3,1},{4,6},{5,7},{6,4},{7,5},{8,10},{9,11},{10,... | collective-permute-start | bytes 2654216 | tf_op jit(solution)/shard_map/ppermute | solution.py:413
  62.9 13.4 %collective-permute-start.6 = (bf16[192,2304]{1,0:T(8,128)(2,1)S(1)}, bf16[192,2304]{1,0:T(8,128)(2,1)S(1)}, u32[]{:S(2)}, u32[]{:S(2)}) collective-permute-start(bf16[192,2304]{1,0:T(8,128)(2,1)S(1)} %get-tuple-element.40), channel_id=1, source_target_pairs={{0,1},{1,0},{2,3},{3,2},{4,5},{5,4},{6,7},{7,6},{8,9},{9,8},{10,11... | collective-permute-start | bytes 2654216 | tf_op jit(solution)/shard_map/ppermute | solution.py:413
